TPU v7x, 256 devices: a whole 4x4x8 slice. The times are simulated.
256 devices in a mesh: wide: 32 (over z, x), narrow: 8 (over y, core).
Axes of the slice: x: 4, y: 4, z: 8, core: 2. Of those that a mesh axis runs over, the one named last changes fastest.
Arguments:
- grid_adjoint_fields: bfloat16 [256, 2560, 512], P('wide', 'narrow'), may hold values from -6 to 6
- interp_weights: bfloat16 [20480, 32, 32], P(('wide', 'narrow')), may hold values from -1 to 1
- depart_owner: int32 [20480, 1], P(('wide', 'narrow')), may hold values from 0 to 31; in each aligned block of 80 rows (0 to 79, 80 to 159, ...) at most 5 rows name the same one
- depart_block: int32 [20480], P(('wide', 'narrow')), may hold values from 0 to 79
- wave_perm: int32 [512], replicated, may hold values from 0 to 511, each once
- legendre: bfloat16 [512, 256, 512], P(('wide', 'narrow')), may hold values from -0.375 to 0.375
- mode_proj: float32 [512, 512], replicated, may hold values from -0.25 to 0.25
- mode_back: float32 [512, 512], replicated, may hold values from -0.25 to 0.25
- mode_depth: float32 [512], replicated, may hold values from 1e-06 to 0.001
Outputs:
- adj_out: float32 [256, 2560, 512], P('wide', 'narrow')
Inputs may be any that keep to these rules, and one draw needn't show every extreme that they name: `depart_owner`: each block's departure owner shares the block's narrow index. Among the 80 blocks of one device at most 5 name one owner, and exactly 5 do in some devices. `wave_perm`: every wavenumber appears once.
All inputs are finite; a program needn't handle non-finite values.
Results may differ from a plain program's by a relative error of at most 0.013.
Values may be sent and summed in bfloat16 or wider, within the bound.
No kernel may reach another device: no remote copies, remote signals or barrier semaphores. Data moves between devices by JAX's collectives and lax.ppermute only.
A program may use at most 256 MiB of HBM per device.

v0:
```python
import math

import jax
import jax.numpy as jnp
from jax import lax
from jax.sharding import PartitionSpec as P

NLON = 2560
BS = 32


def trig_table(lon_index, col_index, wave_perm):
    wavenumber = jnp.take(wave_perm, col_index // 2)
    phase_int = lon_index[:, None] * wavenumber[None, :] % NLON
    angles = phase_int.astype(jnp.float32) * (2.0 * math.pi / NLON)
    values = jnp.where((col_index % 2 == 0)[None, :], jnp.cos(angles), jnp.sin(angles))
    return values.astype(jnp.bfloat16)


def apply_modes(spectra, mode_proj, mode_back, mode_depth):
    slot_count, degrees, parts, channels = spectra.shape
    mode_rows = jnp.dot(
        spectra.reshape(-1, channels),
        mode_proj,
        precision=lax.Precision.HIGHEST,
        preferred_element_type=jnp.float32,
    )
    degree_float = jnp.arange(degrees, dtype=jnp.float32)
    damping = 1.0 / (1.0 + (degree_float * (degree_float + 1.0))[:, None] * mode_depth[None, :])
    mode_rows = mode_rows.reshape(slot_count, degrees, parts, channels) * damping[None, :, None, :]
    returned = jnp.dot(
        mode_rows.reshape(-1, channels),
        mode_back,
        precision=lax.Precision.HIGHEST,
        preferred_element_type=jnp.float32,
    )
    return returned.astype(jnp.bfloat16).reshape(slot_count, degrees, parts, channels)


def shards(
    grid_adjoint_fields,
    interp_weights,
    depart_owner,
    depart_block,
    wave_perm,
    legendre,
    mode_proj,
    mode_back,
    mode_depth,
):
    wide_count = lax.axis_size("wide")
    narrow_count = lax.axis_size("narrow")
    wide_index = lax.axis_index("wide")
    narrow_index = lax.axis_index("narrow")
    lat_dev, lon_dev, channels = grid_adjoint_fields.shape
    slot_count, lat_total, degrees = legendre.shape
    two_m = 2 * degrees
    normalizing_scale = NLON ** (-0.5)
    slot_ids = (wide_index * narrow_count + narrow_index) * slot_count + jnp.arange(
        slot_count, dtype=jnp.int32
    )
    wavenumber = jnp.take(wave_perm, slot_ids)
    degree_ids = jnp.arange(degrees, dtype=jnp.int32)
    masked_values = jnp.where(
        degree_ids[None, None, :] >= wavenumber[:, None, None], legendre, jnp.zeros_like(legendre)
    )
    per_set = two_m // narrow_count
    lon_ids = narrow_index * lon_dev + jnp.arange(lon_dev, dtype=jnp.int32)

    def column_of(order_index):
        set_id = order_index // per_set
        within = order_index % per_set
        band_id = within // (2 * slot_count)
        return (
            band_id * (two_m // wide_count) + set_id * (2 * slot_count) + within % (2 * slot_count)
        )

    cols = column_of(jnp.arange(lax.axis_size("narrow") * per_set, dtype=jnp.int32))
    trig_part = trig_table(lon_ids, cols, wave_perm)
    summed = lax.psum_scatter(
        jnp.einsum(
            "alc,lr->rac", grid_adjoint_fields, trig_part, preferred_element_type=jnp.float32
        ).astype(jnp.bfloat16),
        "narrow",
        scatter_dimension=0,
        tiled=True,
    ).astype(jnp.float32)
    fourier_harmonics = (summed * normalizing_scale).astype(jnp.bfloat16)
    fourier_harmonics = fourier_harmonics.reshape(wide_count, 2 * slot_count, lat_dev, channels)
    fourier_harmonics = lax.all_to_all(
        fourier_harmonics, "wide", split_axis=0, concat_axis=2, tiled=True
    )
    fourier_harmonics = fourier_harmonics.reshape(slot_count, 2, lat_total, channels)
    spectra = jnp.einsum(
        "kgn,kpgc->knpc", masked_values, fourier_harmonics, preferred_element_type=jnp.float32
    )
    returned = apply_modes(spectra, mode_proj, mode_back, mode_depth)
    synthesis_output = jnp.einsum(
        "kgn,knpc->kpgc", masked_values, returned, preferred_element_type=jnp.float32
    ).astype(jnp.bfloat16)
    synthesis_output = synthesis_output.reshape(1, 2 * slot_count, wide_count, lat_dev, channels)
    synthesis_output = lax.all_to_all(
        synthesis_output, "wide", split_axis=2, concat_axis=0, tiled=True
    )
    synthesis_output = synthesis_output.reshape(per_set, lat_dev, channels)
    shard_rows = lax.all_gather(synthesis_output, "narrow", axis=0, tiled=True)
    cols = column_of(jnp.arange(shard_rows.shape[0], dtype=jnp.int32))
    trig_part = trig_table(lon_ids, cols, wave_perm)
    wave_sum = jnp.einsum("rac,lr->alc", shard_rows, trig_part, preferred_element_type=jnp.float32)
    wavenumber_grid = (wave_sum * normalizing_scale).astype(jnp.bfloat16)
    blocks_per_row = lon_dev // BS
    block_count = lat_dev * blocks_per_row
    blocks = grid_adjoint_fields.reshape(block_count, BS, channels)
    contrib = jnp.einsum(
        "bai,bac->bic", interp_weights, blocks, preferred_element_type=jnp.float32
    ).astype(jnp.bfloat16)
    owner_band = depart_owner[:, 0]
    block_ids = jnp.arange(block_count, dtype=jnp.int32)
    capacity = (2 * block_count + wide_count - 1) // wide_count
    same_owner = owner_band[:, None] == owner_band[None, :]
    earlier = block_ids[None, :] < block_ids[:, None]
    slot_rank = jnp.sum((same_owner & earlier).astype(jnp.int32), axis=1)
    send_slot = owner_band * capacity + slot_rank
    pick_slot = jnp.arange(wide_count * capacity, dtype=jnp.int32)[:, None] == send_slot[None, :]
    packed = jnp.einsum(
        "sb,bjc->sjc", pick_slot.astype(jnp.bfloat16), contrib, preferred_element_type=jnp.float32
    )
    packed = packed.astype(jnp.bfloat16).reshape(wide_count, capacity, BS, channels)
    slot_target = jnp.max(jnp.where(pick_slot, depart_block[None, :], -1), axis=1).reshape(
        wide_count, capacity
    )
    recv_values, recv_targets = (
        lax.all_to_all(packed, "wide", split_axis=0, concat_axis=0, tiled=True),
        lax.all_to_all(slot_target, "wide", split_axis=0, concat_axis=0, tiled=True),
    )
    hit_table = (recv_targets.reshape(-1)[None, :] == block_ids[:, None]).astype(jnp.bfloat16)
    deposit = jnp.einsum(
        "bs,sjc->bjc",
        hit_table,
        recv_values.reshape(-1, BS, channels),
        preferred_element_type=jnp.float32,
    )
    return wavenumber_grid.astype(jnp.float32) + deposit.reshape(lat_dev, lon_dev, channels)


def solution(mesh):
    in_specs = (
        P("wide", "narrow", None),
        P(("wide", "narrow"), None, None),
        P(("wide", "narrow"), None),
        P(("wide", "narrow")),
        P(),
        P(("wide", "narrow"), None, None),
        P(),
        P(),
        P(),
    )
    out_specs = P("wide", "narrow", None)
    return jax.shard_map(shards, mesh=mesh, in_specs=in_specs, out_specs=out_specs, check_vma=False)
```

profile of v0, /device:TPU:26, one launch (start us, length us, event | category | flops | bytes accessed | tf_op | source)
XLA Modules:
  0.0 375.3 jit_solution(12278908487408674721)
XLA Ops:
  6.6 0.8 copy-done.2
  7.4 6.9 %gather_fusion.1 = s32[1024]{0:T(1024)S(1)} fusion(s32[512]{0:T(512)S(1)} %copy-done.2, s32[1024]{0:T(1024)S(1)} %broadcast_clamp_fusion), kind=kCustom, calls=%fused_computation.clone | custom fusion | bytes 12288 | tf_op jit(solution)/shard_map/jit(_take)/gather | solution.py:13
  14.3 11.6 %convolution_convert_fusion = bf16[1024,8,512]{2,0,1:T(8,128)(2,1)} fusion(bf16[8,320,512]{2,1,0:T(8,128)(2,1)S(1)} %copy-done, s32[1024]{0:T(1024)S(1)} %and_select_fusion, s32[320]{0:T(512)S(1)} %iota_add_fusion, pred[1024]{0:T(1024)(128)(4,1)S(1)} %fusion.46), kind=kOutput, calls=%fused_computation.2 | convolution fusion | flops 2692153344 | bytes 11016448 | tf_op jit(solution)/shard_map/alc,lr->rac/dot_general | solution.py:81
  25.9 0.0 reduce-scatter.2.cloned.1.call-update
  25.9 55.9 %reduce-scatter.2.cloned.1.call-done = bf16[128,8,512]{2,0,1:T(8,128)(2,1)} async-done(((bf16[1024,8,512]{2,0,1:T(8,128)(2,1)}), bf16[128,8,512]{2,0,1:T(8,128)(2,1)}) %reduce-scatter.2.cloned.1.call-update) | async-done | bytes 1048592 | tf_op jit(solution)/shard_map/reduce_scatter | solution.py:80
  81.8 1.4 multiply_convert_fusion.1
  83.3 0.0 copy-start.10
  83.3 1.5 copy.51
  84.8 10.3 %all-to-all-start = ((bf16[32,4,8,512]{3,2,1,0:T(8,128)(2,1)}), bf16[32,4,8,512]{3,2,1,0:T(8,128)(2,1)}, u32[]{:S(2)}, u32[]{:S(2)}) async-start(bf16[32,4,8,512]{3,2,1,0:T(8,128)(2,1)} %bitcast.64), calls=%async_computation.1 | async-start | bytes 2097152 | tf_op jit(solution)/shard_map/all_to_all | solution.py:90
  95.1 0.3 all-gather.2.cloned.1.call-start
  95.4 0.6 gather_fusion
  96.1 0.1 iota_compare_fusion.3
  96.2 1.2 add_divide_fusion
  97.4 26.1 %all-to-all-done = bf16[32,4,8,512]{3,2,1,0:T(8,128)(2,1)} async-done(((bf16[32,4,8,512]{3,2,1,0:T(8,128)(2,1)}), bf16[32,4,8,512]{3,2,1,0:T(8,128)(2,1)}, u32[]{:S(2)}, u32[]{:S(2)}) %all-to-all-start) | async-done | bytes 1048608 | tf_op jit(solution)/shard_map/all_to_all | solution.py:90
  123.4 1.3 copy.34
  124.8 0.8 fusion.25
  125.5 0.4 copy-done.4
  126.0 0.3 copy-done.5
  126.3 7.6 %convolution_multiply_fusion = f32[2,512,2,512]{3,1,2,0:T(8,128)S(1)} fusion(f32[2,512,2,512]{3,1,2,0:T(8,128)S(1)} %fusion.25, f32[512,512]{1,0:T(8,128)S(1)} %copy-done.4, f32[512,512]{1,0:T(8,128)S(1)} %copy-done.5), kind=kOutput, calls=%fused_computation.10 | convolution fusion | flops 6443499520 | bytes 10485760 | tf_op jit(solution)/shard_map/dot_general | solution.py:22
  133.9 5.2 %copy.36 = f32[2,512,2,512]{3,2,1,0:T(2,128)} copy(f32[2,512,2,512]{3,1,2,0:T(8,128)S(1)} %convolution_multiply_fusion) | data formatting | bytes 8388608 | tf_op jit(solution)/shard_map/mul | solution.py:30
  139.2 6.3 %reshape.216 = f32[2048,512]{1,0:T(8,128)} reshape(f32[2,512,2,512]{3,2,1,0:T(2,128)} %copy.36) | data formatting | bytes 8388608 | tf_op jit(solution)/shard_map/reshape | solution.py:32
  145.5 9.7 %convolution_convert_fusion.2 = bf16[2048,512]{1,0:T(8,128)(2,1)} fusion(f32[2048,512]{1,0:T(8,128)} %reshape.216, f32[512,512]{1,0:T(8,128)} %param.18), kind=kOutput, calls=%fused_computation.8 | convolution fusion | flops 6443499520 | bytes 7340032 | tf_op jit(solution)/shard_map/dot_general | solution.py:31
  155.2 4.1 %reshape.217 = bf16[2,512,2,512]{3,2,1,0:T(2,128)(2,1)} reshape(bf16[2048,512]{1,0:T(8,128)(2,1)} %convolution_convert_fusion.2) | data formatting | bytes 4194304 | tf_op jit(solution)/shard_map/reshape | solution.py:37
  159.3 2.3 fusion.5
  161.7 0.1 copy.38
  161.8 0.0 copy-start.16
  161.8 32.8 %all_to_all.44 = bf16[1,4,32,8,512]{4,3,1,0,2:T(8,128)(2,1)S(1)} all-to-all(bf16[1,4,32,8,512]{4,3,1,0,2:T(8,128)(2,1)S(1)} %copy.38), channel_id=1, replica_groups=mesh['wide'=32,'narrow'=8] {'wide'}, dimensions={2} | all-to-all | bytes 2097152 | tf_op jit(solution)/shard_map/all_to_all | solution.py:102
  194.6 1.3 copy.52
  195.9 0.0 all-gather.2.cloned.1.call-update
  196.0 0.2 convert_reduce_fusion
  196.2 0.1 select_reduce_fusion
  196.3 0.7 all_to_all.37
  197.0 6.1 %all-to-all-start.2 = ((s32[32,1,5]{2,1,0:T(1,128)}), s32[32,1,5]{2,1,0:T(1,128)S(1)}, u32[]{:S(2)}, u32[]{:S(2)}) async-start(s32[32,1,5]{2,1,0:T(1,128)} %bitcast.18), calls=%async_computation.3 | async-start | bytes 32768 | tf_op jit(solution)/shard_map/all_to_all | solution.py:134
  203.1 1.1 copy.41
  204.2 0.0 copy-start.12
  204.2 0.8 convolution_convert_fusion.3
  205.1 3.9 %convolution_convert_fusion.1 = bf16[160,32,512]{2,0,1:T(8,128)(2,1)S(1)} fusion(bf16[80,32,512]{2,1,0:T(8,128)(2,1)S(1)} %convolution_convert_fusion.3, s32[80]{0:T(128)S(1)} %copy-done.12), kind=kOutput, calls=%fused_computation.7 | convolution fusion | flops 422064640 | bytes 7864640 | tf_op jit(solution)/shard_map/sb,bjc->sjc/dot_general | solution.py:125
  208.9 5.3 %copy.43 = bf16[160,32,512]{2,1,0:T(8,128)(2,1)} copy(bf16[160,32,512]{2,0,1:T(8,128)(2,1)S(1)} %convolution_convert_fusion.1) | data formatting | bytes 10485760 | tf_op jit(solution)/shard_map/convert_element_type | solution.py:128
  214.2 10.0 %all-to-all-start.3 = ((bf16[32,5,32,512]{3,2,1,0:T(8,128)(2,1)}), bf16[32,5,32,512]{3,2,1,0:T(8,128)(2,1)}, u32[]{:S(2)}, u32[]{:S(2)}) async-start(bf16[32,5,32,512]{3,2,1,0:T(8,128)(2,1)} %bitcast.61), calls=%async_computation.4 | async-start | bytes 10485760 | tf_op jit(solution)/shard_map/all_to_all | solution.py:133
  224.2 0.5 broadcast.317
  224.8 0.6 reduce.3
  225.4 0.1 eq.66
  225.5 112.9 %all-to-all-done.3 = bf16[32,5,32,512]{3,2,1,0:T(8,128)(2,1)} async-done(((bf16[32,5,32,512]{3,2,1,0:T(8,128)(2,1)}), bf16[32,5,32,512]{3,2,1,0:T(8,128)(2,1)}, u32[]{:S(2)}, u32[]{:S(2)}) %all-to-all-start.3) | async-done | bytes 5242912 | tf_op jit(solution)/shard_map/all_to_all | solution.py:133
  338.4 8.6 %fusion = f32[80,32,512]{2,0,1:T(8,128)S(1)} fusion(bf16[160,32,512]{2,1,0:T(8,128)(2,1)} %bitcast.23, s32[160]{0:T(256)S(1)} %eq.66), kind=kOutput, calls=%fused_computation.4 | convolution fusion | flops 419443200 | bytes 10486400 | tf_op jit(solution)/shard_map/bs,sjc->bjc/dot_general | solution.py:137
  347.0 5.4 %copy.45 = f32[80,32,512]{2,1,0:T(8,128)} copy(f32[80,32,512]{2,0,1:T(8,128)S(1)} %fusion) | data formatting | bytes 10485760 | tf_op jit(solution)/shard_map/bs,sjc->bjc/dot_general | solution.py:137
  352.4 0.0 copy-start.3
  352.4 11.7 %fusion.15 = f32[320,8,512]{2,0,1:T(8,128)S(1)} fusion(bf16[1024,8,512]{2,0,1:T(8,128)(2,1)} %all-gather.2.cloned.1.call-done, s32[1024]{0:T(1024)S(1)} %copy-done.9, s32[320]{0:T(512)S(1)} %copy-done.14, pred[1024]{0:T(1024)(128)(4,1)S(1)} %copy-done.18), kind=kOutput, calls=%fused_computation.27 | convolution fusion | flops 2687959040 | bytes 13637888 | tf_op jit(solution)/shard_map/rac,lr->alc/dot_general | solution.py:109
  364.2 4.0 %bitcast_add_fusion = f32[8,320,512]{2,1,0:T(8,128)} fusion(f32[320,8,512]{2,0,1:T(8,128)S(1)} %fusion.15, f32[8,320,512]{2,1,0:T(8,128)S(1)} %bitcast.62), kind=kLoop, calls=%fused_computation.3 | loop fusion | flops 5242880 | bytes 15728640 | tf_op jit(solution)/shard_map/add | solution.py:143
  (43 shorter events, 0.2 us)
Async XLA Ops:
  6.5 7.7 %copy-start = (bf16[8,320,512]{2,1,0:T(8,128)(2,1)S(1)}, bf16[8,320,512]{2,1,0:T(8,128)(2,1)}, u32[]{:S(2)}) copy-start(bf16[8,320,512]{2,1,0:T(8,128)(2,1)} %param.11) | copy-start | bytes 7864324
  6.5 0.8 copy-start.2
  6.5 75.3 %reduce-scatter.2.cloned.1.call-start = ((), (), s32[]{:S(2)}) async-start(), calls=%async_computation.5 | async-start | bytes 9437184 | tf_op jit(solution)/shard_map/reduce_scatter | solution.py:80
  6.6 19.3 %copy-start.17 = (pred[1024]{0:T(1024)(128)(4,1)}, pred[1024]{0:T(1024)(128)(4,1)S(1)}, u32[]{:S(2)}) copy-start(pred[1024]{0:T(1024)(128)(4,1)S(1)} %fusion.46) | copy-start | bytes 3076
  7.4 18.5 %copy-start.13 = (s32[320]{0:T(512)}, s32[320]{0:T(512)S(1)}, u32[]{:S(2)}) copy-start(s32[320]{0:T(512)S(1)} %iota_add_fusion) | copy-start | bytes 3844
  14.3 11.6 %copy-start.8 = (s32[1024]{0:T(1024)}, s32[1024]{0:T(1024)S(1)}, u32[]{:S(2)}) copy-start(s32[1024]{0:T(1024)S(1)} %and_select_fusion) | copy-start | bytes 12292
  83.3 12.9 %copy-start.10 = (f32[512]{0:T(512)S(1)}, f32[512]{0:T(512)}, u32[]{:S(2)}) copy-start(f32[512]{0:T(512)} %param.19) | copy-start | bytes 6148
  84.8 39.9 %copy-start.6 = (bf16[2,256,512]{2,1,0:T(8,128)(2,1)S(1)}, bf16[2,256,512]{2,1,0:T(8,128)(2,1)}, u32[]{:S(2)}) copy-start(bf16[2,256,512]{2,1,0:T(8,128)(2,1)} %param.16) | copy-start | bytes 1572868
  84.8 38.6 %all-to-all-start = ((bf16[32,4,8,512]{3,2,1,0:T(8,128)(2,1)}), bf16[32,4,8,512]{3,2,1,0:T(8,128)(2,1)}, u32[]{:S(2)}, u32[]{:S(2)}) async-start(bf16[32,4,8,512]{3,2,1,0:T(8,128)(2,1)} %bitcast.64), calls=%async_computation.1 | async-start | bytes 2097152 | tf_op jit(solution)/shard_map/all_to_all | solution.py:90
  95.1 257.3 %all-gather.2.cloned.1.call-start = ((), (), s32[]{:S(2)}) async-start(), calls=%async_computation.6 | async-start | bytes 9437184 | tf_op jit(solution)/shard_map/all_gather | solution.py:106
  124.7 1.2 copy-start.4
  124.8 1.5 copy-start.5
  161.8 34.2 %copy-start.16 = (s32[80,1]{0,1:T(1,128)S(1)}, s32[80,1]{0,1:T(1,128)}, u32[]{:S(2)}) copy-start(s32[80,1]{0,1:T(1,128)} %param.13) | copy-start | bytes 964
  161.8 34.4 %copy-start.15 = (s32[80]{0:T(128)S(1)}, s32[80]{0:T(128)}, u32[]{:S(2)}) copy-start(s32[80]{0:T(128)} %param.14) | copy-start | bytes 964
  161.8 41.3 %copy-start.7 = (bf16[80,32,32]{0,2,1:T(8,128)(2,1)S(1)}, bf16[80,32,32]{0,2,1:T(8,128)(2,1)}, u32[]{:S(2)}) copy-start(bf16[80,32,32]{0,2,1:T(8,128)(2,1)} %param.12) | copy-start | bytes 491524
  196.1 0.8 copy-start.11
  197.0 17.3 %all-to-all-start.2 = ((s32[32,1,5]{2,1,0:T(1,128)}), s32[32,1,5]{2,1,0:T(1,128)S(1)}, u32[]{:S(2)}, u32[]{:S(2)}) async-start(s32[32,1,5]{2,1,0:T(1,128)} %bitcast.18), calls=%async_computation.3 | async-start | bytes 32768 | tf_op jit(solution)/shard_map/all_to_all | solution.py:134
  204.2 0.8 copy-start.12
  214.2 124.2 %all-to-all-start.3 = ((bf16[32,5,32,512]{3,2,1,0:T(8,128)(2,1)}), bf16[32,5,32,512]{3,2,1,0:T(8,128)(2,1)}, u32[]{:S(2)}, u32[]{:S(2)}) async-start(bf16[32,5,32,512]{3,2,1,0:T(8,128)(2,1)} %bitcast.61), calls=%async_computation.4 | async-start | bytes 10485760 | tf_op jit(solution)/shard_map/all_to_all | solution.py:133
  347.0 5.4 %copy-start.9 = (s32[1024]{0:T(1024)S(1)}, s32[1024]{0:T(1024)}, u32[]{:S(2)}) copy-start(s32[1024]{0:T(1024)} %copy-done.8) | copy-start | bytes 12292
  347.0 5.4 %copy-start.14 = (s32[320]{0:T(512)S(1)}, s32[320]{0:T(512)}, u32[]{:S(2)}) copy-start(s32[320]{0:T(512)} %copy-done.13) | copy-start | bytes 3844
  347.0 5.4 %copy-start.18 = (pred[1024]{0:T(1024)(128)(4,1)S(1)}, pred[1024]{0:T(1024)(128)(4,1)}, u32[]{:S(2)}) copy-start(pred[1024]{0:T(1024)(128)(4,1)} %copy-done.17) | copy-start | bytes 3076
  352.4 11.8 %copy-start.3 = (f32[80,32,512]{2,1,0:T(8,128)S(1)}, f32[80,32,512]{2,1,0:T(8,128)}, u32[]{:S(2)}) copy-start(f32[80,32,512]{2,1,0:T(8,128)} %copy.45) | copy-start | bytes 15728644
  364.2 4.0 %copy-start.1 = (bf16[8,320,512]{2,1,0:T(8,128)(2,1)S(1)}, bf16[8,320,512]{2,1,0:T(8,128)(2,1)}, u32[]{:S(2)}) copy-start(bf16[8,320,512]{2,1,0:T(8,128)(2,1)} %param.11) | copy-start | bytes 7864324
Sparse Core Ops, SparseCore 0:
  26.0 55.7 reduce-scatter.1
  196.1 48.1 all-gather.1
where the time goes:
time: 383 us; the launch traced here: 375 us
  waiting for transfers between devices  195 us (51%)
  matrix products  57 us (15%)
  local copies, waits for them, and re-layouts  42.1 us (11%)
  blocking collectives  32.8 us (9%)
  starting transfers between devices  26.7 us (7%)
  between operations  14 us (4%)
  other arithmetic  7.67 us (2%)
    all_to_all x1, waiting for transfers between devices, shards(): lax.all_to_all(packed, 'wide', split_axis=0, concat_axis=0, tiled=True)  113 us
    reduce_scatter x1, waiting for transfers between devices, shards(): lax.psum_scatter(jnp.einsum('alc,lr->rac', grid_adjoint_fields, trig_part...  55.9 us
    all_to_all x1, blocking collectives, shards(): lax.all_to_all(synthesis_output, 'wide', split_axis=2, concat_axis=0, til...  32.8 us
    all_to_all x1, waiting for transfers between devices, shards(): lax.all_to_all(fourier_harmonics, 'wide', split_axis=0, concat_axis=2, ti...  26.1 us
    dot_general x1, matrix products, shards(): jnp.einsum('rac,lr->alc', shard_rows, trig_part, preferred_element_type=j...  11.7 us
    dot_general x1, matrix products, shards(): jnp.einsum('alc,lr->rac', grid_adjoint_fields, trig_part, preferred_eleme...  11.6 us
    all_to_all x1, starting transfers between devices, shards(): lax.all_to_all(fourier_harmonics, 'wide', split_axis=0, concat_axis=2, ti...  10.3 us
    all_to_all x1, starting transfers between devices, shards(): lax.all_to_all(packed, 'wide', split_axis=0, concat_axis=0, tiled=True)  10 us
  transfers between devices with their start and end apart: 5, of which 3 were waited for; matrix products, arithmetic and copies ran while one was open for 8% of the time, Pallas kernels for 0%

commit v1 on v0

v1 whole, which is shorter than its diff:
```python
import math

import numpy as np
import jax
import jax.numpy as jnp
from jax import lax
from jax.experimental import pallas as pl
from jax.experimental.pallas import tpu as pltpu
from jax.sharding import PartitionSpec as P

NLON = 2560
BS = 32
CAP = 5
BF = jnp.bfloat16
F32 = jnp.float32


def _half_sine_coefficients():
    nodes = (np.cos(np.pi * (np.arange(64) + 0.5) / 64) + 1) * 0.5 * (np.pi / 2) ** 2
    root = np.sqrt(nodes)
    return [float(c) for c in np.polynomial.polynomial.polyfit(nodes, np.sin(root) / root, 5)]


SINE = _half_sine_coefficients()


def cosine_of_phase(phase):
    turns = jnp.round(phase * (1.0 / NLON))
    u = (phase - turns * NLON) * (math.pi / NLON)
    z = u * u
    poly = jnp.full_like(z, SINE[-1])
    for coefficient in SINE[-2::-1]:
        poly = poly * z + coefficient
    s = u * poly
    return (1.0 - 2.0 * s * s).astype(BF)


def dft_body(core_ref, t_ref, own_ref, got_ref, *outs):
    for lat in range(own_ref.shape[0]):
        x = jnp.concatenate([own_ref[lat], got_ref[lat]], axis=0)
        r = jnp.dot(t_ref[...], x, preferred_element_type=F32)
        for i, o in enumerate(outs):
            o[lat] = r[128 * i : 128 * i + 128].astype(BF)


def dft(core, table, x, got, step):
    rows = table.shape[0]
    lat, lon, channels = x.shape
    half = channels // 2
    n = rows // 128
    return pl.pallas_call(
        dft_body,
        out_shape=[jax.ShapeDtypeStruct((lat, 128, half), BF)] * n,
        grid_spec=pltpu.PrefetchScalarGridSpec(
            num_scalar_prefetch=1,
            grid=(lat // step,),
            in_specs=[
                pl.BlockSpec((rows, 2 * lon), lambda i, c: (0, 0)),
                pl.BlockSpec((step, lon, half), lambda i, c: (i, 0, c[0])),
                pl.BlockSpec((step, lon, half), lambda i, c: (i, 0, 0)),
            ],
            out_specs=[pl.BlockSpec((step, 128, half), lambda i, c: (i, 0, 0))] * n,
        ),
        compiler_params=pltpu.CompilerParams(vmem_limit_bytes=48 << 20),
        name="dft",
    )(core, table, x, got)


def rows_body(own_a, sum_a, direct_a, own_b, sum_b, direct_b, marks, o_ref, tmp):
    wide, lat, _ = o_ref.shape
    half = own_a.shape[2]
    for s, parts in enumerate(((own_a, sum_a, direct_a), (own_b, sum_b, direct_b))):
        for q in range(4):
            for h in range(half // 128):
                t = tmp.at[(q * (half // 128) + h) % 4]
                lanes = slice(128 * h, 128 * h + 128)
                for l in range(lat):
                    value = sum(p[l, wide * q : wide * q + wide, lanes].astype(F32) for p in parts)
                    value = value * NLON ** (-0.5)
                    for j in range(wide // 8):
                        t[pl.ds(lat * 8 * j + l, 8, stride=lat), :] = value[8 * j : 8 * j + 8]
                col = (s * 4 + q) * half + 128 * h
                o_ref[:, :, col : col + 128] = t[...].astype(BF).reshape(wide, lat, 128)
    o_ref[:, :, 8 * half :] = marks[...]


def to_rows(pieces, marks, wide):
    lat, _, half = pieces[0].shape
    return pl.pallas_call(
        rows_body,
        out_shape=jax.ShapeDtypeStruct((wide, lat, 8 * half + 128), BF),
        scratch_shapes=[pltpu.VMEM((4, wide * lat, 128), F32)],
        compiler_params=pltpu.CompilerParams(vmem_limit_bytes=48 << 20),
        name="to_rows",
    )(*pieces, marks)


def modes_body(f0_ref, f1_ref, mt_ref, m_ref, proj_ref, back_ref, damp_ref, o_ref):
    f = jnp.concatenate([f0_ref[...], f1_ref[...]], axis=1)
    spectra = jnp.dot(mt_ref[0], f, preferred_element_type=F32)
    modal = jnp.dot(spectra.astype(BF), proj_ref[...], preferred_element_type=F32) * damp_ref[...]
    back = jnp.dot(modal.astype(BF), back_ref[...], preferred_element_type=F32).astype(BF)
    synth = jnp.dot(m_ref[0], back, preferred_element_type=F32).astype(BF)
    wide, _, lat, half = o_ref.shape
    o_ref[:, 0] = synth[:, :half].reshape(wide, lat, half)
    o_ref[:, 1] = synth[:, half:].reshape(wide, lat, half)


def modes(f, other, masked_t, masked, proj, back, damp, wide, lat):
    total = f.shape[0]
    slots, degrees, _ = masked_t.shape
    channels = proj.shape[0]
    half = channels // 2
    return pl.pallas_call(
        modes_body,
        out_shape=jax.ShapeDtypeStruct((wide, 2, lat, 4 * half), BF),
        grid=(slots, 2),
        in_specs=[
            pl.BlockSpec((total, half), lambda k, p: (0, p * 2 + k)),
            pl.BlockSpec((total, half), lambda k, p: (0, p * 2 + k)),
            pl.BlockSpec((1, degrees, total), lambda k, p: (k, 0, 0)),
            pl.BlockSpec((1, total, degrees), lambda k, p: (k, 0, 0)),
            pl.BlockSpec((channels, channels), lambda k, p: (0, 0)),
            pl.BlockSpec((channels, channels), lambda k, p: (0, 0)),
            pl.BlockSpec((degrees, channels), lambda k, p: (0, 0)),
        ],
        out_specs=pl.BlockSpec((wide, 2, lat, half), lambda k, p: (0, 0, 0, p * 2 + k)),
        compiler_params=pltpu.CompilerParams(vmem_limit_bytes=48 << 20),
        name="modes",
    )(f, other, masked_t, masked, proj, back, damp)


def columns_body(keep, take, o_a, o_b, tmp):
    wide, lat, _ = take.shape
    half = o_a.shape[2]
    for s, (src, o) in enumerate(((keep, o_a), (take, o_b))):
        for q in range(4):
            for h in range(half // 128):
                t = tmp.at[(q * (half // 128) + h) % 4]
                col = slice(half * q + 128 * h, half * q + 128 * h + 128)
                value = src[:, 0, :, col] if s == 0 else src[:, :, col]
                t[...] = value.astype(F32).reshape(wide * lat, 128)
                for l in range(lat):
                    rows = [t[pl.ds(lat * 8 * j + l, 8, stride=lat), :] for j in range(wide // 8)]
                    rows = jnp.concatenate(rows, axis=0).astype(BF)
                    o[l, wide * q : wide * q + wide, 128 * h : 128 * h + 128] = rows


def to_columns(keep, take):
    wide, lat, width = take.shape
    half = width // 4
    return pl.pallas_call(
        columns_body,
        out_shape=[jax.ShapeDtypeStruct((lat, 4 * wide, half), BF)] * 2,
        grid=(1,),
        in_specs=[
            pl.BlockSpec((wide, 1, lat, width), lambda i: (0, 0, 0, 0)),
            pl.BlockSpec((wide, lat, width), lambda i: (0, 0, 0)),
        ],
        out_specs=[pl.BlockSpec((lat, 4 * wide, half), lambda i: (0, 0, 0))] * 2,
        scratch_shapes=[pltpu.VMEM((4, wide * lat, 128), F32)],
        compiler_params=pltpu.CompilerParams(vmem_limit_bytes=48 << 20),
        name="to_columns",
    )(keep, take)


def idft_body(t_ref, *refs):
    pieces, o_ref = refs[:8], refs[8]
    for lat in range(o_ref.shape[0]):
        g = jnp.concatenate([p[lat] for p in pieces], axis=0)
        r = jnp.dot(t_ref[...], g, preferred_element_type=F32)
        o_ref[lat] = (r * NLON ** (-0.5)).astype(BF)


def idft(table, pieces, step):
    lat, rows, half = pieces[0].shape
    lon = table.shape[0]
    return pl.pallas_call(
        idft_body,
        out_shape=jax.ShapeDtypeStruct((lat, lon, half), BF),
        grid=(lat // step,),
        in_specs=[pl.BlockSpec(table.shape, lambda i: (0, 0))]
        + [pl.BlockSpec((step, rows, half), lambda i: (i, 0, 0))] * 8,
        out_specs=pl.BlockSpec((step, lon, half), lambda i: (i, 0, 0)),
        compiler_params=pltpu.CompilerParams(vmem_limit_bytes=48 << 20),
        name="idft",
    )(table, *pieces)


def pack_body(slot_ref, contrib_ref, *outs):
    blocks = contrib_ref.shape[0]
    rows = contrib_ref.shape[1] // len(outs)

    def step(b, _):
        s = slot_ref[b]
        for i, o in enumerate(outs):
            o[s] = contrib_ref[b, pl.ds(i * rows, rows), :]
        return 0

    lax.fori_loop(0, blocks, step, 0)


def pack(slot, contrib, slots, parts):
    blocks, rows, channels = contrib.shape
    return pl.pallas_call(
        pack_body,
        out_shape=[jax.ShapeDtypeStruct((slots, rows // parts, channels), BF)] * parts,
        grid_spec=pltpu.PrefetchScalarGridSpec(
            num_scalar_prefetch=1,
            grid=(),
            in_specs=[pl.BlockSpec(memory_space=pltpu.VMEM)],
            out_specs=[pl.BlockSpec(memory_space=pltpu.VMEM)] * parts,
        ),
        compiler_params=pltpu.CompilerParams(vmem_limit_bytes=48 << 20),
        name="pack",
    )(slot, contrib)


def deposit_body(target_ref, *refs):
    pieces, o_ref = refs[:-1], refs[-1]
    o_ref[...] = jnp.zeros_like(o_ref)
    slots = pieces[0].shape[0]

    def step(s, _):
        t = target_ref[s]

        @pl.when(t >= 0)
        def _():
            at = 0
            for p in pieces:
                rows = pl.ds(at, p.shape[1])
                o_ref[t, rows, :] = o_ref[t, rows, :] + p[s].astype(F32)
                at += p.shape[1]

        return 0

    lax.fori_loop(0, slots, step, 0)


def deposit(target, pieces, blocks):
    rows = sum(p.shape[1] for p in pieces)
    channels = pieces[0].shape[2]
    return pl.pallas_call(
        deposit_body,
        out_shape=jax.ShapeDtypeStruct((blocks, rows, channels), F32),
        grid_spec=pltpu.PrefetchScalarGridSpec(
            num_scalar_prefetch=1,
            grid=(),
            in_specs=[pl.BlockSpec(memory_space=pltpu.VMEM)] * len(pieces),
            out_specs=pl.BlockSpec(memory_space=pltpu.VMEM),
        ),
        compiler_params=pltpu.CompilerParams(vmem_limit_bytes=48 << 20),
        name="deposit",
    )(target, *pieces)


def finish_body(core_ref, own_ref, got_ref, dep_ref, o_ref):
    half = own_ref.shape[2]
    mine = pl.ds(pl.multiple_of(core_ref[0] * half, half), half)
    other = pl.ds(pl.multiple_of((1 - core_ref[0]) * half, half), half)
    o_ref[:, :, mine] = own_ref[...].astype(F32) + dep_ref[:, :, mine]
    o_ref[:, :, other] = got_ref[...].astype(F32) + dep_ref[:, :, other]


def finish(core, own, got, dep):
    lat, lon, half = own.shape
    return pl.pallas_call(
        finish_body,
        out_shape=jax.ShapeDtypeStruct(dep.shape, F32),
        grid_spec=pltpu.PrefetchScalarGridSpec(
            num_scalar_prefetch=1,
            grid=(lat,),
            in_specs=[
                pl.BlockSpec((1, lon, half), lambda i, c: (i, 0, 0)),
                pl.BlockSpec((1, lon, half), lambda i, c: (i, 0, 0)),
                pl.BlockSpec((1, lon, 2 * half), lambda i, c: (i, 0, 0)),
            ],
            out_specs=pl.BlockSpec((1, lon, 2 * half), lambda i, c: (i, 0, 0)),
        ),
        name="finish",
    )(core, own, got, dep)


def shards(
    grid_adjoint_fields,
    interp_weights,
    depart_owner,
    depart_block,
    wave_perm,
    legendre,
    mode_proj,
    mode_back,
    mode_depth,
):
    x = grid_adjoint_fields
    wide = lax.axis_size("wide")
    narrow = lax.axis_size("narrow")
    w = lax.axis_index("wide")
    v = lax.axis_index("narrow")
    y, core = v // 2, v % 2
    ring = narrow // 2
    lat, lon, channels = x.shape
    half = channels // 2
    slots, lat_total, degrees = legendre.shape
    swap = [(i, i ^ 1) for i in range(narrow)]
    up = [(i, (i + 2) % narrow) for i in range(narrow)]
    down = [(i, (i - 2) % narrow) for i in range(narrow)]
    core_ids = core[None].astype(jnp.int32)

    x_other = jnp.where(core == 0, x[:, :, half:], x[:, :, :half])
    x_got = lax.ppermute(x_other, "narrow", swap)

    order = wave_perm.reshape(wide, ring, 2, slots).transpose(1, 2, 3, 0).reshape(ring, 2, 1, slots * wide)
    order = jnp.concatenate([order, order], axis=0)
    order = jnp.concatenate([order, order[:, :1]], axis=1)
    order = lax.dynamic_slice(order, (y, core, 0, 0), (ring, 2, 1, slots * wide))
    wave = jnp.broadcast_to(order, (ring, 2, 2, slots * wide)).reshape(-1).astype(F32)
    shift = jnp.broadcast_to(
        jnp.array([0.0, 640.0], F32)[None, None, :, None], (ring, 2, 2, slots * wide)
    ).reshape(-1)
    lons = jnp.arange(2 * lon, dtype=jnp.int32) % lon
    side = jnp.arange(2 * lon, dtype=jnp.int32) // lon
    lons = (lons + lon * jnp.where(side == 0, v, v ^ 1)).astype(F32)

    def table(columns):
        return cosine_of_phase(wave[columns][:, None] * lons[None, :] - shift[columns][:, None])

    def table_t(rows):
        return cosine_of_phase(wave[None, :] * lons[rows][:, None] - shift[None, :])

    per = 256
    far_a, far_b = dft(core_ids, table(slice(2 * per, 3 * per)), x, x_got, 4)
    near = jnp.concatenate([wave[3 * per :], wave[: 2 * per]])
    near = cosine_of_phase(
        near[:, None] * lons[None, :] - jnp.concatenate([shift[3 * per :], shift[: 2 * per]])[:, None]
    )
    down_a, down_b, own_a, own_b, up_a, up_b = dft(core_ids, near, x, x_got, 4)

    x_late, own_a = lax.optimization_barrier((x, own_a))
    blocks = interp_weights.shape[0]
    contrib = jnp.einsum(
        "bai,bac->bic", interp_weights, x_late.reshape(blocks, BS, channels), preferred_element_type=F32
    ).astype(BF)
    owner = depart_owner[:, 0]
    ids = jnp.arange(blocks, dtype=jnp.int32)
    rank = jnp.sum(
        ((owner[:, None] == owner[None, :]) & (ids[None, :] < ids[:, None])).astype(jnp.int32), axis=1
    )
    slot = owner * CAP + rank
    pick = jnp.arange(wide * CAP, dtype=jnp.int32)[:, None] == slot[None, :]
    target = jnp.max(jnp.where(pick, depart_block[None, :], -1), axis=1)
    packed = pack(slot, contrib, wide * CAP, 2)

    def send_deposit(piece):
        piece = piece.reshape(wide, CAP * piece.shape[1], channels)
        out = lax.all_to_all(piece, "wide", split_axis=0, concat_axis=0, tiled=True)
        return out.reshape(wide * CAP, -1, channels)

    got_1 = send_deposit(packed[0])

    relay_a = lax.ppermute(far_a, "narrow", up)
    relay_b = lax.ppermute(far_b, "narrow", down)
    direct_b = lax.ppermute(up_b, "narrow", up)
    direct_a = lax.ppermute(down_a, "narrow", down)
    sum_a = lax.ppermute((relay_a.astype(F32) + up_a.astype(F32)).astype(BF), "narrow", up)
    sum_b = lax.ppermute((relay_b.astype(F32) + down_b.astype(F32)).astype(BF), "narrow", down)
    marks = jnp.pad(
        target.reshape(wide, 1, CAP).astype(BF), ((0, 0), (0, lat - 1), (0, 128 - CAP))
    )
    rows = to_rows([own_a, sum_a, direct_a, own_b, sum_b, direct_b], marks, wide)
    rows, got_1 = lax.optimization_barrier((rows, got_1))
    rows = lax.all_to_all(rows, "wide", split_axis=0, concat_axis=0, tiled=True)
    other = lax.ppermute(rows[:, :, 2 * channels : 4 * channels], "narrow", swap)
    targets = rows[:, 0, 4 * channels : 4 * channels + CAP].astype(jnp.int32).reshape(wide * CAP)

    wavenumber = lax.dynamic_slice(wave_perm, ((w * narrow + v) * slots,), (slots,))
    degree_ids = jnp.arange(degrees, dtype=jnp.int32)
    masked = jnp.where(
        degree_ids[None, None, :] >= wavenumber[:, None, None], legendre, jnp.zeros_like(legendre)
    )
    masked_t = masked.transpose(0, 2, 1)
    degree = jnp.arange(degrees, dtype=F32)
    damp = 1.0 / (1.0 + (degree * (degree + 1.0))[:, None] * mode_depth[None, :])
    proj = jnp.where(core == 0, mode_proj, jnp.roll(mode_proj, half, axis=0)).astype(BF)
    back = jnp.where(core == 0, mode_back, jnp.roll(mode_back, half, axis=1)).astype(BF)
    synth = modes(
        rows.reshape(lat_total, -1), other.reshape(lat_total, -1), masked_t, masked, proj, back,
        damp, wide, lat,
    )
    synth = lax.all_to_all(synth, "wide", split_axis=0, concat_axis=0, tiled=True)
    second_piece, synth = lax.optimization_barrier((packed[1], synth))
    got_2 = send_deposit(second_piece)

    block_a, block_b = to_columns(synth, lax.ppermute(synth[:, 1], "narrow", swap))
    below_a = lax.ppermute(block_a, "narrow", up)
    above_b = lax.ppermute(block_b, "narrow", down)
    below_b = lax.ppermute(block_b, "narrow", up)
    above_a = lax.ppermute(block_a, "narrow", down)
    across_a = lax.ppermute(below_a, "narrow", up)
    across_b = lax.ppermute(above_b, "narrow", down)
    pieces = [block_a, block_b, above_a, above_b, across_a, across_b, below_a, below_b]
    wave_got = lax.ppermute(idft(table_t(slice(lon, 2 * lon)), pieces, 4), "narrow", swap)
    wave_own = idft(table_t(slice(0, lon)), pieces, 4)
    dep = deposit(targets, [got_1, got_2], blocks).reshape(lat, lon, channels)
    return finish(core_ids, wave_own, wave_got, dep)


def solution(mesh):
    in_specs = (
        P("wide", "narrow", None),
        P(("wide", "narrow"), None, None),
        P(("wide", "narrow"), None),
        P(("wide", "narrow")),
        P(),
        P(("wide", "narrow"), None, None),
        P(),
        P(),
        P(),
    )
    out_specs = P("wide", "narrow", None)
    return jax.shard_map(shards, mesh=mesh, in_specs=in_specs, out_specs=out_specs, check_vma=False)
```

time: 383 us -> 256 us (0.67); the launches traced: 375 us -> 255 us
  waiting for transfers between devices: 195 us -> 114 us
  matrix products: 57 us -> 2.32 us
  Pallas kernels: 0 us -> 39.5 us
  local copies, waits for them, and re-layouts: 42.1 us -> 18.4 us
  between operations: 14 us -> 0.48 us
  starting transfers between devices: 26.7 us -> 37.3 us
    all_to_all x3, waiting for transfers between devices: 139 us -> 54.3 us  [the longest x1 27.4 us: shards(): rows = lax.all_to_all(rows, 'wide', split_axis=0, concat_axis=0, tiled=True)]
    ppermute x0 -> x16, waiting for transfers between devices: none -> 59.3 us  [the longest x1 11 us: shards(): below_a = lax.ppermute(block_a, 'narrow', up)]
    reduce_scatter x1 -> x0, waiting for transfers between devices: 55.9 us -> none  [shards(): lax.psum_scatter(jnp.einsum('alc,lr->rac', grid_adjoint_fields, trig_part...]
    dot_general x9 -> x1, matrix products: 57 us -> 2.32 us  [shards(): jnp.einsum('bai,bac->bic', interp_weights, x_late.reshape(blocks, BS, cha...]
    pallas_call x0 -> x10, Pallas kernels: none -> 39.5 us  [the longest x1 7.9 us: finish(): pl.pallas_call(finish_body, out_shape=jax.ShapeDtypeStruct(dep.shape, F32...]
    ppermute x0 -> x16, starting transfers between devices: none -> 13.7 us  [the longest x1 2.49 us: shards(): direct_b = lax.ppermute(up_b, 'narrow', up)]
    reshape x5 -> x2, local copies, waits for them, and re-layouts: 13.4 us -> 0.31 us  [shards(): wave_perm.reshape(wide, ring, 2, slots).transpose(1, 2, 3, 0)]
    unnamed x39 -> x56, local copies, waits for them, and re-layouts: 2.67 us -> 14.5 us
  transfers between devices with their start and end apart: 5 -> 19, of which waited for: 3 -> 13; matrix products, arithmetic and copies ran while one was open for 8% -> 6% of each run, Pallas kernels for 0% -> 8%
where the time goes in v1:
time: 256 us; the launch traced here: 255 us
  waiting for transfers between devices  114 us (45%)
  Pallas kernels  39.5 us (15%)
  starting transfers between devices  37.3 us (15%)
  blocking collectives  32.6 us (13%)
  local copies, waits for them, and re-layouts  18.4 us (7%)
  other arithmetic  11.3 us (4%)
    all_to_all x1, blocking collectives, shards(): lax.all_to_all(synth, 'wide', split_axis=0, concat_axis=0, tiled=True)  32.6 us
    all_to_all x1, waiting for transfers between devices, shards(): rows = lax.all_to_all(rows, 'wide', split_axis=0, concat_axis=0, tiled=True)  27.4 us
    all_to_all x2, waiting for transfers between devices, send_deposit(): out = lax.all_to_all(piece, 'wide', split_axis=0, concat_axis=0, tiled=True)  26.8 us
    all_to_all x2, starting transfers between devices, send_deposit(): out = lax.all_to_all(piece, 'wide', split_axis=0, concat_axis=0, tiled=True)  17.2 us
    unnamed x56, local copies, waits for them, and re-layouts  14.5 us
    ppermute x1, waiting for transfers between devices, shards(): below_a = lax.ppermute(block_a, 'narrow', up)  11 us
    ppermute x1, waiting for transfers between devices, shards(): relay_a = lax.ppermute(far_a, 'narrow', up)  9.54 us
    ppermute x1, waiting for transfers between devices, shards(): across_a = lax.ppermute(below_a, 'narrow', up)  8.96 us
  transfers between devices with their start and end apart: 19, of which 13 were waited for; matrix products, arithmetic and copies ran while one was open for 6% of the time, Pallas kernels for 8%

profile of v1, /device:TPU:26, one launch (start us, length us, event | category | flops | bytes accessed | tf_op | source)
XLA Modules:
  0.0 255.4 jit_solution(17907375219756122971)
XLA Ops:
  0.0 1.9 slice_select_fusion
  3.1 1.8 copy.32
  5.1 1.8 fusion.1.t_ref
  7.0 1.1 copy-done.3
  8.1 1.3 copy-done.4
  9.4 4.8 %dft.2 = (bf16[8,128,256]{2,1,0:T(8,128)(2,1)}, bf16[8,128,256]{2,1,0:T(8,128)(2,1)S(1)}, bf16[8,128,256]{2,1,0:T(8,128)(2,1)S(1)}, bf16[8,128,256]{2,1,0:T(8,12...) custom-call(s32[1]{0:T(128)} %bitcast.core_ref, bf16[768,640]{1,0:T(8,128)(2,1)S(1)} %fusion.1.t_ref, ...), custom_call_target="tpu_custom_call" | custom-call | tf_op jit(solution)/shard_map/dft/pallas_call | solution.py:51
  16.6 2.3 convert_bitcast_fusion.contrib_ref
  18.9 2.8 %pack.1 = (bf16[160,16,512]{2,1,0:T(8,128)(2,1)S(1)}, bf16[160,16,512]{2,1,0:T(8,128)(2,1)S(1)}) custom-call(s32[80]{0:T(128)S(1)} %multiply_add_fusion.slot_ref, bf16[80,32,512]{2,1,0:T(8,128)(2,1)} %convert_bitcast_fusion.contrib_ref), custom_call_target="tpu_custom_call" | custom-call | tf_op jit(solution)/shard_map/pack/pallas_call | solution.py:205
  21.7 1.5 copy-done.7
  23.2 1.5 copy-done.8
  24.7 11.7 %all-to-all-start = ((bf16[32,80,512]{2,1,0:T(8,128)(2,1)}), bf16[32,80,512]{2,1,0:T(8,128)(2,1)}, u32[]{:S(2)}, u32[]{:S(2)}) async-start(bf16[32,80,512]{2,1,0:T(8,128)(2,1)} %bitcast.32), calls=%async_computation | async-start | bytes 5242880 | tf_op jit(solution)/shard_map/all_to_all | solution.py:356
  37.0 1.3 copy-done.5
  38.3 1.3 dft.3
  39.9 1.8 collective-permute-start.4
  42.5 2.5 collective-permute-start.6
  45.0 9.5 %collective-permute-done.1 = bf16[8,128,256]{2,1,0:T(8,128)(2,1)S(1)} collective-permute-done((bf16[8,128,256]{2,1,0:T(8,128)(2,1)S(1)}, bf16[8,128,256]{2,1,0:T(8,128)(2,1)S(1)}, u32[]{:S(2)}, u32[]{:S(2)}) %collective-permute-start.1) | collective-permute-done | bytes 524320 | tf_op jit(solution)/shard_map/ppermute | solution.py:361
  55.5 1.4 collective-permute-start.2
  56.9 0.9 add_convert_fusion
  58.7 8.5 %collective-permute-done.3.direct_a = bf16[8,128,256]{2,1,0:T(8,128)(2,1)S(1)} collective-permute-done((bf16[8,128,256]{2,1,0:T(8,128)(2,1)}, bf16[8,128,256]{2,1,0:T(8,128)(2,1)S(1)}, u32[]{:S(2)}, u32[]{:S(2)}) %collective-permute-start.3) | collective-permute-done | bytes 524320 | tf_op jit(solution)/shard_map/ppermute | solution.py:364
  67.2 8.7 %collective-permute-done.2.sum_a = bf16[8,128,256]{2,1,0:T(8,128)(2,1)S(1)} collective-permute-done((bf16[8,128,256]{2,1,0:T(8,128)(2,1)}, bf16[8,128,256]{2,1,0:T(8,128)(2,1)S(1)}, u32[]{:S(2)}, u32[]{:S(2)}) %collective-permute-start.2) | collective-permute-done | bytes 524320 | tf_op jit(solution)/shard_map/ppermute | solution.py:365
  75.9 1.3 collective-permute-done.5.sum_b
  77.2 1.7 to_rows.1
  78.9 18.6 %all-to-all-done = bf16[32,80,512]{2,1,0:T(8,128)(2,1)} async-done(((bf16[32,80,512]{2,1,0:T(8,128)(2,1)}), bf16[32,80,512]{2,1,0:T(8,128)(2,1)}, u32[]{:S(2)}, u32[]{:S(2)}) %all-to-all-start) | async-done | bytes 2621472 | tf_op jit(solution)/shard_map/all_to_all | solution.py:356
  97.5 6.4 %all-to-all-start.1 = ((bf16[32,8,2176]{2,1,0:T(8,128)(2,1)}), bf16[32,8,2176]{2,1,0:T(8,128)(2,1)S(1)}, u32[]{:S(2)}, u32[]{:S(2)}) async-start(bf16[32,8,2176]{2,1,0:T(8,128)(2,1)} %to_rows.1), calls=%async_computation.1 | async-start | bytes 2228224 | tf_op jit(solution)/shard_map/all_to_all | solution.py:372
  106.1 27.4 %all-to-all-done.1 = bf16[32,8,2176]{2,1,0:T(8,128)(2,1)S(1)} async-done(((bf16[32,8,2176]{2,1,0:T(8,128)(2,1)}), bf16[32,8,2176]{2,1,0:T(8,128)(2,1)S(1)}, u32[]{:S(2)}, u32[]{:S(2)}) %all-to-all-start.1) | async-done | bytes 1114144 | tf_op jit(solution)/shard_map/all_to_all | solution.py:372
  133.7 1.5 copy-done.16
  135.5 1.3 fusion.15
  136.8 4.6 %modes.1 = bf16[32,2,8,1024]{3,2,1,0:T(8,128)(2,1)S(1)} custom-call(bf16[256,2176]{1,0:T(8,128)(2,1)S(1)} %bitcast.30, bf16[256,1024]{1,0:T(8,128)(2,1)S(1)} %bitcast.33, bf16[2,512,256]{2,1,0:T(8,128)(2,1)S(1)} %copy.34.mt_ref, bf16[2,256,512]{2,1,0:T(8,128)(2,1)S(1)} %broadcast_select_fusion.m_ref, bf16[512,512]{1,0:T(8,128)(2,1)S(1)} %get-tuple-element.53.proj_ref, ...), custom_call_target="tpu_custom_call" | custom-call | tf_op jit(solution)/shard_map/modes/pallas_call | solution.py:114
  141.4 32.6 %all_to_all.20.keep = bf16[32,2,8,1024]{3,2,1,0:T(8,128)(2,1)} all-to-all(bf16[32,2,8,1024]{3,2,1,0:T(8,128)(2,1)S(1)} %modes.1), channel_id=1, replica_groups=mesh['wide'=32,'narrow'=8] {'wide'}, dimensions={0} | all-to-all | bytes 2097152 | tf_op jit(solution)/shard_map/all_to_all | solution.py:390
  174.0 5.6 %all-to-all-start.3 = ((bf16[32,80,512]{2,1,0:T(8,128)(2,1)}), bf16[32,80,512]{2,1,0:T(8,128)(2,1)S(1)}, u32[]{:S(2)}, u32[]{:S(2)}) async-start(bf16[32,80,512]{2,1,0:T(8,128)(2,1)} %bitcast.31), calls=%async_computation.3 | async-start | bytes 5242880 | tf_op jit(solution)/shard_map/all_to_all | solution.py:356
  179.6 1.2 slice_bitcast_fusion
  180.9 1.9 collective-permute-done.8.take
  182.8 1.6 to_columns.1
  184.6 1.8 collective-permute-start.10
  186.4 1.4 collective-permute-start.14
  188.5 11.0 %collective-permute-done.11.refs_6_ = bf16[8,128,256]{2,1,0:T(8,128)(2,1)} collective-permute-done((bf16[8,128,256]{2,1,0:T(8,128)(2,1)}, bf16[8,128,256]{2,1,0:T(8,128)(2,1)}, u32[]{:S(2)}, u32[]{:S(2)}) %collective-permute-start.11) | collective-permute-done | bytes 524320 | tf_op jit(solution)/shard_map/ppermute | solution.py:395
  199.4 1.4 collective-permute-start.12
  201.8 2.2 fusion.8
  203.9 6.7 %collective-permute-done.14.refs_7_ = bf16[8,128,256]{2,1,0:T(8,128)(2,1)} collective-permute-done((bf16[8,128,256]{2,1,0:T(8,128)(2,1)}, bf16[8,128,256]{2,1,0:T(8,128)(2,1)}, u32[]{:S(2)}, u32[]{:S(2)}) %collective-permute-start.14) | collective-permute-done | bytes 524320 | tf_op jit(solution)/shard_map/ppermute | solution.py:397
  210.6 1.5 collective-permute-done.9.refs_2_
  212.1 9.0 %collective-permute-done.12.refs_4_ = bf16[8,128,256]{2,1,0:T(8,128)(2,1)} collective-permute-done((bf16[8,128,256]{2,1,0:T(8,128)(2,1)}, bf16[8,128,256]{2,1,0:T(8,128)(2,1)}, u32[]{:S(2)}, u32[]{:S(2)}) %collective-permute-start.12) | collective-permute-done | bytes 524320 | tf_op jit(solution)/shard_map/ppermute | solution.py:399
  221.1 1.2 collective-permute-done.13.refs_5_
  222.3 4.1 %idft.3 = bf16[8,320,256]{2,1,0:T(8,128)(2,1)} custom-call(bf16[320,1024]{1,0:T(8,128)(2,1)S(1)} %get-tuple-element.45.t_ref, bf16[8,128,256]{2,1,0:T(8,128)(2,1)} %get-tuple-element.37.refs_0_, bf16[8,128,256]{2,1,0:T(8,128)(2,1)} %get-tuple-element.38.refs_1_, bf16[8,128,256]{2,1,0:T(8,128)(2,1)} %collective-permute-done.9.refs_2_, ...), custom_call_target="tpu_custom_call" | custom-call | tf_op jit(solution)/shard_map/idft/pallas_call | solution.py:178
  227.4 3.3 %idft.2.own_ref = bf16[8,320,256]{2,1,0:T(8,128)(2,1)S(1)} custom-call(bf16[320,1024]{1,0:T(8,128)(2,1)S(1)} %get-tuple-element.46.t_ref, bf16[8,128,256]{2,1,0:T(8,128)(2,1)} %get-tuple-element.37.refs_0_, bf16[8,128,256]{2,1,0:T(8,128)(2,1)} %get-tuple-element.38.refs_1_, bf16[8,128,256]{2,1,0:T(8,128)(2,1)} %collective-permute-done.9.refs_2_, ...), custom_call_target="tpu_custom_call" | custom-call | tf_op jit(solution)/shard_map/idft/pallas_call | solution.py:178
  230.7 1.0 copy-done.6
  231.7 8.3 %all-to-all-done.3 = bf16[32,80,512]{2,1,0:T(8,128)(2,1)S(1)} async-done(((bf16[32,80,512]{2,1,0:T(8,128)(2,1)}), bf16[32,80,512]{2,1,0:T(8,128)(2,1)S(1)}, u32[]{:S(2)}, u32[]{:S(2)}) %all-to-all-start.3) | async-done | bytes 2621472 | tf_op jit(solution)/shard_map/all_to_all | solution.py:356
  240.0 7.5 %deposit.1 = f32[80,32,512]{2,1,0:T(8,128)} custom-call(s32[160]{0:T(256)S(1)} %reshape.152.target_ref, bf16[160,16,512]{2,1,0:T(8,128)(2,1)} %bitcast.10.refs_0_, bf16[160,16,512]{2,1,0:T(8,128)(2,1)S(1)} %bitcast.29), custom_call_target="tpu_custom_call" | custom-call | tf_op jit(solution)/shard_map/deposit/pallas_call | solution.py:243
  247.5 7.9 %finish.1 = f32[8,320,512]{2,1,0:T(8,128)} custom-call(s32[1]{0:T(128)} %bitcast.core_ref, bf16[8,320,256]{2,1,0:T(8,128)(2,1)} %copy-done.6, bf16[8,320,256]{2,1,0:T(8,128)(2,1)} %collective-permute-done.15.got_ref, f32[8,320,512]{2,1,0:T(8,128)} %bitcast.34), custom_call_target="tpu_custom_call" | custom-call | tf_op jit(solution)/shard_map/finish/pallas_call | solution.py:267
  (110 shorter events, 12.8 us)
Async XLA Ops:
  0.0 2.0 copy-start.23
  0.0 2.8 %copy-start.22 = (f32[2]{0:T(128)S(1)}, f32[2]{0:T(128)}, u32[]{:S(2)}) copy-start(f32[2]{0:T(128)} %constant.58.clone) | copy-start | bytes 28
  0.0 3.1 %copy-start.21 = (bf16[80,32,32]{0,2,1:T(8,128)(2,1)S(1)}, bf16[80,32,32]{0,2,1:T(8,128)(2,1)}, u32[]{:S(2)}) copy-start(bf16[80,32,32]{0,2,1:T(8,128)(2,1)} %param.11) | copy-start | bytes 491524
  1.9 3.0 %copy-start.26 = (s32[80,1]{0,1:T(1,128)S(1)}, s32[80,1]{0,1:T(1,128)}, u32[]{:S(2)}) copy-start(s32[80,1]{0,1:T(1,128)} %param.12) | copy-start | bytes 964
  1.9 5.1 %collective-permute-start = (bf16[8,320,256]{2,1,0:T(8,128)(2,1)S(1)}, bf16[8,320,256]{2,1,0:T(8,128)(2,1)S(1)}, u32[]{:S(2)}, u32[]{:S(2)}) collective-permute-start(bf16[8,320,256]{2,1,0:T(8,128)(2,1)S(1)} %slice_select_fusion), channel_id=1, source_target_pairs={{0,1},{1,0},{2,3},{3,2},{4,5},{5,4},{6,7},{7,6},{8,9},{9,8},{10,11... | collective-permute-start | bytes 3932168 | tf_op jit(solution)/shard_map/ppermute | solution.py:311
  7.0 1.1 copy-start.3
  8.1 1.3 copy-start.4
  9.4 7.2 %copy-start = (bf16[8,320,512]{2,1,0:T(8,128)(2,1)S(1)}, bf16[8,320,512]{2,1,0:T(8,128)(2,1)}, u32[]{:S(2)}) copy-start(bf16[8,320,512]{2,1,0:T(8,128)(2,1)} %own_ref.3) | copy-start | bytes 7864324
  9.4 7.2 %copy-start.15 = (bf16[80,32,32]{1,2,0:T(8,128)(2,1)S(1)}, bf16[80,32,32]{1,2,0:T(8,128)(2,1)}, u32[]{:S(2)}) copy-start(bf16[80,32,32]{1,2,0:T(8,128)(2,1)} %copy.32) | copy-start | bytes 491524
  14.1 0.8 copy-start.9
  15.0 0.8 copy-start.11
  15.8 0.8 copy-start.13
  21.7 1.5 copy-start.7
  23.2 1.5 copy-start.8
  24.7 72.9 %all-to-all-start = ((bf16[32,80,512]{2,1,0:T(8,128)(2,1)}), bf16[32,80,512]{2,1,0:T(8,128)(2,1)}, u32[]{:S(2)}, u32[]{:S(2)}) async-start(bf16[32,80,512]{2,1,0:T(8,128)(2,1)} %bitcast.32), calls=%async_computation | async-start | bytes 5242880 | tf_op jit(solution)/shard_map/all_to_all | solution.py:356
  37.0 1.3 copy-start.5
  38.3 16.2 %copy-start.14 = (bf16[8,128,256]{2,1,0:T(8,128)(2,1)S(1)}, bf16[8,128,256]{2,1,0:T(8,128)(2,1)}, u32[]{:S(2)}) copy-start(bf16[8,128,256]{2,1,0:T(8,128)(2,1)} %copy-done.13) | copy-start | bytes 1572868
  39.6 17.3 %copy-start.12 = (bf16[8,128,256]{2,1,0:T(8,128)(2,1)S(1)}, bf16[8,128,256]{2,1,0:T(8,128)(2,1)}, u32[]{:S(2)}) copy-start(bf16[8,128,256]{2,1,0:T(8,128)(2,1)} %copy-done.11) | copy-start | bytes 1572868
  39.6 14.9 %collective-permute-start.1 = (bf16[8,128,256]{2,1,0:T(8,128)(2,1)S(1)}, bf16[8,128,256]{2,1,0:T(8,128)(2,1)S(1)}, u32[]{:S(2)}, u32[]{:S(2)}) collective-permute-start(bf16[8,128,256]{2,1,0:T(8,128)(2,1)S(1)} %get-tuple-element.27), channel_id=1, source_target_pairs={{0,2},{1,3},{2,4},{3,5},{4,6},{5,7},{6,0},{7,1},{8,10},{9,11},{10,... | collective-permute-start | bytes 1572872 | tf_op jit(solution)/shard_map/ppermute | solution.py:361
  39.9 17.0 %collective-permute-start.4 = (bf16[8,128,256]{2,1,0:T(8,128)(2,1)S(1)}, bf16[8,128,256]{2,1,0:T(8,128)(2,1)S(1)}, u32[]{:S(2)}, u32[]{:S(2)}) collective-permute-start(bf16[8,128,256]{2,1,0:T(8,128)(2,1)S(1)} %get-tuple-element.31), channel_id=1, source_target_pairs={{0,6},{1,7},{2,0},{3,1},{4,2},{5,3},{6,4},{7,5},{8,14},{9,15},{10,... | collective-permute-start | bytes 1572872 | tf_op jit(solution)/shard_map/ppermute | solution.py:362
  41.7 25.5 %collective-permute-start.3 = (bf16[8,128,256]{2,1,0:T(8,128)(2,1)}, bf16[8,128,256]{2,1,0:T(8,128)(2,1)S(1)}, u32[]{:S(2)}, u32[]{:S(2)}) collective-permute-start(bf16[8,128,256]{2,1,0:T(8,128)(2,1)} %get-tuple-element.29), channel_id=1, source_target_pairs={{0,6},{1,7},{2,0},{3,1},{4,2},{5,3},{6,4},{7,5},{8,14},{9,15},{10,... | collective-permute-start | bytes 1572872 | tf_op jit(solution)/shard_map/ppermute | solution.py:364
  42.5 24.7 %collective-permute-start.6 = (bf16[8,128,256]{2,1,0:T(8,128)(2,1)}, bf16[8,128,256]{2,1,0:T(8,128)(2,1)S(1)}, u32[]{:S(2)}, u32[]{:S(2)}) collective-permute-start(bf16[8,128,256]{2,1,0:T(8,128)(2,1)} %get-tuple-element.33), channel_id=1, source_target_pairs={{0,2},{1,3},{2,4},{3,5},{4,6},{5,7},{6,0},{7,1},{8,10},{9,11},{10,... | collective-permute-start | bytes 1572872 | tf_op jit(solution)/shard_map/ppermute | solution.py:363
  54.5 3.9 %copy-start.25 = (s32[80]{0:T(128)S(1)}, s32[80]{0:T(128)}, u32[]{:S(2)}) copy-start(s32[80]{0:T(128)} %param.13) | copy-start | bytes 964
  54.5 22.7 %copy-start.10 = (bf16[8,128,256]{2,1,0:T(8,128)(2,1)S(1)}, bf16[8,128,256]{2,1,0:T(8,128)(2,1)}, u32[]{:S(2)}) copy-start(bf16[8,128,256]{2,1,0:T(8,128)(2,1)} %copy-done.9) | copy-start | bytes 1572868
  55.5 20.5 %collective-permute-start.2 = (bf16[8,128,256]{2,1,0:T(8,128)(2,1)}, bf16[8,128,256]{2,1,0:T(8,128)(2,1)S(1)}, u32[]{:S(2)}, u32[]{:S(2)}) collective-permute-start(bf16[8,128,256]{2,1,0:T(8,128)(2,1)} %add_convert_fusion.1), channel_id=1, source_target_pairs={{0,2},{1,3},{2,4},{3,5},{4,6},{5,7},{6,0},{7,1},{8,10},{9,11},{10,... | collective-permute-start | bytes 1572872 | tf_op jit(solution)/shard_map/ppermute | solution.py:365
  57.8 19.4 %collective-permute-start.5 = (bf16[8,128,256]{2,1,0:T(8,128)(2,1)}, bf16[8,128,256]{2,1,0:T(8,128)(2,1)S(1)}, u32[]{:S(2)}, u32[]{:S(2)}) collective-permute-start(bf16[8,128,256]{2,1,0:T(8,128)(2,1)} %add_convert_fusion), channel_id=1, source_target_pairs={{0,6},{1,7},{2,0},{3,1},{4,2},{5,3},{6,4},{7,5},{8,14},{9,15},{10,... | collective-permute-start | bytes 1572872 | tf_op jit(solution)/shard_map/ppermute | solution.py:366
  78.9 25.1 %copy-start.19 = (bf16[2,256,512]{2,1,0:T(8,128)(2,1)S(1)}, bf16[2,256,512]{2,1,0:T(8,128)(2,1)}, u32[]{:S(2)}) copy-start(bf16[2,256,512]{2,1,0:T(8,128)(2,1)} %param.15) | copy-start | bytes 1572868
  97.5 36.0 %all-to-all-start.1 = ((bf16[32,8,2176]{2,1,0:T(8,128)(2,1)}), bf16[32,8,2176]{2,1,0:T(8,128)(2,1)S(1)}, u32[]{:S(2)}, u32[]{:S(2)}) async-start(bf16[32,8,2176]{2,1,0:T(8,128)(2,1)} %to_rows.1), calls=%async_computation.1 | async-start | bytes 2228224 | tf_op jit(solution)/shard_map/all_to_all | solution.py:372
  103.9 1.2 copy-start.17
  104.3 1.6 copy-start.20
  104.3 1.6 copy-start.24
  133.5 3.3 %copy-start.1 = (bf16[32,8,2176]{2,1,0:T(8,128)(2,1)}, bf16[32,8,2176]{2,1,0:T(8,128)(2,1)S(1)}, u32[]{:S(2)}) copy-start(bf16[32,8,2176]{2,1,0:T(8,128)(2,1)S(1)} %all-to-all-done.1) | copy-start | bytes 3342340
  133.6 1.6 copy-start.16
  133.6 1.9 copy-start.18
  133.6 3.2 %collective-permute-start.7 = (bf16[32,8,1024]{2,1,0:T(8,128)(2,1)S(1)}, bf16[32,8,1024]{2,1,0:T(8,128)(2,1)S(1)}, u32[]{:S(2)}, u32[]{:S(2)}) collective-permute-start(bf16[32,8,1024]{2,1,0:T(8,128)(2,1)S(1)} %slice.113), channel_id=1, source_target_pairs={{0,1},{1,0},{2,3},{3,2},{4,5},{5,4},{6,7},{7,6},{8,9},{9,8},{10,11... | collective-permute-start | bytes 1572872 | tf_op jit(solution)/shard_map/ppermute | solution.py:373
  174.0 66.0 %all-to-all-start.3 = ((bf16[32,80,512]{2,1,0:T(8,128)(2,1)}), bf16[32,80,512]{2,1,0:T(8,128)(2,1)S(1)}, u32[]{:S(2)}, u32[]{:S(2)}) async-start(bf16[32,80,512]{2,1,0:T(8,128)(2,1)} %bitcast.31), calls=%async_computation.3 | async-start | bytes 5242880 | tf_op jit(solution)/shard_map/all_to_all | solution.py:356
  179.6 3.2 %copy-start.2 = (bf16[32,2,8,1024]{3,2,1,0:T(8,128)(2,1)S(1)}, bf16[32,2,8,1024]{3,2,1,0:T(8,128)(2,1)}, u32[]{:S(2)}) copy-start(bf16[32,2,8,1024]{3,2,1,0:T(8,128)(2,1)} %all_to_all.20.keep) | copy-start | bytes 3145732
  180.8 2.0 collective-permute-start.8
  184.3 15.1 %collective-permute-start.11 = (bf16[8,128,256]{2,1,0:T(8,128)(2,1)}, bf16[8,128,256]{2,1,0:T(8,128)(2,1)}, u32[]{:S(2)}, u32[]{:S(2)}) collective-permute-start(bf16[8,128,256]{2,1,0:T(8,128)(2,1)} %get-tuple-element.37.refs_0_), channel_id=1, source_target_pairs={{0,2},{1,3},{2,4},{3,5},{4,6},{5,7},{6,0},{7,1},{8,10},{9,11},{10,... | collective-permute-start | bytes 1572872 | tf_op jit(solution)/shard_map/ppermute | solution.py:395
  184.6 16.3 %collective-permute-start.10 = (bf16[8,128,256]{2,1,0:T(8,128)(2,1)}, bf16[8,128,256]{2,1,0:T(8,128)(2,1)}, u32[]{:S(2)}, u32[]{:S(2)}) collective-permute-start(bf16[8,128,256]{2,1,0:T(8,128)(2,1)} %get-tuple-element.38.refs_1_), channel_id=1, source_target_pairs={{0,6},{1,7},{2,0},{3,1},{4,2},{5,3},{6,4},{7,5},{8,14},{9,15},{10,... | collective-permute-start | bytes 1572872 | tf_op jit(solution)/shard_map/ppermute | solution.py:396
  186.4 24.2 %collective-permute-start.14 = (bf16[8,128,256]{2,1,0:T(8,128)(2,1)}, bf16[8,128,256]{2,1,0:T(8,128)(2,1)}, u32[]{:S(2)}, u32[]{:S(2)}) collective-permute-start(bf16[8,128,256]{2,1,0:T(8,128)(2,1)} %get-tuple-element.38.refs_1_), channel_id=1, source_target_pairs={{0,2},{1,3},{2,4},{3,5},{4,6},{5,7},{6,0},{7,1},{8,10},{9,11},{10,... | collective-permute-start | bytes 1572872 | tf_op jit(solution)/shard_map/ppermute | solution.py:397
  187.9 24.3 %collective-permute-start.9 = (bf16[8,128,256]{2,1,0:T(8,128)(2,1)}, bf16[8,128,256]{2,1,0:T(8,128)(2,1)}, u32[]{:S(2)}, u32[]{:S(2)}) collective-permute-start(bf16[8,128,256]{2,1,0:T(8,128)(2,1)} %get-tuple-element.37.refs_0_), channel_id=1, source_target_pairs={{0,6},{1,7},{2,0},{3,1},{4,2},{5,3},{6,4},{7,5},{8,14},{9,15},{10,... | collective-permute-start | bytes 1572872 | tf_op jit(solution)/shard_map/ppermute | solution.py:398
  199.4 21.7 %collective-permute-start.12 = (bf16[8,128,256]{2,1,0:T(8,128)(2,1)}, bf16[8,128,256]{2,1,0:T(8,128)(2,1)}, u32[]{:S(2)}, u32[]{:S(2)}) collective-permute-start(bf16[8,128,256]{2,1,0:T(8,128)(2,1)} %collective-permute-done.11.refs_6_), channel_id=1, source_target_pairs={{0,2},{1,3},{2,4},{3,5},{4,6},{5,7},{6,0},{7,1},{8,10},{9,11},{10,... | collective-permute-start | bytes 1572872 | tf_op jit(solution)/shard_map/ppermute | solution.py:399
  200.9 21.4 %collective-permute-start.13 = (bf16[8,128,256]{2,1,0:T(8,128)(2,1)}, bf16[8,128,256]{2,1,0:T(8,128)(2,1)}, u32[]{:S(2)}, u32[]{:S(2)}) collective-permute-start(bf16[8,128,256]{2,1,0:T(8,128)(2,1)} %collective-permute-done.10.refs_3_), channel_id=1, source_target_pairs={{0,6},{1,7},{2,0},{3,1},{4,2},{5,3},{6,4},{7,5},{8,14},{9,15},{10,... | collective-permute-start | bytes 1572872 | tf_op jit(solution)/shard_map/ppermute | solution.py:400
  226.4 21.1 %collective-permute-start.15 = (bf16[8,320,256]{2,1,0:T(8,128)(2,1)}, bf16[8,320,256]{2,1,0:T(8,128)(2,1)}, u32[]{:S(2)}, u32[]{:S(2)}) collective-permute-start(bf16[8,320,256]{2,1,0:T(8,128)(2,1)} %idft.3), channel_id=1, source_target_pairs={{0,1},{1,0},{2,3},{3,2},{4,5},{5,4},{6,7},{7,6},{8,9},{9,8},{10,11... | collective-permute-start | bytes 3932168 | tf_op jit(solution)/shard_map/ppermute | solution.py:402
  230.7 1.1 copy-start.6

commit v2 on v1

v2 whole, which is shorter than its diff:
```python
import math

import numpy as np
import jax
import jax.numpy as jnp
from jax import lax
from jax.experimental import pallas as pl
from jax.experimental.pallas import tpu as pltpu
from jax.sharding import PartitionSpec as P

NLON = 2560
BS = 32
CAP = 5
COUNTS = (2, 3)
BF = jnp.bfloat16
F32 = jnp.float32


def _half_sine_coefficients():
    nodes = (np.cos(np.pi * (np.arange(64) + 0.5) / 64) + 1) * 0.5 * (np.pi / 2) ** 2
    root = np.sqrt(nodes)
    return [float(c) for c in np.polynomial.polynomial.polyfit(nodes, np.sin(root) / root, 5)]


SINE = _half_sine_coefficients()


def cosine_of_phase(phase):
    turns = jnp.round(phase * (1.0 / NLON))
    u = (phase - turns * NLON) * (math.pi / NLON)
    z = u * u
    poly = jnp.full_like(z, SINE[-1])
    for coefficient in SINE[-2::-1]:
        poly = poly * z + coefficient
    s = u * poly
    return (1.0 - 2.0 * s * s).astype(BF)


def hbm(value):
    return pltpu.with_memory_space_constraint(value, pltpu.HBM)


def half_body(side_ref, x_ref, o_ref):
    o_ref[...] = x_ref[...]


def take_half(side, x):
    lat, lon, channels = x.shape
    half = channels // 2
    step = lat // 2
    return pl.pallas_call(
        half_body,
        out_shape=jax.ShapeDtypeStruct((lat, lon, half), BF),
        grid_spec=pltpu.PrefetchScalarGridSpec(
            num_scalar_prefetch=1,
            grid=(lat // step,),
            in_specs=[pl.BlockSpec((step, lon, half), lambda i, c: (i, 0, c[0]))],
            out_specs=pl.BlockSpec((step, lon, half), lambda i, c: (i, 0, 0)),
        ),
        name="take_half",
    )(side, x)


def dft_body(core_ref, t_ref, own_ref, got_ref, *outs):
    for lat in range(own_ref.shape[0]):
        x = jnp.concatenate([own_ref[lat], got_ref[lat]], axis=0)
        r = jnp.dot(t_ref[...], x, preferred_element_type=F32)
        for i, o in enumerate(outs):
            o[lat] = r[128 * i : 128 * i + 128].astype(BF)


def dft(core, table, x, got, step):
    rows = table.shape[0]
    lat, lon, channels = x.shape
    half = channels // 2
    n = rows // 128
    return pl.pallas_call(
        dft_body,
        out_shape=[jax.ShapeDtypeStruct((lat, 128, half), BF)] * n,
        grid_spec=pltpu.PrefetchScalarGridSpec(
            num_scalar_prefetch=1,
            grid=(lat // step,),
            in_specs=[
                pl.BlockSpec((rows, 2 * lon), lambda i, c: (0, 0)),
                pl.BlockSpec((step, lon, half), lambda i, c: (i, 0, c[0])),
                pl.BlockSpec((step, lon, half), lambda i, c: (i, 0, 0)),
            ],
            out_specs=[pl.BlockSpec((step, 128, half), lambda i, c: (i, 0, 0))] * n,
        ),
        compiler_params=pltpu.CompilerParams(vmem_limit_bytes=48 << 20),
        name="dft",
    )(core, table, x, got)


def rows_body(own_a, sum_a, direct_a, own_b, sum_b, direct_b, marks, o_hbm, o_other, o_mine, tmp, sem):
    wide, lat, width = o_mine.shape
    copies = [
        pltpu.make_async_copy(marks, o_hbm.at[:, :, pl.ds(2 * width, 128)], sem.at[0]),
        pltpu.make_async_copy(o_mine, o_hbm.at[:, :, pl.ds(0, width)], sem.at[1]),
    ]
    copies[0].start()
    half = own_a.shape[2]
    for s, parts in enumerate(((own_a, sum_a, direct_a), (own_b, sum_b, direct_b))):
        for q in range(4):
            for h in range(half // 128):
                t = tmp.at[(q * (half // 128) + h) % 4]
                lanes = slice(128 * h, 128 * h + 128)
                for l in range(lat):
                    value = sum(p[l, wide * q : wide * q + wide, lanes].astype(F32) for p in parts)
                    value = value * NLON ** (-0.5)
                    for j in range(wide // 8):
                        t[pl.ds(lat * 8 * j + l, 8, stride=lat), :] = value[8 * j : 8 * j + 8]
                col = q * half + 128 * h
                o_ref = (o_mine, o_other)[s]
                o_ref[:, :, col : col + 128] = t[...].astype(BF).reshape(wide, lat, 128)
        if s == 0:
            copies[1].start()
    for c in copies:
        c.wait()


def to_rows(pieces, marks, wide):
    lat, _, half = pieces[0].shape
    part = jax.ShapeDtypeStruct((wide, lat, 4 * half), BF)
    whole = jax.ShapeDtypeStruct((wide, lat, 8 * half + 128), BF)
    vmem, free = pl.BlockSpec(memory_space=pltpu.VMEM), pl.BlockSpec(memory_space=pl.ANY)
    return pl.pallas_call(
        rows_body,
        out_shape=[whole, part],
        in_specs=[vmem] * 7,
        out_specs=[free, vmem],
        scratch_shapes=[
            pltpu.VMEM(part.shape, BF),
            pltpu.VMEM((4, wide * lat, 128), F32),
            pltpu.SemaphoreType.DMA((2,)),
        ],
        compiler_params=pltpu.CompilerParams(vmem_limit_bytes=48 << 20),
        name="to_rows",
    )(*pieces, marks)


def join_body(rows_ref, got_ref, o_ref, sem):
    wide, _, width = got_ref.shape
    part = wide // 4
    copies = [
        pltpu.make_async_copy(
            got_ref.at[pl.ds(part * i, part)],
            o_ref.at[pl.ds(part * i, part), :, pl.ds(width, width)],
            sem.at[i],
        )
        for i in range(4)
    ]
    for c in copies:
        c.start()
    for c in copies:
        c.wait()


def join(rows, got):
    free = pl.BlockSpec(memory_space=pl.ANY)
    return pl.pallas_call(
        join_body,
        out_shape=jax.ShapeDtypeStruct(rows.shape, BF),
        in_specs=[free, pl.BlockSpec(memory_space=pltpu.VMEM)],
        out_specs=free,
        input_output_aliases={0: 0},
        scratch_shapes=[pltpu.SemaphoreType.DMA((4,))],
        name="join",
    )(rows, got)


def modes_body(ids_ref, fa_ref, fb_ref, fc_ref, fd_ref, leg_ref, p0_ref, p1_ref, b0_ref, b1_ref, depth_ref, o_ref, damp_ref):
    half = fa_ref.shape[1]
    degrees = leg_ref.shape[2]

    @pl.when(pl.program_id(0) == 0)
    def _():
        n = lax.broadcasted_iota(jnp.int32, damp_ref.shape, 0).astype(F32)
        damp_ref[...] = 1.0 / (1.0 + n * (n + 1.0) * depth_ref[...])

    degree = lax.broadcasted_iota(jnp.int32, leg_ref.shape[1:], 1)
    leg = leg_ref[0].astype(F32)
    leg = jnp.where(degree >= ids_ref[1 + pl.program_id(0)], leg, jnp.zeros_like(leg))
    turned = leg.T.astype(BF)
    leg = leg.astype(BF)
    spectra = [
        jnp.dot(turned, f[...], preferred_element_type=F32).astype(BF)
        for f in (fa_ref, fb_ref, fc_ref, fd_ref)
    ]
    low = jnp.concatenate([spectra[0], spectra[2]], axis=0)
    high = jnp.concatenate([spectra[1], spectra[3]], axis=0)
    modal = jnp.dot(low, p0_ref[...], preferred_element_type=F32)
    modal += jnp.dot(high, p1_ref[...], preferred_element_type=F32)
    modal = jnp.concatenate(
        [(modal[degrees * p : degrees * p + degrees] * damp_ref[...]).astype(BF) for p in range(2)], axis=0
    )
    wide, _, lat, _ = o_ref.shape
    for i, b_ref in enumerate((b0_ref, b1_ref)):
        back = jnp.dot(modal, b_ref[...], preferred_element_type=F32).astype(BF)
        for p in range(2):
            synth = jnp.dot(leg, back[degrees * p : degrees * p + degrees], preferred_element_type=F32)
            o_ref[:, i, :, half * p : half * p + half] = synth.astype(BF).reshape(wide, lat, half)


def modes(ids, f, legendre, proj, back, depth, wide, lat):
    slots, total, degrees = legendre.shape
    channels = proj.shape[0]
    half = channels // 2
    part = [pl.BlockSpec((total, half), lambda k, c, j=j: (0, j + 2 * k)) for j in (0, 4, 1, 5)]
    return pl.pallas_call(
        modes_body,
        out_shape=jax.ShapeDtypeStruct((wide, 2, lat, 4 * half), BF),
        grid_spec=pltpu.PrefetchScalarGridSpec(
            num_scalar_prefetch=1,
            grid=(slots,),
            in_specs=part
            + [
                pl.BlockSpec((1, total, degrees), lambda k, c: (k, 0, 0)),
                pl.BlockSpec((half, channels), lambda k, c: (c[0], 0)),
                pl.BlockSpec((half, channels), lambda k, c: (1 - c[0], 0)),
                pl.BlockSpec((channels, half), lambda k, c: (0, c[0])),
                pl.BlockSpec((channels, half), lambda k, c: (0, 1 - c[0])),
                pl.BlockSpec((1, channels), lambda k, c: (0, 0)),
            ],
            out_specs=pl.BlockSpec((wide, 2, lat, 2 * half), lambda k, c: (0, 0, 0, k)),
            scratch_shapes=[pltpu.VMEM((degrees, channels), F32)],
        ),
        compiler_params=pltpu.CompilerParams(vmem_limit_bytes=48 << 20),
        name="modes",
    )(ids, f, f, f, f, legendre, proj, proj, back, back, depth)


def columns_body(keep, take, o_ref, tmp):
    wide, lat, _ = take.shape
    half = o_ref.shape[3]
    for s, src in enumerate((keep, take)):
        for q in range(4):
            for h in range(half // 128):
                t = tmp.at[(q * (half // 128) + h) % 4]
                col = slice(half * q + 128 * h, half * q + 128 * h + 128)
                value = src[:, 0, :, col] if s == 0 else src[:, :, col]
                t[...] = value.astype(F32).reshape(wide * lat, 128)
                for l in range(lat):
                    rows = [t[pl.ds(lat * 8 * j + l, 8, stride=lat), :] for j in range(wide // 8)]
                    rows = jnp.concatenate(rows, axis=0).astype(BF)
                    o_ref[s, l, wide * q : wide * q + wide, 128 * h : 128 * h + 128] = rows


def to_columns(keep, take):
    wide, lat, width = take.shape
    half = width // 4
    return pl.pallas_call(
        columns_body,
        out_shape=jax.ShapeDtypeStruct((2, lat, 4 * wide, half), BF),
        grid=(1,),
        in_specs=[
            pl.BlockSpec((wide, 1, lat, width), lambda i: (0, 0, 0, 0)),
            pl.BlockSpec((wide, lat, width), lambda i: (0, 0, 0)),
        ],
        out_specs=pl.BlockSpec((2, lat, 4 * wide, half), lambda i: (0, 0, 0, 0)),
        scratch_shapes=[pltpu.VMEM((4, wide * lat, 128), F32)],
        compiler_params=pltpu.CompilerParams(vmem_limit_bytes=48 << 20),
        name="to_columns",
    )(keep, take)


def idft_body(t_ref, own, above, across_a, across_b, below, o_ref):
    for lat in range(o_ref.shape[0]):
        g = [own[0, lat], own[1, lat], above[0, lat], above[1, lat]]
        g += [across_a[lat], across_b[lat], below[0, lat], below[1, lat]]
        r = jnp.dot(t_ref[...], jnp.concatenate(g, axis=0), preferred_element_type=F32)
        o_ref[lat] = (r * NLON ** (-0.5)).astype(BF)


def idft(table, own, above, across_a, across_b, below, step):
    _, lat, rows, half = own.shape
    lon = table.shape[0]
    pair = pl.BlockSpec((2, step, rows, half), lambda i: (0, i, 0, 0))
    single = pl.BlockSpec((step, rows, half), lambda i: (i, 0, 0))
    return pl.pallas_call(
        idft_body,
        out_shape=jax.ShapeDtypeStruct((lat, lon, half), BF),
        grid=(lat // step,),
        in_specs=[pl.BlockSpec(table.shape, lambda i: (0, 0)), pair, pair, single, single, pair],
        out_specs=pl.BlockSpec((step, lon, half), lambda i: (i, 0, 0)),
        compiler_params=pltpu.CompilerParams(vmem_limit_bytes=48 << 20),
        name="idft",
    )(table, own, above, across_a, across_b, below)


def pack(owner, rank, contrib, owners, first, count):
    blocks, rows, channels = contrib.shape

    def body(owner_ref, rank_ref, contrib_ref, o_ref):
        def step(b, _):
            r = rank_ref[b] - first

            @pl.when((r >= 0) & (r < count))
            def _():
                o_ref[owner_ref[b], r] = contrib_ref[b]

            return 0

        lax.fori_loop(0, blocks, step, 0)

    return pl.pallas_call(
        body,
        out_shape=jax.ShapeDtypeStruct((owners, count, rows, channels), BF),
        grid_spec=pltpu.PrefetchScalarGridSpec(
            num_scalar_prefetch=2,
            grid=(),
            in_specs=[pl.BlockSpec(memory_space=pltpu.VMEM)],
            out_specs=pl.BlockSpec(memory_space=pltpu.VMEM),
        ),
        compiler_params=pltpu.CompilerParams(vmem_limit_bytes=48 << 20),
        name="pack",
    )(owner, rank, contrib)


def finish(core, own, got, lists, pieces):
    lat, lon, half = own.shape
    n = len(pieces)
    blocks = lon // BS

    def body(core_ref, start, order, target, own_hbm, got_hbm, *refs):
        pieces_hbm, (o_hbm, own_ref, got_ref, out, sem, out_sem) = refs[:n], refs[n : n + 6]
        piece_refs = refs[n + 6 :]
        copies, k = [], 0
        for p, dst in zip(pieces_hbm, piece_refs):
            part = p.shape[0] // 4
            for j in range(4):
                rows = pl.ds(j * part, part)
                copies.append(pltpu.make_async_copy(p.at[rows], dst.at[rows], sem.at[k]))
                k += 1
        for src, dst in ((own_hbm, own_ref), (got_hbm, got_ref)):
            for j in range(2):
                rows = pl.ds(j * (lat // 2), lat // 2)
                copies.append(pltpu.make_async_copy(src.at[rows], dst.at[rows], sem.at[k]))
                k += 1
        for c in copies:
            c.start()
        for c in copies:
            c.wait()
        mine = pl.ds(pl.multiple_of(core_ref[0] * half, half), half)
        other = pl.ds(pl.multiple_of((1 - core_ref[0]) * half, half), half)

        def write(i):
            return pltpu.make_async_copy(out.at[i], o_hbm.at[i], out_sem.at[i])

        def latitude(i, _):
            out[i, :, mine] = own_ref[i].astype(F32)
            out[i, :, other] = got_ref[i].astype(F32)

            for p, piece in enumerate(piece_refs):

                def step(e, _):
                    s = order[p, e]
                    rows = pl.ds(pl.multiple_of((target[p, s] - i * blocks) * BS, BS), BS)
                    out[i, rows, :] = out[i, rows, :] + piece[s].astype(F32)
                    return 0

                lax.fori_loop(start[p, i], start[p, i + 1], step, 0)
            write(i).start()
            return 0

        lax.fori_loop(0, lat, latitude, 0)
        for i in range(lat):
            write(i).wait()

    return pl.pallas_call(
        body,
        out_shape=jax.ShapeDtypeStruct((lat, lon, 2 * half), F32),
        grid_spec=pltpu.PrefetchScalarGridSpec(
            num_scalar_prefetch=4,
            grid=(),
            in_specs=[pl.BlockSpec(memory_space=pl.ANY)] * (2 + n),
            out_specs=pl.BlockSpec(memory_space=pl.ANY),
            scratch_shapes=[
                pltpu.VMEM((lat, lon, half), BF),
                pltpu.VMEM((lat, lon, half), BF),
                pltpu.VMEM((lat, lon, 2 * half), F32),
                pltpu.SemaphoreType.DMA((4 + 4 * n,)),
                pltpu.SemaphoreType.DMA((lat,)),
            ]
            + [pltpu.VMEM(p.shape, BF) for p in pieces],
        ),
        compiler_params=pltpu.CompilerParams(vmem_limit_bytes=48 << 20),
        name="finish",
    )(core, *lists, own, got, *pieces)


def by_latitude(target, lat, blocks):
    ids = jnp.arange(target.shape[0], dtype=jnp.int32)
    before = (target[None, :] < target[:, None]) | (
        (target[None, :] == target[:, None]) & (ids[None, :] < ids[:, None])
    )
    place = jnp.sum(before.astype(jnp.int32), axis=1)
    order = jnp.sum(jnp.where(place[None, :] == ids[:, None], ids[None, :], 0), axis=1)
    first = jnp.arange(lat + 1, dtype=jnp.int32) * blocks
    start = jnp.sum((target[None, :] < first[:, None]).astype(jnp.int32), axis=1)
    return start, order, target


def shards(
    grid_adjoint_fields,
    interp_weights,
    depart_owner,
    depart_block,
    wave_perm,
    legendre,
    mode_proj,
    mode_back,
    mode_depth,
):
    x = grid_adjoint_fields
    wide = lax.axis_size("wide")
    narrow = lax.axis_size("narrow")
    w = lax.axis_index("wide")
    v = lax.axis_index("narrow")
    y, core = v // 2, v % 2
    ring = narrow // 2
    lat, lon, channels = x.shape
    half = channels // 2
    slots, lat_total, degrees = legendre.shape
    swap = [(i, i ^ 1) for i in range(narrow)]
    up = [(i, (i + 2) % narrow) for i in range(narrow)]
    down = [(i, (i - 2) % narrow) for i in range(narrow)]
    core_ids = core[None].astype(jnp.int32)

    x_got = lax.ppermute(take_half(1 - core_ids, hbm(x)), "narrow", swap)

    order = wave_perm.reshape(wide, ring, 2, slots).transpose(1, 2, 3, 0)
    order = jnp.concatenate([order, order], axis=0)
    order = jnp.concatenate([order, order[:, :1]], axis=1)
    order = lax.dynamic_slice(order, (y, core, 0, 0), (ring, 2, slots, wide))[:, :, :, None]
    columns = (ring, 2, slots, 2, wide)
    wave = jnp.broadcast_to(order, columns).reshape(-1).astype(F32)
    shift = jnp.tile(jnp.repeat(jnp.array([0.0, 640.0], F32), wide), ring * 2 * slots)
    lons = jnp.arange(2 * lon, dtype=jnp.int32) % lon
    side = jnp.arange(2 * lon, dtype=jnp.int32) // lon
    lons = (lons + lon * jnp.where(side == 0, v, v ^ 1)).astype(F32)

    def table(columns):
        return cosine_of_phase(wave[columns][:, None] * lons[None, :] - shift[columns][:, None])

    def table_t(rows):
        return cosine_of_phase(wave[None, :] * lons[rows][:, None] - shift[None, :])

    blocks = interp_weights.shape[0]
    contrib = jnp.einsum(
        "bai,bac->bic", interp_weights, x.reshape(blocks, BS, channels), preferred_element_type=F32
    ).astype(BF)
    owner = depart_owner[:, 0]
    ids = jnp.arange(blocks, dtype=jnp.int32)
    rank = jnp.sum(
        ((owner[:, None] == owner[None, :]) & (ids[None, :] < ids[:, None])).astype(jnp.int32), axis=1
    )
    slot = owner * CAP + rank
    pick = jnp.arange(wide * CAP, dtype=jnp.int32)[:, None] == slot[None, :]
    target = jnp.max(jnp.where(pick, depart_block[None, :], -1), axis=1)
    cut = [0]
    for n in COUNTS:
        cut.append(cut[-1] + n)

    def send_deposit(piece):
        out = lax.all_to_all(
            piece.reshape(wide, -1, channels), "wide", split_axis=0, concat_axis=0, tiled=True
        )
        return out.reshape(-1, BS, channels)

    piece_1 = pack(owner, rank, contrib, wide, cut[0], COUNTS[0])
    got_1 = send_deposit(piece_1)

    per = 256
    x_late, piece_1 = lax.optimization_barrier((x, piece_1))
    x = x_late
    far_a, far_b = dft(core_ids, table(slice(2 * per, 3 * per)), x, x_got, 4)

    near = jnp.concatenate([wave[3 * per :], wave[: 2 * per]])
    near_shift = jnp.concatenate([shift[3 * per :], shift[: 2 * per]])
    near = cosine_of_phase(near[:, None] * lons[None, :] - near_shift[:, None])
    down_a, down_b, own_a, own_b, up_a, up_b = dft(core_ids, near, x, x_got, 4)

    relay_a = lax.ppermute(far_a, "narrow", up)
    relay_b = lax.ppermute(far_b, "narrow", down)
    direct_b = lax.ppermute(up_b, "narrow", up)
    direct_a = lax.ppermute(down_a, "narrow", down)
    sum_a = lax.ppermute((relay_a.astype(F32) + up_a.astype(F32)).astype(BF), "narrow", up)
    sum_b = lax.ppermute((relay_b.astype(F32) + down_b.astype(F32)).astype(BF), "narrow", down)
    marks = jnp.pad(
        target.reshape(wide, 1, CAP).astype(BF), ((0, 0), (0, lat - 1), (0, 128 - CAP))
    )
    slot_waves = lax.dynamic_slice(wave_perm, ((w * narrow + v) * slots,), (slots,))
    mode_ids = jnp.concatenate([core_ids, slot_waves])
    proj, back = mode_proj.astype(BF), mode_back.astype(BF)
    piece_2 = pack(owner, rank, contrib, wide, cut[1], COUNTS[1])
    own_a, piece_2, proj, back, marks = lax.optimization_barrier(
        (own_a, piece_2, proj, back, marks)
    )
    rows, other = to_rows([own_a, sum_a, direct_a, own_b, sum_b, direct_b], marks, wide)
    rows = join(rows, lax.ppermute(other, "narrow", swap))
    rows, got_1 = lax.optimization_barrier((rows, got_1))
    rows = lax.all_to_all(rows, "wide", split_axis=0, concat_axis=0, tiled=True)
    targets = rows[:, 0, 4 * channels : 4 * channels + CAP].astype(jnp.int32)
    most = wide * max(COUNTS)
    lists = []
    for a, b in zip(cut, cut[1:]):
        part = targets[:, a:b].reshape(-1)
        lists.append(by_latitude(jnp.pad(part, (0, most - part.shape[0]), constant_values=-1), lat, lon // BS))
    lists = [jnp.stack(group) for group in zip(*lists)]
    synth = modes(
        mode_ids, rows.reshape(lat_total, -1), hbm(legendre), hbm(proj), hbm(back),
        mode_depth.reshape(1, -1), wide, lat,
    )
    synth = lax.all_to_all(synth, "wide", split_axis=0, concat_axis=0, tiled=True)
    piece_2, synth = lax.optimization_barrier((piece_2, synth))
    got_2 = send_deposit(piece_2)

    own = to_columns(synth, lax.ppermute(synth[:, 1], "narrow", swap))
    below = lax.ppermute(own, "narrow", up)
    above = lax.ppermute(own, "narrow", down)
    across_a = lax.ppermute(below[0], "narrow", up)
    across_b = lax.ppermute(above[1], "narrow", down)
    pieces = [own, above, across_a, across_b, below]
    wave_got = lax.ppermute(idft(table_t(slice(lon, 2 * lon)), *pieces, 4), "narrow", swap)
    wave_own = idft(table_t(slice(0, lon)), *pieces, 4)
    return finish(core_ids, wave_own, wave_got, lists, [hbm(got_1), hbm(got_2)])


def solution(mesh):
    in_specs = (
        P("wide", "narrow", None),
        P(("wide", "narrow"), None, None),
        P(("wide", "narrow"), None),
        P(("wide", "narrow")),
        P(),
        P(("wide", "narrow"), None, None),
        P(),
        P(),
        P(),
    )
    out_specs = P("wide", "narrow", None)
    return jax.shard_map(shards, mesh=mesh, in_specs=in_specs, out_specs=out_specs, check_vma=False)
```

time: 256 us -> 238 us (0.930)
  waiting for transfers between devices: 114 us -> 98.7 us
  local copies, waits for them, and re-layouts: 18.4 us -> 15.5 us
    all_to_all x2, waiting for transfers between devices: 26.8 us -> 13.7 us  [send_deposit(): lax.all_to_all(piece.reshape(wide, -1, channels), 'wide', split_axis=0, c...]
    ppermute x10 -> x8, waiting for transfers between devices: 31.3 us -> 39.5 us  [the longest x1 23.2 us: shards(): below = lax.ppermute(own, 'narrow', up)]
    ppermute x1, waiting for transfers between devices: 9.54 us -> 2.88 us  [shards(): relay_a = lax.ppermute(far_a, 'narrow', up)]
    ppermute x1, waiting for transfers between devices: 8.5 us -> 2.71 us  [shards(): direct_a = lax.ppermute(down_a, 'narrow', down)]
    pallas_call x5 -> x7, Pallas kernels: 21.5 us -> 17.1 us  [the longest x1 6.27 us: finish(): pl.pallas_call(body, out_shape=jax.ShapeDtypeStruct((lat, lon, 2 * half),...]
    all_to_all x1, starting transfers between devices: 6.35 us -> 9.79 us  [shards(): rows = lax.all_to_all(rows, 'wide', split_axis=0, concat_axis=0, tiled=True)]
    pallas_call x1, Pallas kernels: 4.6 us -> 7.3 us  [modes(): pl.pallas_call(modes_body, out_shape=jax.ShapeDtypeStruct((wide, 2, lat,...]
    unnamed x56 -> x39, local copies, waits for them, and re-layouts: 14.5 us -> 12 us
  transfers between devices with their start and end apart: 19 -> 17, of which waited for: 13 -> 12; matrix products, arithmetic and copies ran while one was open for 6% -> 6% of each run, Pallas kernels for 8% -> 9%
where the time goes in v2:
time: 238 us; the launch traced here: 237 us
  waiting for transfers between devices  98.7 us (41%)
  starting transfers between devices  38.7 us (16%)
  Pallas kernels  38 us (16%)
  blocking collectives  32.4 us (14%)
  local copies, waits for them, and re-layouts  15.5 us (7%)
  other arithmetic  10.9 us (5%)
  matrix products  2.56 us (1%)
    all_to_all x1, blocking collectives, shards(): lax.all_to_all(synth, 'wide', split_axis=0, concat_axis=0, tiled=True)  32.4 us
    all_to_all x1, waiting for transfers between devices, shards(): rows = lax.all_to_all(rows, 'wide', split_axis=0, concat_axis=0, tiled=True)  29.6 us
    ppermute x1, waiting for transfers between devices, shards(): below = lax.ppermute(own, 'narrow', up)  23.2 us
    all_to_all x2, starting transfers between devices, send_deposit(): lax.all_to_all(piece.reshape(wide, -1, channels), 'wide', split_axis=0, c...  17.3 us
    all_to_all x2, waiting for transfers between devices, send_deposit(): lax.all_to_all(piece.reshape(wide, -1, channels), 'wide', split_axis=0, c...  13.7 us
    unnamed x39, local copies, waits for them, and re-layouts  12 us
    all_to_all x1, starting transfers between devices, shards(): rows = lax.all_to_all(rows, 'wide', split_axis=0, concat_axis=0, tiled=True)  9.79 us
    ppermute x1, waiting for transfers between devices, shards(): lax.ppermute((relay_a.astype(F32) + up_a.astype(F32)).astype(BF), 'narrow...  8.98 us
  transfers between devices with their start and end apart: 17, of which 12 were waited for; matrix products, arithmetic and copies ran while one was open for 6% of the time, Pallas kernels for 9%

profile of v2, /device:TPU:26, one launch (start us, length us, event | category | flops | bytes accessed | tf_op | source)
XLA Modules:
  0.0 237.4 jit_solution(2144963395491440583)
XLA Ops:
  0.0 0.9 convert_reduce_fusion.2.rank_ref
  0.9 2.1 copy.33
  3.0 2.6 %convolution_convert_fusion.contrib_ref = bf16[80,32,512]{2,1,0:T(8,128)(2,1)S(1)} fusion(bf16[80,32,32]{1,2,0:T(8,128)(2,1)S(1)} %copy.33, bf16[80,32,512]{2,1,0:T(8,128)(2,1)} %bitcast.29), kind=kOutput, calls=%fused_computation.1 | convolution fusion | flops 85196800 | bytes 5406720 | tf_op jit(solution)/shard_map/bai,bac->bic/dot_general | solution.py:450
  5.6 3.3 %pack.2 = bf16[32,2,32,512]{3,2,1,0:T(8,128)(2,1)} custom-call(s32[80]{0:T(128)S(1)} %bitcast.37, s32[80]{0:T(128)S(1)} %convert_reduce_fusion.2.rank_ref, bf16[80,32,512]{2,1,0:T(8,128)(2,1)S(1)} %convolution_convert_fusion.contrib_ref), custom_call_target="tpu_custom_call" | custom-call | tf_op jit(solution)/shard_map/pack/pallas_call | solution.py:306
  8.8 11.7 %all-to-all-start = ((bf16[32,64,512]{2,1,0:T(8,128)(2,1)}), bf16[32,64,512]{2,1,0:T(8,128)(2,1)}, u32[]{:S(2)}, u32[]{:S(2)}) async-start(bf16[32,64,512]{2,1,0:T(8,128)(2,1)} %bitcast.6), calls=%async_computation | async-start | bytes 4194304 | tf_op jit(solution)/shard_map/all_to_all | solution.py:466
  20.6 2.3 take_half.1
  24.6 1.7 collective-permute-done.got_ref
  26.3 2.3 dft.3
  28.9 1.8 collective-permute-start.4
  30.8 1.8 fusion.1.t_ref
  32.6 4.8 %dft.2 = (bf16[8,128,256]{2,1,0:T(8,128)(2,1)}, bf16[8,128,256]{2,1,0:T(8,128)(2,1)S(1)}, bf16[8,128,256]{2,1,0:T(8,128)(2,1)S(1)}, bf16[8,128,256]{2,1,0:T(8,12...) custom-call(s32[1]{0:T(128)} %bitcast.core_ref, bf16[768,640]{1,0:T(8,128)(2,1)S(1)} %fusion.1.t_ref, ...), custom_call_target="tpu_custom_call" | custom-call | tf_op jit(solution)/shard_map/dft/pallas_call | solution.py:77
  38.1 2.5 %collective-permute-start.6 = (bf16[8,128,256]{2,1,0:T(8,128)(2,1)}, bf16[8,128,256]{2,1,0:T(8,128)(2,1)S(1)}, u32[]{:S(2)}, u32[]{:S(2)}) collective-permute-start(bf16[8,128,256]{2,1,0:T(8,128)(2,1)} %get-tuple-element.34), channel_id=1, source_target_pairs={{0,2},{1,3},{2,4},{3,5},{4,6},{5,7},{6,0},{7,1},{8,10},{9,11},{10,... | collective-permute-start | bytes 1572872 | tf_op jit(solution)/shard_map/ppermute | solution.py:486
  40.6 2.9 %collective-permute-done.1 = bf16[8,128,256]{2,1,0:T(8,128)(2,1)S(1)} collective-permute-done((bf16[8,128,256]{2,1,0:T(8,128)(2,1)S(1)}, bf16[8,128,256]{2,1,0:T(8,128)(2,1)S(1)}, u32[]{:S(2)}, u32[]{:S(2)}) %collective-permute-start.1) | collective-permute-done | bytes 524320 | tf_op jit(solution)/shard_map/ppermute | solution.py:484
  43.5 0.9 add_convert_fusion.1
  44.4 0.9 collective-permute-start.2
  45.3 1.0 add_convert_fusion
  46.3 1.1 collective-permute-start.5
  47.4 1.8 pack.3
  49.2 1.7 copy-done.3
  50.9 0.9 convert_element_type.99.p0_ref.p1_ref
  53.5 2.7 %collective-permute-done.3.direct_a = bf16[8,128,256]{2,1,0:T(8,128)(2,1)S(1)} collective-permute-done((bf16[8,128,256]{2,1,0:T(8,128)(2,1)}, bf16[8,128,256]{2,1,0:T(8,128)(2,1)S(1)}, u32[]{:S(2)}, u32[]{:S(2)}) %collective-permute-start.3) | collective-permute-done | bytes 524320 | tf_op jit(solution)/shard_map/ppermute | solution.py:487
  56.2 9.0 %collective-permute-done.2.sum_a = bf16[8,128,256]{2,1,0:T(8,128)(2,1)S(1)} collective-permute-done((bf16[8,128,256]{2,1,0:T(8,128)(2,1)}, bf16[8,128,256]{2,1,0:T(8,128)(2,1)S(1)}, u32[]{:S(2)}, u32[]{:S(2)}) %collective-permute-start.2) | collective-permute-done | bytes 524320 | tf_op jit(solution)/shard_map/ppermute | solution.py:488
  65.2 1.3 collective-permute-done.5.sum_b
  66.5 0.9 to_rows.1
  67.4 1.0 copy-done.9
  68.4 1.9 collective-permute-done.7.got_ref
  71.1 1.9 join.1
  73.1 9.8 %all-to-all-start.1 = ((bf16[32,8,2176]{2,1,0:T(8,128)(2,1)}), bf16[32,8,2176]{2,1,0:T(8,128)(2,1)S(1)}, u32[]{:S(2)}, u32[]{:S(2)}) async-start(bf16[32,8,2176]{2,1,0:T(8,128)(2,1)} %join.1), calls=%async_computation.1 | async-start | bytes 2228224 | tf_op jit(solution)/shard_map/all_to_all | solution.py:503
  83.1 29.6 %all-to-all-done.1 = bf16[32,8,2176]{2,1,0:T(8,128)(2,1)S(1)} async-done(((bf16[32,8,2176]{2,1,0:T(8,128)(2,1)}), bf16[32,8,2176]{2,1,0:T(8,128)(2,1)S(1)}, u32[]{:S(2)}, u32[]{:S(2)}) %all-to-all-start.1) | async-done | bytes 1114144 | tf_op jit(solution)/shard_map/all_to_all | solution.py:503
  112.7 7.3 %modes.1 = bf16[32,2,8,1024]{3,2,1,0:T(8,128)(2,1)S(1)} custom-call(s32[3]{0:T(128)S(1)} %pad_add_fusion.4.ids_ref, bf16[256,2176]{1,0:T(8,128)(2,1)S(1)} %bitcast.30, bf16[256,2176]{1,0:T(8,128)(2,1)S(1)} %bitcast.31, bf16[256,2176]{1,0:T(8,128)(2,1)S(1)} %bitcast.32, bf16[256,2176]{1,0:T(8,128)(2,1)S(1)} %bitcast.33, bf16[2,256,512]{2,1,0:T(8,128)(2,1)} %leg_ref.1, ...), custom_call_target="tpu_custom_call" | custom-call | tf_op jit(solution)/shard_map/modes/pallas_call | solution.py:210
  120.0 32.4 %all_to_all.20.keep = bf16[32,2,8,1024]{3,2,1,0:T(8,128)(2,1)S(1)} all-to-all(bf16[32,2,8,1024]{3,2,1,0:T(8,128)(2,1)S(1)} %modes.1), channel_id=1, replica_groups=mesh['wide'=32,'narrow'=8] {'wide'}, dimensions={0} | all-to-all | bytes 2097152 | tf_op jit(solution)/shard_map/all_to_all | solution.py:515
  152.4 5.6 %all-to-all-start.3 = ((bf16[32,96,512]{2,1,0:T(8,128)(2,1)}), bf16[32,96,512]{2,1,0:T(8,128)(2,1)}, u32[]{:S(2)}, u32[]{:S(2)}) async-start(bf16[32,96,512]{2,1,0:T(8,128)(2,1)} %bitcast.34), calls=%async_computation.3 | async-start | bytes 6291456 | tf_op jit(solution)/shard_map/all_to_all | solution.py:466
  158.2 1.9 collective-permute-done.8.take
  160.9 1.8 collective-permute-start.9
  162.7 23.2 %collective-permute-done.10.below = bf16[2,8,128,256]{3,2,1,0:T(8,128)(2,1)S(1)} collective-permute-done((bf16[2,8,128,256]{3,2,1,0:T(8,128)(2,1)S(1)}, bf16[2,8,128,256]{3,2,1,0:T(8,128)(2,1)S(1)}, u32[]{:S(2)}, u32[]{:S(2)}) %collective-permute-start.10) | collective-permute-done | bytes 1048608 | tf_op jit(solution)/shard_map/ppermute | solution.py:520
  186.8 1.5 collective-permute-start.11
  189.1 1.1 copy-done.4
  190.9 2.9 %fusion.8 = (bf16[320,1024]{1,0:T(8,128)(2,1)S(1)}, bf16[320,1024]{1,0:T(8,128)(2,1)}) fusion(f32[320]{0:T(512)S(1)} %get-tuple-element.51, f32[1024]{0:T(1024)S(1)} %sub.80, f32[1024]{0:T(1024)S(1)} %convert_element_type.116, f32[320]{0:T(512)S(1)} %get-tuple-element.52), kind=kLoop, calls=%fused_computation.15 | loop fusion | flops 15073280 | bytes 1321472 | tf_op jit(solution)/shard_map/convert_element_type | solution.py:36
  193.9 6.4 %collective-permute-done.11.across_a = bf16[8,128,256]{2,1,0:T(8,128)(2,1)} collective-permute-done((bf16[8,128,256]{2,1,0:T(8,128)(2,1)}, bf16[8,128,256]{2,1,0:T(8,128)(2,1)}, u32[]{:S(2)}, u32[]{:S(2)}) %collective-permute-start.11) | collective-permute-done | bytes 524320 | tf_op jit(solution)/shard_map/ppermute | solution.py:522
  200.3 4.3 %collective-permute-done.12.across_b = bf16[8,128,256]{2,1,0:T(8,128)(2,1)} collective-permute-done((bf16[8,128,256]{2,1,0:T(8,128)(2,1)}, bf16[8,128,256]{2,1,0:T(8,128)(2,1)}, u32[]{:S(2)}, u32[]{:S(2)}) %collective-permute-start.12) | collective-permute-done | bytes 524320 | tf_op jit(solution)/shard_map/ppermute | solution.py:523
  204.6 3.7 %idft.3 = bf16[8,320,256]{2,1,0:T(8,128)(2,1)} custom-call(bf16[320,1024]{1,0:T(8,128)(2,1)S(1)} %get-tuple-element.47.t_ref, bf16[2,8,128,256]{3,2,1,0:T(8,128)(2,1)S(1)} %to_columns.1.own, bf16[2,8,128,256]{3,2,1,0:T(8,128)(2,1)S(1)} %copy-done.5, bf16[8,128,256]{2,1,0:T(8,128)(2,1)} %collective-permute-done.11.across_a, ...), custom_call_target="tpu_custom_call" | custom-call | tf_op jit(solution)/shard_map/idft/pallas_call | solution.py:280
  209.6 1.2 copy-done.6
  210.8 1.1 copy-done.10
  211.9 2.8 %idft.2.own_hbm = bf16[8,320,256]{2,1,0:T(8,128)(2,1)S(1)} custom-call(bf16[320,1024]{1,0:T(8,128)(2,1)S(1)} %copy-done.10, bf16[2,8,128,256]{3,2,1,0:T(8,128)(2,1)S(1)} %to_columns.1.own, bf16[2,8,128,256]{3,2,1,0:T(8,128)(2,1)S(1)} %copy-done.6, bf16[8,128,256]{2,1,0:T(8,128)(2,1)} %collective-permute-done.11.across_a, ...), custom_call_target="tpu_custom_call" | custom-call | tf_op jit(solution)/shard_map/idft/pallas_call | solution.py:280
  214.7 1.2 copy-done.7
  215.9 13.7 %all-to-all-done.3 = bf16[32,96,512]{2,1,0:T(8,128)(2,1)} async-done(((bf16[32,96,512]{2,1,0:T(8,128)(2,1)}), bf16[32,96,512]{2,1,0:T(8,128)(2,1)}, u32[]{:S(2)}, u32[]{:S(2)}) %all-to-all-start.3) | async-done | bytes 3145760 | tf_op jit(solution)/shard_map/all_to_all | solution.py:466
  229.6 1.3 copy-done.8
  230.9 6.3 %finish.1 = f32[8,320,512]{2,1,0:T(8,128)} custom-call(s32[1]{0:T(128)} %bitcast.core_ref, s32[2,9]{1,0:T(2,128)S(1)} %pad_add_fusion.1.start, s32[2,96]{1,0:T(2,128)S(1)} %pad_add_fusion.2.order, s32[2,96]{1,0:T(2,128)S(1)} %pad_add_fusion.3.target, bf16[8,320,256]{2,1,0:T(8,128)(2,1)S(1)} %copy-done.8, ...), custom_call_target="tpu_custom_call" | custom-call | tf_op jit(solution)/shard_map/finish/pallas_call | solution.py:370
  (99 shorter events, 10.0 us)
Async XLA Ops:
  3.0 2.6 %copy-start.12 = (s32[80,1]{0,1:T(1,128)S(1)}, s32[80,1]{0,1:T(1,128)}, u32[]{:S(2)}) copy-start(s32[80,1]{0,1:T(1,128)} %param.12) | copy-start | bytes 964
  5.6 3.3 %copy-start.1 = (bf16[80,32,512]{2,1,0:T(8,128)(2,1)}, bf16[80,32,512]{2,1,0:T(8,128)(2,1)S(1)}, u32[]{:S(2)}) copy-start(bf16[80,32,512]{2,1,0:T(8,128)(2,1)S(1)} %convolution_convert_fusion.contrib_ref) | copy-start | bytes 7864324
  8.8 64.2 %all-to-all-start = ((bf16[32,64,512]{2,1,0:T(8,128)(2,1)}), bf16[32,64,512]{2,1,0:T(8,128)(2,1)}, u32[]{:S(2)}, u32[]{:S(2)}) async-start(bf16[32,64,512]{2,1,0:T(8,128)(2,1)} %bitcast.6), calls=%async_computation | async-start | bytes 4194304 | tf_op jit(solution)/shard_map/all_to_all | solution.py:466
  20.6 2.4 %copy-start.16 = (s32[512]{0:T(512)S(1)}, s32[512]{0:T(512)}, u32[]{:S(2)}) copy-start(s32[512]{0:T(512)} %param.14) | copy-start | bytes 6148
  20.6 3.0 %copy-start.18 = (f32[2]{0:T(128)S(1)}, f32[2]{0:T(128)}, u32[]{:S(2)}) copy-start(f32[2]{0:T(128)} %constant.63.clone) | copy-start | bytes 28
  20.6 5.7 %copy-start = (bf16[8,320,512]{2,1,0:T(8,128)(2,1)S(1)}, bf16[8,320,512]{2,1,0:T(8,128)(2,1)}, u32[]{:S(2)}) copy-start(bf16[8,320,512]{2,1,0:T(8,128)(2,1)} %own_ref.1) | copy-start | bytes 7864324
  22.9 3.4 %collective-permute-start = (bf16[8,320,256]{2,1,0:T(8,128)(2,1)}, bf16[8,320,256]{2,1,0:T(8,128)(2,1)}, u32[]{:S(2)}, u32[]{:S(2)}) collective-permute-start(bf16[8,320,256]{2,1,0:T(8,128)(2,1)} %take_half.1), channel_id=1, source_target_pairs={{0,1},{1,0},{2,3},{3,2},{4,5},{5,4},{6,7},{7,6},{8,9},{9,8},{10,11... | collective-permute-start | bytes 3932168 | tf_op jit(solution)/shard_map/ppermute | solution.py:430
  28.6 14.8 %collective-permute-start.1 = (bf16[8,128,256]{2,1,0:T(8,128)(2,1)S(1)}, bf16[8,128,256]{2,1,0:T(8,128)(2,1)S(1)}, u32[]{:S(2)}, u32[]{:S(2)}) collective-permute-start(bf16[8,128,256]{2,1,0:T(8,128)(2,1)S(1)} %get-tuple-element.28), channel_id=1, source_target_pairs={{0,2},{1,3},{2,4},{3,5},{4,6},{5,7},{6,0},{7,1},{8,10},{9,11},{10,... | collective-permute-start | bytes 1572872 | tf_op jit(solution)/shard_map/ppermute | solution.py:484
  28.9 16.4 %collective-permute-start.4 = (bf16[8,128,256]{2,1,0:T(8,128)(2,1)S(1)}, bf16[8,128,256]{2,1,0:T(8,128)(2,1)S(1)}, u32[]{:S(2)}, u32[]{:S(2)}) collective-permute-start(bf16[8,128,256]{2,1,0:T(8,128)(2,1)S(1)} %get-tuple-element.32), channel_id=1, source_target_pairs={{0,6},{1,7},{2,0},{3,1},{4,2},{5,3},{6,4},{7,5},{8,14},{9,15},{10,... | collective-permute-start | bytes 1572872 | tf_op jit(solution)/shard_map/ppermute | solution.py:485
  37.4 18.8 %collective-permute-start.3 = (bf16[8,128,256]{2,1,0:T(8,128)(2,1)}, bf16[8,128,256]{2,1,0:T(8,128)(2,1)S(1)}, u32[]{:S(2)}, u32[]{:S(2)}) collective-permute-start(bf16[8,128,256]{2,1,0:T(8,128)(2,1)} %get-tuple-element.30), channel_id=1, source_target_pairs={{0,6},{1,7},{2,0},{3,1},{4,2},{5,3},{6,4},{7,5},{8,14},{9,15},{10,... | collective-permute-start | bytes 1572872 | tf_op jit(solution)/shard_map/ppermute | solution.py:487
  38.1 18.1 %collective-permute-start.6 = (bf16[8,128,256]{2,1,0:T(8,128)(2,1)}, bf16[8,128,256]{2,1,0:T(8,128)(2,1)S(1)}, u32[]{:S(2)}, u32[]{:S(2)}) collective-permute-start(bf16[8,128,256]{2,1,0:T(8,128)(2,1)} %get-tuple-element.34), channel_id=1, source_target_pairs={{0,2},{1,3},{2,4},{3,5},{4,6},{5,7},{6,0},{7,1},{8,10},{9,11},{10,... | collective-permute-start | bytes 1572872 | tf_op jit(solution)/shard_map/ppermute | solution.py:486
  43.5 3.9 %copy-start.2 = (bf16[80,32,512]{2,1,0:T(8,128)(2,1)S(1)}, bf16[80,32,512]{2,1,0:T(8,128)(2,1)}, u32[]{:S(2)}) copy-start(bf16[80,32,512]{2,1,0:T(8,128)(2,1)} %copy-done.1) | copy-start | bytes 7864324
  44.4 20.7 %collective-permute-start.2 = (bf16[8,128,256]{2,1,0:T(8,128)(2,1)}, bf16[8,128,256]{2,1,0:T(8,128)(2,1)S(1)}, u32[]{:S(2)}, u32[]{:S(2)}) collective-permute-start(bf16[8,128,256]{2,1,0:T(8,128)(2,1)} %add_convert_fusion.1), channel_id=1, source_target_pairs={{0,2},{1,3},{2,4},{3,5},{4,6},{5,7},{6,0},{7,1},{8,10},{9,11},{10,... | collective-permute-start | bytes 1572872 | tf_op jit(solution)/shard_map/ppermute | solution.py:488
  46.3 4.6 %copy-start.13 = (f32[512,512]{1,0:T(8,128)S(1)}, f32[512,512]{1,0:T(8,128)}, u32[]{:S(2)}) copy-start(f32[512,512]{1,0:T(8,128)} %param.16) | copy-start | bytes 3145732
  46.3 20.2 %collective-permute-start.5 = (bf16[8,128,256]{2,1,0:T(8,128)(2,1)}, bf16[8,128,256]{2,1,0:T(8,128)(2,1)S(1)}, u32[]{:S(2)}, u32[]{:S(2)}) collective-permute-start(bf16[8,128,256]{2,1,0:T(8,128)(2,1)} %add_convert_fusion), channel_id=1, source_target_pairs={{0,6},{1,7},{2,0},{3,1},{4,2},{5,3},{6,4},{7,5},{8,14},{9,15},{10,... | collective-permute-start | bytes 1572872 | tf_op jit(solution)/shard_map/ppermute | solution.py:489
  49.2 1.7 copy-start.3
  50.9 1.4 copy-start.14
  50.9 2.3 copy-start.17
  67.4 1.0 copy-start.9
  68.4 1.9 collective-permute-start.7
  70.3 0.8 copy-start.15
  73.1 39.6 %copy-start.11 = (f32[512]{0:T(512)S(1)}, f32[512]{0:T(512)}, u32[]{:S(2)}) copy-start(f32[512]{0:T(512)} %param.18) | copy-start | bytes 6148
  73.1 39.6 %all-to-all-start.1 = ((bf16[32,8,2176]{2,1,0:T(8,128)(2,1)}), bf16[32,8,2176]{2,1,0:T(8,128)(2,1)S(1)}, u32[]{:S(2)}, u32[]{:S(2)}) async-start(bf16[32,8,2176]{2,1,0:T(8,128)(2,1)} %join.1), calls=%async_computation.1 | async-start | bytes 2228224 | tf_op jit(solution)/shard_map/all_to_all | solution.py:503
  152.4 77.2 %all-to-all-start.3 = ((bf16[32,96,512]{2,1,0:T(8,128)(2,1)}), bf16[32,96,512]{2,1,0:T(8,128)(2,1)}, u32[]{:S(2)}, u32[]{:S(2)}) async-start(bf16[32,96,512]{2,1,0:T(8,128)(2,1)} %bitcast.34), calls=%async_computation.3 | async-start | bytes 6291456 | tf_op jit(solution)/shard_map/all_to_all | solution.py:466
  158.1 2.0 collective-permute-start.8
  160.6 25.3 %collective-permute-start.10 = (bf16[2,8,128,256]{3,2,1,0:T(8,128)(2,1)S(1)}, bf16[2,8,128,256]{3,2,1,0:T(8,128)(2,1)S(1)}, u32[]{:S(2)}, u32[]{:S(2)}) collective-permute-start(bf16[2,8,128,256]{3,2,1,0:T(8,128)(2,1)S(1)} %to_columns.1.own), channel_id=1, source_target_pairs={{0,2},{1,3},{2,4},{3,5},{4,6},{5,7},{6,0},{7,1},{8,10},{9,11},{10,... | collective-permute-start | bytes 3145736 | tf_op jit(solution)/shard_map/ppermute | solution.py:520
  160.9 27.3 %collective-permute-start.9 = (bf16[2,8,128,256]{3,2,1,0:T(8,128)(2,1)S(1)}, bf16[2,8,128,256]{3,2,1,0:T(8,128)(2,1)S(1)}, u32[]{:S(2)}, u32[]{:S(2)}) collective-permute-start(bf16[2,8,128,256]{3,2,1,0:T(8,128)(2,1)S(1)} %to_columns.1.own), channel_id=1, source_target_pairs={{0,6},{1,7},{2,0},{3,1},{4,2},{5,3},{6,4},{7,5},{8,14},{9,15},{10,... | collective-permute-start | bytes 3145736 | tf_op jit(solution)/shard_map/ppermute | solution.py:521
  186.8 13.6 %collective-permute-start.11 = (bf16[8,128,256]{2,1,0:T(8,128)(2,1)}, bf16[8,128,256]{2,1,0:T(8,128)(2,1)}, u32[]{:S(2)}, u32[]{:S(2)}) collective-permute-start(bf16[8,128,256]{2,1,0:T(8,128)(2,1)} %slice_bitcast_fusion.1), channel_id=1, source_target_pairs={{0,2},{1,3},{2,4},{3,5},{4,6},{5,7},{6,0},{7,1},{8,10},{9,11},{10,... | collective-permute-start | bytes 1572872 | tf_op jit(solution)/shard_map/ppermute | solution.py:522
  189.1 1.1 copy-start.4
  190.2 14.5 %collective-permute-start.12 = (bf16[8,128,256]{2,1,0:T(8,128)(2,1)}, bf16[8,128,256]{2,1,0:T(8,128)(2,1)}, u32[]{:S(2)}, u32[]{:S(2)}) collective-permute-start(bf16[8,128,256]{2,1,0:T(8,128)(2,1)} %slice_bitcast_fusion), channel_id=1, source_target_pairs={{0,6},{1,7},{2,0},{3,1},{4,2},{5,3},{6,4},{7,5},{8,14},{9,15},{10,... | collective-permute-start | bytes 1572872 | tf_op jit(solution)/shard_map/ppermute | solution.py:523
  190.9 13.7 %copy-start.5 = (bf16[2,8,128,256]{3,2,1,0:T(8,128)(2,1)S(1)}, bf16[2,8,128,256]{3,2,1,0:T(8,128)(2,1)}, u32[]{:S(2)}) copy-start(bf16[2,8,128,256]{3,2,1,0:T(8,128)(2,1)} %copy-done.4) | copy-start | bytes 3145732
  208.3 7.6 %collective-permute-start.13 = (bf16[8,320,256]{2,1,0:T(8,128)(2,1)}, bf16[8,320,256]{2,1,0:T(8,128)(2,1)}, u32[]{:S(2)}, u32[]{:S(2)}) collective-permute-start(bf16[8,320,256]{2,1,0:T(8,128)(2,1)} %idft.3), channel_id=1, source_target_pairs={{0,1},{1,0},{2,3},{3,2},{4,5},{5,4},{6,7},{7,6},{8,9},{9,8},{10,11... | collective-permute-start | bytes 3932168 | tf_op jit(solution)/shard_map/ppermute | solution.py:525
  209.6 1.2 copy-start.6
  210.8 1.1 copy-start.10
  214.7 1.2 copy-start.7
  229.6 1.3 copy-start.8

commit v3 on v2

--- a/solution.py
+++ b/solution.py
@@ -38,6 +38,10 @@
 
 def hbm(value):
     return pltpu.with_memory_space_constraint(value, pltpu.HBM)
+
+
+def vmem(value):
+    return pltpu.with_memory_space_constraint(value, pltpu.VMEM)
 
 
 def half_body(side_ref, x_ref, o_ref):
@@ -122,13 +126,13 @@
 def to_rows(pieces, marks, wide):
     lat, _, half = pieces[0].shape
     part = jax.ShapeDtypeStruct((wide, lat, 4 * half), BF)
-    whole = jax.ShapeDtypeStruct((wide, lat, 8 * half + 128), BF)
-    vmem, free = pl.BlockSpec(memory_space=pltpu.VMEM), pl.BlockSpec(memory_space=pl.ANY)
+    whole = pltpu.HBM((wide, lat, 8 * half + 128), BF)
+    near, free = pl.BlockSpec(memory_space=pltpu.VMEM), pl.BlockSpec(memory_space=pl.ANY)
     return pl.pallas_call(
         rows_body,
         out_shape=[whole, part],
-        in_specs=[vmem] * 7,
-        out_specs=[free, vmem],
+        in_specs=[near] * 7,
+        out_specs=[free, near],
         scratch_shapes=[
             pltpu.VMEM(part.shape, BF),
             pltpu.VMEM((4, wide * lat, 128), F32),
@@ -160,7 +164,7 @@
     free = pl.BlockSpec(memory_space=pl.ANY)
     return pl.pallas_call(
         join_body,
-        out_shape=jax.ShapeDtypeStruct(rows.shape, BF),
+        out_shape=pltpu.HBM(rows.shape, BF),
         in_specs=[free, pl.BlockSpec(memory_space=pltpu.VMEM)],
         out_specs=free,
         input_output_aliases={0: 0},
@@ -290,8 +294,10 @@
 
 def pack(owner, rank, contrib, owners, first, count):
     blocks, rows, channels = contrib.shape
-
-    def body(owner_ref, rank_ref, contrib_ref, o_ref):
+    out_parts = 8
+    out_size = owners // out_parts
+
+    def body(owner_ref, rank_ref, contrib_ref, o_hbm, o_ref, out_sem):
         def step(b, _):
             r = rank_ref[b] - first
 
@@ -302,64 +308,100 @@
             return 0
 
         lax.fori_loop(0, blocks, step, 0)
-
+        stores = []
+        for i in range(out_parts):
+            at = pl.ds(i * out_size, out_size)
+            stores.append(pltpu.make_async_copy(o_ref.at[at], o_hbm.at[at], out_sem.at[i]))
+            stores[-1].start()
+        for c in stores:
+            c.wait()
+
+    out = (owners, count, rows, channels)
     return pl.pallas_call(
         body,
-        out_shape=jax.ShapeDtypeStruct((owners, count, rows, channels), BF),
+        out_shape=pltpu.HBM(out, BF),
         grid_spec=pltpu.PrefetchScalarGridSpec(
             num_scalar_prefetch=2,
             grid=(),
             in_specs=[pl.BlockSpec(memory_space=pltpu.VMEM)],
+            out_specs=pl.BlockSpec(memory_space=pl.ANY),
+            scratch_shapes=[
+                pltpu.VMEM(out, BF),
+                pltpu.SemaphoreType.DMA((out_parts,)),
+            ],
+        ),
+        compiler_params=pltpu.CompilerParams(vmem_limit_bytes=48 << 20),
+        name="pack",
+    )(owner, rank, vmem(contrib))
+
+
+def add_blocks(i, start, order, target, piece, out, blocks):
+    def step(e, _):
+        s = order[e]
+        rows = pl.ds(pl.multiple_of((target[s] - i * blocks) * BS, BS), BS)
+        out[i, rows, :] = out[i, rows, :] + piece[s].astype(F32)
+        return 0
+
+    lax.fori_loop(start[i], start[i + 1], step, 0)
+
+
+def base(core, own, got, lists, piece):
+    lat, lon, half = own.shape
+
+    def body(core_ref, start, order, target, own_ref, got_ref, piece_ref, o_ref):
+        mine = pl.ds(pl.multiple_of(core_ref[0] * half, half), half)
+        other = pl.ds(pl.multiple_of((1 - core_ref[0]) * half, half), half)
+
+        def latitude(i, _):
+            o_ref[i, :, mine] = own_ref[i].astype(F32)
+            o_ref[i, :, other] = got_ref[i].astype(F32)
+            add_blocks(i, start, order, target, piece_ref, o_ref, lon // BS)
+            return 0
+
+        lax.fori_loop(0, lat, latitude, 0)
+
+    return pl.pallas_call(
+        body,
+        out_shape=pltpu.HBM((lat, lon, 2 * half), F32),
+        grid_spec=pltpu.PrefetchScalarGridSpec(
+            num_scalar_prefetch=4,
+            grid=(),
+            in_specs=[pl.BlockSpec(memory_space=pltpu.VMEM)] * 3,
             out_specs=pl.BlockSpec(memory_space=pltpu.VMEM),
         ),
         compiler_params=pltpu.CompilerParams(vmem_limit_bytes=48 << 20),
-        name="pack",
-    )(owner, rank, contrib)
-
-
-def finish(core, own, got, lists, pieces):
-    lat, lon, half = own.shape
-    n = len(pieces)
-    blocks = lon // BS
-
-    def body(core_ref, start, order, target, own_hbm, got_hbm, *refs):
-        pieces_hbm, (o_hbm, own_ref, got_ref, out, sem, out_sem) = refs[:n], refs[n : n + 6]
-        piece_refs = refs[n + 6 :]
-        copies, k = [], 0
-        for p, dst in zip(pieces_hbm, piece_refs):
-            part = p.shape[0] // 4
-            for j in range(4):
-                rows = pl.ds(j * part, part)
-                copies.append(pltpu.make_async_copy(p.at[rows], dst.at[rows], sem.at[k]))
-                k += 1
-        for src, dst in ((own_hbm, own_ref), (got_hbm, got_ref)):
-            for j in range(2):
-                rows = pl.ds(j * (lat // 2), lat // 2)
-                copies.append(pltpu.make_async_copy(src.at[rows], dst.at[rows], sem.at[k]))
-                k += 1
-        for c in copies:
-            c.start()
-        for c in copies:
+        name="base",
+    )(core, *lists, own, got, piece)
+
+
+def finish(begun, lists, piece):
+    lat, lon, channels = begun.shape
+
+    slots = piece.shape[0]
+    parts = 6
+    size = slots // parts
+
+    def body(start, order, target, begun_hbm, piece_hbm, o_hbm, out, piece_ref, sem, read_sem, piece_sem):
+        loads = []
+        for j in range(parts):
+            at = pl.ds(j * size, size)
+            loads.append(pltpu.make_async_copy(piece_hbm.at[at], piece_ref.at[at], piece_sem.at[j]))
+            loads[-1].start()
+
+        def read(i):
+            return pltpu.make_async_copy(begun_hbm.at[i], out.at[i], read_sem.at[i])
+
+        for i in range(lat):
+            read(i).start()
+        for c in loads:
             c.wait()
-        mine = pl.ds(pl.multiple_of(core_ref[0] * half, half), half)
-        other = pl.ds(pl.multiple_of((1 - core_ref[0]) * half, half), half)
 
         def write(i):
-            return pltpu.make_async_copy(out.at[i], o_hbm.at[i], out_sem.at[i])
+            return pltpu.make_async_copy(out.at[i], o_hbm.at[i], sem.at[i])
 
         def latitude(i, _):
-            out[i, :, mine] = own_ref[i].astype(F32)
-            out[i, :, other] = got_ref[i].astype(F32)
-
-            for p, piece in enumerate(piece_refs):
-
-                def step(e, _):
-                    s = order[p, e]
-                    rows = pl.ds(pl.multiple_of((target[p, s] - i * blocks) * BS, BS), BS)
-                    out[i, rows, :] = out[i, rows, :] + piece[s].astype(F32)
-                    return 0
-
-                lax.fori_loop(start[p, i], start[p, i + 1], step, 0)
+            read(i).wait()
+            add_blocks(i, start, order, target, piece_ref, out, lon // BS)
             write(i).start()
             return 0
 
@@ -369,24 +411,23 @@
 
     return pl.pallas_call(
         body,
-        out_shape=jax.ShapeDtypeStruct((lat, lon, 2 * half), F32),
+        out_shape=jax.ShapeDtypeStruct(begun.shape, F32),
         grid_spec=pltpu.PrefetchScalarGridSpec(
-            num_scalar_prefetch=4,
+            num_scalar_prefetch=3,
             grid=(),
-            in_specs=[pl.BlockSpec(memory_space=pl.ANY)] * (2 + n),
+            in_specs=[pl.BlockSpec(memory_space=pl.ANY)] * 2,
             out_specs=pl.BlockSpec(memory_space=pl.ANY),
             scratch_shapes=[
-                pltpu.VMEM((lat, lon, half), BF),
-                pltpu.VMEM((lat, lon, half), BF),
-                pltpu.VMEM((lat, lon, 2 * half), F32),
-                pltpu.SemaphoreType.DMA((4 + 4 * n,)),
+                pltpu.VMEM(begun.shape, F32),
+                pltpu.VMEM(piece.shape, BF),
                 pltpu.SemaphoreType.DMA((lat,)),
-            ]
-            + [pltpu.VMEM(p.shape, BF) for p in pieces],
+                pltpu.SemaphoreType.DMA((lat,)),
+                pltpu.SemaphoreType.DMA((parts,)),
+            ],
         ),
         compiler_params=pltpu.CompilerParams(vmem_limit_bytes=48 << 20),
         name="finish",
-    )(core, *lists, own, got, *pieces)
+    )(*lists, begun, piece)
 
 
 def by_latitude(target, lat, blocks):
@@ -427,7 +468,9 @@
     down = [(i, (i - 2) % narrow) for i in range(narrow)]
     core_ids = core[None].astype(jnp.int32)
 
-    x_got = lax.ppermute(take_half(1 - core_ids, hbm(x)), "narrow", swap)
+    x_give = take_half(1 - core_ids, hbm(x))
+    x, x_give = lax.optimization_barrier((x, x_give))
+    x_got = lax.ppermute(x_give, "narrow", swap)
 
     order = wave_perm.reshape(wide, ring, 2, slots).transpose(1, 2, 3, 0)
     order = jnp.concatenate([order, order], axis=0)
@@ -498,18 +541,15 @@
         (own_a, piece_2, proj, back, marks)
     )
     rows, other = to_rows([own_a, sum_a, direct_a, own_b, sum_b, direct_b], marks, wide)
-    rows = join(rows, lax.ppermute(other, "narrow", swap))
+    rows = join(rows, vmem(lax.ppermute(other, "narrow", swap)))
     rows, got_1 = lax.optimization_barrier((rows, got_1))
     rows = lax.all_to_all(rows, "wide", split_axis=0, concat_axis=0, tiled=True)
     targets = rows[:, 0, 4 * channels : 4 * channels + CAP].astype(jnp.int32)
-    most = wide * max(COUNTS)
-    lists = []
-    for a, b in zip(cut, cut[1:]):
-        part = targets[:, a:b].reshape(-1)
-        lists.append(by_latitude(jnp.pad(part, (0, most - part.shape[0]), constant_values=-1), lat, lon // BS))
-    lists = [jnp.stack(group) for group in zip(*lists)]
+    lists = [
+        by_latitude(targets[:, i:j].reshape(-1), lat, lon // BS) for i, j in zip(cut, cut[1:])
+    ]
     synth = modes(
-        mode_ids, rows.reshape(lat_total, -1), hbm(legendre), hbm(proj), hbm(back),
+        mode_ids, rows.reshape(lat_total, -1), hbm(legendre), vmem(proj), vmem(back),
         mode_depth.reshape(1, -1), wide, lat,
     )
     synth = lax.all_to_all(synth, "wide", split_axis=0, concat_axis=0, tiled=True)
@@ -524,7 +564,8 @@
     pieces = [own, above, across_a, across_b, below]
     wave_got = lax.ppermute(idft(table_t(slice(lon, 2 * lon)), *pieces, 4), "narrow", swap)
     wave_own = idft(table_t(slice(0, lon)), *pieces, 4)
-    return finish(core_ids, wave_own, wave_got, lists, [hbm(got_1), hbm(got_2)])
+    begun = base(core_ids, wave_own, wave_got, lists[0], got_1)
+    return finish(begun, lists[1], hbm(got_2))
 
 
 def solution(mesh):

time: 238 us -> 233 us (0.979)
  Pallas kernels: 38 us -> 44.9 us
  local copies, waits for them, and re-layouts: 15.5 us -> 11.5 us
  waiting for transfers between devices: 98.7 us -> 94.7 us
    pallas_call x5 -> x6, Pallas kernels: 14.1 us -> 21.4 us  [the longest x2 6.88 us: pack(): pl.pallas_call(body, out_shape=pltpu.HBM(out, BF), grid_spec=pltpu.Prefet...]
    all_to_all x2, waiting for transfers between devices: 13.7 us -> 8.86 us  [send_deposit(): lax.all_to_all(piece.reshape(wide, -1, channels), 'wide', split_axis=0, c...]
    unnamed x39 -> x33, local copies, waits for them, and re-layouts: 12 us -> 8.05 us
  transfers between devices with their start and end apart: 17 -> 17, of which waited for: 12 -> 13; matrix products, arithmetic and copies ran while one was open for 6% -> 5% of each run, Pallas kernels for 9% -> 12%
where the time goes in v3:
time: 233 us; the launch traced here: 232 us
  waiting for transfers between devices  94.7 us (41%)
  Pallas kernels  44.9 us (19%)
  starting transfers between devices  38.6 us (17%)
  blocking collectives  32.4 us (14%)
  local copies, waits for them, and re-layouts  11.5 us (5%)
  other arithmetic  8.78 us (4%)
    all_to_all x1, blocking collectives, shards(): lax.all_to_all(synth, 'wide', split_axis=0, concat_axis=0, tiled=True)  32.4 us
    all_to_all x1, waiting for transfers between devices, shards(): rows = lax.all_to_all(rows, 'wide', split_axis=0, concat_axis=0, tiled=True)  29.6 us
    ppermute x1, waiting for transfers between devices, shards(): below = lax.ppermute(own, 'narrow', up)  23.2 us
    all_to_all x2, starting transfers between devices, send_deposit(): lax.all_to_all(piece.reshape(wide, -1, channels), 'wide', split_axis=0, c...  17.3 us
    all_to_all x1, starting transfers between devices, shards(): rows = lax.all_to_all(rows, 'wide', split_axis=0, concat_axis=0, tiled=True)  9.52 us
    ppermute x1, waiting for transfers between devices, shards(): lax.ppermute((relay_a.astype(F32) + up_a.astype(F32)).astype(BF), 'narrow...  9.09 us
    all_to_all x2, waiting for transfers between devices, send_deposit(): lax.all_to_all(piece.reshape(wide, -1, channels), 'wide', split_axis=0, c...  8.86 us
    unnamed x33, local copies, waits for them, and re-layouts  8.05 us
  transfers between devices with their start and end apart: 17, of which 13 were waited for; matrix products, arithmetic and copies ran while one was open for 5% of the time, Pallas kernels for 12%

profile of v3, /device:TPU:26, one launch (start us, length us, event | category | flops | bytes accessed | tf_op | source)
XLA Modules:
  0.0 232.4 jit_solution(18424716294108608073)
XLA Ops:
  0.0 2.4 %take_half.1 = bf16[8,320,256]{2,1,0:T(8,128)(2,1)} custom-call(s32[1]{0:T(128)S(6)} %sub.75.side_ref, bf16[8,320,512]{2,1,0:T(8,128)(2,1)} %own_ref.1), custom_call_target="tpu_custom_call" | custom-call | tf_op jit(solution)/shard_map/take_half/pallas_call | solution.py:55
  2.6 1.1 copy.33
  3.7 0.8 convert_bitcast_fusion.contrib_ref
  4.5 3.4 %pack.2 = bf16[32,2,32,512]{3,2,1,0:T(8,128)(2,1)} custom-call(s32[80]{0:T(128)S(1)} %bitcast.32, s32[80]{0:T(128)S(1)} %convert_reduce_fusion.1.rank_ref, bf16[80,32,512]{2,1,0:T(8,128)(2,1)S(1)} %convert_bitcast_fusion.contrib_ref), custom_call_target="tpu_custom_call" | custom-call | tf_op jit(solution)/shard_map/pack/pallas_call | solution.py:320
  7.9 11.7 %all-to-all-start = ((bf16[32,64,512]{2,1,0:T(8,128)(2,1)}), bf16[32,64,512]{2,1,0:T(8,128)(2,1)}, u32[]{:S(2)}, u32[]{:S(2)}) async-start(bf16[32,64,512]{2,1,0:T(8,128)(2,1)} %bitcast.35), calls=%async_computation | async-start | bytes 4194304 | tf_op jit(solution)/shard_map/all_to_all | solution.py:509
  21.4 1.7 collective-permute-done.got_ref
  23.1 2.3 dft.3
  25.7 1.8 collective-permute-start.4
  27.5 1.8 fusion.1.t_ref
  29.3 4.8 %dft.2 = (bf16[8,128,256]{2,1,0:T(8,128)(2,1)}, bf16[8,128,256]{2,1,0:T(8,128)(2,1)S(1)}, bf16[8,128,256]{2,1,0:T(8,128)(2,1)S(1)}, bf16[8,128,256]{2,1,0:T(8,12...) custom-call(s32[1]{0:T(128)} %bitcast.core_ref, bf16[768,640]{1,0:T(8,128)(2,1)S(1)} %fusion.1.t_ref, ...), custom_call_target="tpu_custom_call" | custom-call | tf_op jit(solution)/shard_map/dft/pallas_call | solution.py:81
  34.1 0.7 collective-permute-start.3
  34.9 2.5 %collective-permute-start.6 = (bf16[8,128,256]{2,1,0:T(8,128)(2,1)}, bf16[8,128,256]{2,1,0:T(8,128)(2,1)S(1)}, u32[]{:S(2)}, u32[]{:S(2)}) collective-permute-start(bf16[8,128,256]{2,1,0:T(8,128)(2,1)} %get-tuple-element.38), channel_id=1, source_target_pairs={{0,2},{1,3},{2,4},{3,5},{4,6},{5,7},{6,0},{7,1},{8,10},{9,11},{10,... | collective-permute-start | bytes 1572872 | tf_op jit(solution)/shard_map/ppermute | solution.py:529
  37.4 2.8 %collective-permute-done.1 = bf16[8,128,256]{2,1,0:T(8,128)(2,1)S(1)} collective-permute-done((bf16[8,128,256]{2,1,0:T(8,128)(2,1)S(1)}, bf16[8,128,256]{2,1,0:T(8,128)(2,1)S(1)}, u32[]{:S(2)}, u32[]{:S(2)}) %collective-permute-start.1) | collective-permute-done | bytes 524320 | tf_op jit(solution)/shard_map/ppermute | solution.py:527
  40.2 1.0 add_convert_fusion.1
  41.2 0.8 collective-permute-start.2
  42.1 1.0 add_convert_fusion
  43.0 1.2 collective-permute-start.5
  44.2 3.5 %pack.3 = bf16[32,3,32,512]{3,2,1,0:T(8,128)(2,1)} custom-call(s32[80]{0:T(128)S(1)} %bitcast.33, s32[80]{0:T(128)S(1)} %convert_reduce_fusion.1.rank_ref, bf16[80,32,512]{2,1,0:T(8,128)(2,1)S(1)} %copy-done.2), custom_call_target="tpu_custom_call" | custom-call | tf_op jit(solution)/shard_map/pack/pallas_call | solution.py:320
  47.8 1.1 copy-done.11
  49.3 3.6 %collective-permute-done.3.direct_a = bf16[8,128,256]{2,1,0:T(8,128)(2,1)S(1)} collective-permute-done((bf16[8,128,256]{2,1,0:T(8,128)(2,1)}, bf16[8,128,256]{2,1,0:T(8,128)(2,1)S(1)}, u32[]{:S(2)}, u32[]{:S(2)}) %collective-permute-start.3) | collective-permute-done | bytes 524320 | tf_op jit(solution)/shard_map/ppermute | solution.py:530
  52.9 9.1 %collective-permute-done.2.sum_a = bf16[8,128,256]{2,1,0:T(8,128)(2,1)} collective-permute-done((bf16[8,128,256]{2,1,0:T(8,128)(2,1)}, bf16[8,128,256]{2,1,0:T(8,128)(2,1)}, u32[]{:S(2)}, u32[]{:S(2)}) %collective-permute-start.2) | collective-permute-done | bytes 524320 | tf_op jit(solution)/shard_map/ppermute | solution.py:531
  62.0 1.3 collective-permute-done.5.sum_b
  63.3 2.4 %to_rows.1 = (bf16[32,8,2176]{2,1,0:T(8,128)(2,1)}, bf16[32,8,1024]{2,1,0:T(8,128)(2,1)S(1)}) custom-call(bf16[8,128,256]{2,1,0:T(8,128)(2,1)S(1)} %get-tuple-element.31.own_a, bf16[8,128,256]{2,1,0:T(8,128)(2,1)} %collective-permute-done.2.sum_a, bf16[8,128,256]{2,1,0:T(8,128)(2,1)S(1)} %collective-permute-done.3.direct_a, ...), custom_call_target="tpu_custom_call" | custom-call | tf_op jit(solution)/shard_map/to_rows/pallas_call | solution.py:131
  65.9 1.9 collective-permute-done.7.got_ref
  67.8 0.8 join.1
  68.9 9.5 %all-to-all-start.1 = ((bf16[32,8,2176]{2,1,0:T(8,128)(2,1)}), bf16[32,8,2176]{2,1,0:T(8,128)(2,1)S(1)}, u32[]{:S(2)}, u32[]{:S(2)}) async-start(bf16[32,8,2176]{2,1,0:T(8,128)(2,1)} %join.1), calls=%async_computation.1 | async-start | bytes 2228224 | tf_op jit(solution)/shard_map/all_to_all | solution.py:546
  78.6 29.6 %all-to-all-done.1 = bf16[32,8,2176]{2,1,0:T(8,128)(2,1)S(1)} async-done(((bf16[32,8,2176]{2,1,0:T(8,128)(2,1)}), bf16[32,8,2176]{2,1,0:T(8,128)(2,1)S(1)}, u32[]{:S(2)}, u32[]{:S(2)}) %all-to-all-start.1) | async-done | bytes 1114144 | tf_op jit(solution)/shard_map/all_to_all | solution.py:546
  108.2 6.9 %modes.1 = bf16[32,2,8,1024]{3,2,1,0:T(8,128)(2,1)S(1)} custom-call(s32[3]{0:T(128)S(1)} %pad_add_fusion.1.ids_ref, bf16[256,2176]{1,0:T(8,128)(2,1)S(1)} %bitcast.26, bf16[256,2176]{1,0:T(8,128)(2,1)S(1)} %bitcast.27, bf16[256,2176]{1,0:T(8,128)(2,1)S(1)} %bitcast.28, bf16[256,2176]{1,0:T(8,128)(2,1)S(1)} %bitcast.29, bf16[2,256,512]{2,1,0:T(8,128)(2,1)} %leg_ref.1, ...), custom_call_target="tpu_custom_call" | custom-call | tf_op jit(solution)/shard_map/modes/pallas_call | solution.py:214
  115.1 32.4 %all_to_all.20.keep = bf16[32,2,8,1024]{3,2,1,0:T(8,128)(2,1)S(1)} all-to-all(bf16[32,2,8,1024]{3,2,1,0:T(8,128)(2,1)S(1)} %modes.1), channel_id=1, replica_groups=mesh['wide'=32,'narrow'=8] {'wide'}, dimensions={0} | all-to-all | bytes 2097152 | tf_op jit(solution)/shard_map/all_to_all | solution.py:555
  147.6 5.6 %all-to-all-start.3 = ((bf16[32,96,512]{2,1,0:T(8,128)(2,1)}), bf16[32,96,512]{2,1,0:T(8,128)(2,1)}, u32[]{:S(2)}, u32[]{:S(2)}) async-start(bf16[32,96,512]{2,1,0:T(8,128)(2,1)} %bitcast.34), calls=%async_computation.3 | async-start | bytes 6291456 | tf_op jit(solution)/shard_map/all_to_all | solution.py:509
  153.3 1.9 collective-permute-done.8.take
  156.1 1.8 collective-permute-start.9
  157.9 23.2 %collective-permute-done.10.below = bf16[2,8,128,256]{3,2,1,0:T(8,128)(2,1)S(1)} collective-permute-done((bf16[2,8,128,256]{3,2,1,0:T(8,128)(2,1)S(1)}, bf16[2,8,128,256]{3,2,1,0:T(8,128)(2,1)S(1)}, u32[]{:S(2)}, u32[]{:S(2)}) %collective-permute-start.10) | collective-permute-done | bytes 1048608 | tf_op jit(solution)/shard_map/ppermute | solution.py:560
  181.1 0.8 slice_bitcast_fusion.1
  181.9 1.5 collective-permute-start.11
  183.4 0.9 slice_bitcast_fusion
  184.3 1.0 copy-done.4
  186.1 2.9 %fusion.8 = (bf16[320,1024]{1,0:T(8,128)(2,1)S(1)}, bf16[320,1024]{1,0:T(8,128)(2,1)}) fusion(f32[320]{0:T(512)S(1)} %get-tuple-element.53, f32[1024]{0:T(1024)S(1)} %sub.80, f32[1024]{0:T(1024)S(1)} %convert_element_type.119, f32[320]{0:T(512)S(1)} %get-tuple-element.54), kind=kLoop, calls=%fused_computation.15 | loop fusion | flops 15073280 | bytes 1321472 | tf_op jit(solution)/shard_map/convert_element_type | solution.py:36
  189.0 6.5 %collective-permute-done.11.across_a = bf16[8,128,256]{2,1,0:T(8,128)(2,1)} collective-permute-done((bf16[8,128,256]{2,1,0:T(8,128)(2,1)}, bf16[8,128,256]{2,1,0:T(8,128)(2,1)}, u32[]{:S(2)}, u32[]{:S(2)}) %collective-permute-start.11) | collective-permute-done | bytes 524320 | tf_op jit(solution)/shard_map/ppermute | solution.py:562
  195.5 4.3 %collective-permute-done.12.across_b = bf16[8,128,256]{2,1,0:T(8,128)(2,1)} collective-permute-done((bf16[8,128,256]{2,1,0:T(8,128)(2,1)}, bf16[8,128,256]{2,1,0:T(8,128)(2,1)}, u32[]{:S(2)}, u32[]{:S(2)}) %collective-permute-start.12) | collective-permute-done | bytes 524320 | tf_op jit(solution)/shard_map/ppermute | solution.py:563
  199.8 3.7 %idft.3 = bf16[8,320,256]{2,1,0:T(8,128)(2,1)} custom-call(bf16[320,1024]{1,0:T(8,128)(2,1)S(1)} %get-tuple-element.49.t_ref, bf16[2,8,128,256]{3,2,1,0:T(8,128)(2,1)S(1)} %to_columns.1.own, bf16[2,8,128,256]{3,2,1,0:T(8,128)(2,1)S(1)} %copy-done.5, bf16[8,128,256]{2,1,0:T(8,128)(2,1)} %collective-permute-done.11.across_a, ...), custom_call_target="tpu_custom_call" | custom-call | tf_op jit(solution)/shard_map/idft/pallas_call | solution.py:284
  204.7 1.2 copy-done.6
  206.0 1.1 copy-done.7
  207.0 2.8 %idft.2.own_ref = bf16[8,320,256]{2,1,0:T(8,128)(2,1)S(1)} custom-call(bf16[320,1024]{1,0:T(8,128)(2,1)S(1)} %copy-done.7, bf16[2,8,128,256]{3,2,1,0:T(8,128)(2,1)S(1)} %to_columns.1.own, bf16[2,8,128,256]{3,2,1,0:T(8,128)(2,1)S(1)} %copy-done.6, bf16[8,128,256]{2,1,0:T(8,128)(2,1)} %collective-permute-done.11.across_a, ...), custom_call_target="tpu_custom_call" | custom-call | tf_op jit(solution)/shard_map/idft/pallas_call | solution.py:284
  209.9 6.3 %base.1.begun_hbm = f32[8,320,512]{2,1,0:T(8,128)} custom-call(s32[1]{0:T(128)} %bitcast.core_ref, s32[9]{0:T(128)S(1)} %convert_reduce_fusion.3.start, s32[64]{0:T(128)S(1)} %select_reduce_fusion.2.order, s32[64]{0:T(128)S(1)} %lt.143.target, bf16[8,320,256]{2,1,0:T(8,128)(2,1)S(1)} %idft.2.own_ref, bf16[8,320,256]{2,1,0:T(8,128)(2,1)} %collective-permute-done.13.got_ref, ...), custom_call_target="tpu_custom_call" | custom-call | tf_op jit(solution)/shard_map/base/pallas_call | solution.py:363
  216.2 8.6 %all-to-all-done.3 = bf16[32,96,512]{2,1,0:T(8,128)(2,1)} async-done(((bf16[32,96,512]{2,1,0:T(8,128)(2,1)}), bf16[32,96,512]{2,1,0:T(8,128)(2,1)}, u32[]{:S(2)}, u32[]{:S(2)}) %all-to-all-start.3) | async-done | bytes 3145760 | tf_op jit(solution)/shard_map/all_to_all | solution.py:509
  224.8 2.5 %copy-done.3 = f32[8,320,512]{2,1,0:T(8,128)S(1)} copy-done((f32[8,320,512]{2,1,0:T(8,128)S(1)}, f32[8,320,512]{2,1,0:T(8,128)}, u32[]{:S(2)}) %copy-start.3) | copy-done | bytes 5242904
  227.3 4.9 %finish.1 = f32[8,320,512]{2,1,0:T(8,128)} custom-call(s32[9]{0:T(128)S(1)} %convert_reduce_fusion.4.start, s32[96]{0:T(128)S(1)} %select_reduce_fusion.1.order, s32[96]{0:T(128)S(1)} %lt.131.target, f32[8,320,512]{2,1,0:T(8,128)S(1)} %copy-done.3, bf16[96,32,512]{2,1,0:T(8,128)(2,1)} %bitcast.16.piece_hbm), custom_call_target="tpu_custom_call" | custom-call | tf_op jit(solution)/shard_map/finish/pallas_call | solution.py:412
  (90 shorter events, 6.1 us)
Async XLA Ops:
  0.0 2.4 %copy-start.9 = (s32[80,1]{0,1:T(1,128)S(1)}, s32[80,1]{0,1:T(1,128)}, u32[]{:S(2)}) copy-start(s32[80,1]{0,1:T(1,128)} %param.12) | copy-start | bytes 964
  0.0 2.6 %copy-start.12 = (bf16[80,32,32]{0,2,1:T(8,128)(2,1)S(1)}, bf16[80,32,32]{0,2,1:T(8,128)(2,1)}, u32[]{:S(2)}) copy-start(bf16[80,32,32]{0,2,1:T(8,128)(2,1)} %param.11) | copy-start | bytes 491524
  0.0 3.7 %copy-start = (bf16[8,320,512]{2,1,0:T(8,128)(2,1)S(1)}, bf16[8,320,512]{2,1,0:T(8,128)(2,1)}, u32[]{:S(2)}) copy-start(bf16[8,320,512]{2,1,0:T(8,128)(2,1)} %own_ref.1) | copy-start | bytes 7864324
  4.5 3.4 %copy-start.1 = (bf16[80,32,512]{2,1,0:T(8,128)(2,1)}, bf16[80,32,512]{2,1,0:T(8,128)(2,1)S(1)}, u32[]{:S(2)}) copy-start(bf16[80,32,512]{2,1,0:T(8,128)(2,1)S(1)} %convert_bitcast_fusion.contrib_ref) | copy-start | bytes 7864324
  7.9 11.9 %copy-start.13 = (s32[512]{0:T(512)S(1)}, s32[512]{0:T(512)}, u32[]{:S(2)}) copy-start(s32[512]{0:T(512)} %param.14) | copy-start | bytes 6148
  7.9 12.5 %copy-start.15 = (f32[2]{0:T(128)S(1)}, f32[2]{0:T(128)}, u32[]{:S(2)}) copy-start(f32[2]{0:T(128)} %constant.63.clone) | copy-start | bytes 28
  7.9 61.0 %all-to-all-start = ((bf16[32,64,512]{2,1,0:T(8,128)(2,1)}), bf16[32,64,512]{2,1,0:T(8,128)(2,1)}, u32[]{:S(2)}, u32[]{:S(2)}) async-start(bf16[32,64,512]{2,1,0:T(8,128)(2,1)} %bitcast.35), calls=%async_computation | async-start | bytes 4194304 | tf_op jit(solution)/shard_map/all_to_all | solution.py:509
  19.6 3.5 %collective-permute-start = (bf16[8,320,256]{2,1,0:T(8,128)(2,1)}, bf16[8,320,256]{2,1,0:T(8,128)(2,1)}, u32[]{:S(2)}, u32[]{:S(2)}) collective-permute-start(bf16[8,320,256]{2,1,0:T(8,128)(2,1)} %take_half.1), channel_id=1, source_target_pairs={{0,1},{1,0},{2,3},{3,2},{4,5},{5,4},{6,7},{7,6},{8,9},{9,8},{10,11... | collective-permute-start | bytes 3932168 | tf_op jit(solution)/shard_map/ppermute | solution.py:473
  25.4 14.8 %collective-permute-start.1 = (bf16[8,128,256]{2,1,0:T(8,128)(2,1)S(1)}, bf16[8,128,256]{2,1,0:T(8,128)(2,1)S(1)}, u32[]{:S(2)}, u32[]{:S(2)}) collective-permute-start(bf16[8,128,256]{2,1,0:T(8,128)(2,1)S(1)} %get-tuple-element.32), channel_id=1, source_target_pairs={{0,2},{1,3},{2,4},{3,5},{4,6},{5,7},{6,0},{7,1},{8,10},{9,11},{10,... | collective-permute-start | bytes 1572872 | tf_op jit(solution)/shard_map/ppermute | solution.py:527
  25.7 16.4 %collective-permute-start.4 = (bf16[8,128,256]{2,1,0:T(8,128)(2,1)S(1)}, bf16[8,128,256]{2,1,0:T(8,128)(2,1)S(1)}, u32[]{:S(2)}, u32[]{:S(2)}) collective-permute-start(bf16[8,128,256]{2,1,0:T(8,128)(2,1)S(1)} %get-tuple-element.36), channel_id=1, source_target_pairs={{0,6},{1,7},{2,0},{3,1},{4,2},{5,3},{6,4},{7,5},{8,14},{9,15},{10,... | collective-permute-start | bytes 1572872 | tf_op jit(solution)/shard_map/ppermute | solution.py:528
  34.1 18.8 %collective-permute-start.3 = (bf16[8,128,256]{2,1,0:T(8,128)(2,1)}, bf16[8,128,256]{2,1,0:T(8,128)(2,1)S(1)}, u32[]{:S(2)}, u32[]{:S(2)}) collective-permute-start(bf16[8,128,256]{2,1,0:T(8,128)(2,1)} %get-tuple-element.34), channel_id=1, source_target_pairs={{0,6},{1,7},{2,0},{3,1},{4,2},{5,3},{6,4},{7,5},{8,14},{9,15},{10,... | collective-permute-start | bytes 1572872 | tf_op jit(solution)/shard_map/ppermute | solution.py:530
  34.9 18.0 %collective-permute-start.6 = (bf16[8,128,256]{2,1,0:T(8,128)(2,1)}, bf16[8,128,256]{2,1,0:T(8,128)(2,1)S(1)}, u32[]{:S(2)}, u32[]{:S(2)}) collective-permute-start(bf16[8,128,256]{2,1,0:T(8,128)(2,1)} %get-tuple-element.38), channel_id=1, source_target_pairs={{0,2},{1,3},{2,4},{3,5},{4,6},{5,7},{6,0},{7,1},{8,10},{9,11},{10,... | collective-permute-start | bytes 1572872 | tf_op jit(solution)/shard_map/ppermute | solution.py:529
  40.2 4.0 %copy-start.2 = (bf16[80,32,512]{2,1,0:T(8,128)(2,1)S(1)}, bf16[80,32,512]{2,1,0:T(8,128)(2,1)}, u32[]{:S(2)}) copy-start(bf16[80,32,512]{2,1,0:T(8,128)(2,1)} %copy-done.1) | copy-start | bytes 7864324
  41.2 20.8 %collective-permute-start.2 = (bf16[8,128,256]{2,1,0:T(8,128)(2,1)}, bf16[8,128,256]{2,1,0:T(8,128)(2,1)}, u32[]{:S(2)}, u32[]{:S(2)}) collective-permute-start(bf16[8,128,256]{2,1,0:T(8,128)(2,1)} %add_convert_fusion.1), channel_id=1, source_target_pairs={{0,2},{1,3},{2,4},{3,5},{4,6},{5,7},{6,0},{7,1},{8,10},{9,11},{10,... | collective-permute-start | bytes 1572872 | tf_op jit(solution)/shard_map/ppermute | solution.py:531
  43.0 4.7 %copy-start.10 = (f32[512,512]{1,0:T(8,128)S(1)}, f32[512,512]{1,0:T(8,128)}, u32[]{:S(2)}) copy-start(f32[512,512]{1,0:T(8,128)} %param.16) | copy-start | bytes 3145732
  43.0 20.3 %collective-permute-start.5 = (bf16[8,128,256]{2,1,0:T(8,128)(2,1)}, bf16[8,128,256]{2,1,0:T(8,128)(2,1)}, u32[]{:S(2)}, u32[]{:S(2)}) collective-permute-start(bf16[8,128,256]{2,1,0:T(8,128)(2,1)} %add_convert_fusion), channel_id=1, source_target_pairs={{0,6},{1,7},{2,0},{3,1},{4,2},{5,3},{6,4},{7,5},{8,14},{9,15},{10,... | collective-permute-start | bytes 1572872 | tf_op jit(solution)/shard_map/ppermute | solution.py:532
  47.7 1.2 copy-start.11
  47.8 1.3 copy-start.14
  65.8 2.0 collective-permute-start.7
  68.6 39.6 %copy-start.8 = (f32[512]{0:T(512)S(1)}, f32[512]{0:T(512)}, u32[]{:S(2)}) copy-start(f32[512]{0:T(512)} %param.18) | copy-start | bytes 6148
  68.9 39.3 %all-to-all-start.1 = ((bf16[32,8,2176]{2,1,0:T(8,128)(2,1)}), bf16[32,8,2176]{2,1,0:T(8,128)(2,1)S(1)}, u32[]{:S(2)}, u32[]{:S(2)}) async-start(bf16[32,8,2176]{2,1,0:T(8,128)(2,1)} %join.1), calls=%async_computation.1 | async-start | bytes 2228224 | tf_op jit(solution)/shard_map/all_to_all | solution.py:546
  147.6 77.2 %all-to-all-start.3 = ((bf16[32,96,512]{2,1,0:T(8,128)(2,1)}), bf16[32,96,512]{2,1,0:T(8,128)(2,1)}, u32[]{:S(2)}, u32[]{:S(2)}) async-start(bf16[32,96,512]{2,1,0:T(8,128)(2,1)} %bitcast.34), calls=%async_computation.3 | async-start | bytes 6291456 | tf_op jit(solution)/shard_map/all_to_all | solution.py:509
  153.2 2.0 collective-permute-start.8
  155.8 25.3 %collective-permute-start.10 = (bf16[2,8,128,256]{3,2,1,0:T(8,128)(2,1)S(1)}, bf16[2,8,128,256]{3,2,1,0:T(8,128)(2,1)S(1)}, u32[]{:S(2)}, u32[]{:S(2)}) collective-permute-start(bf16[2,8,128,256]{3,2,1,0:T(8,128)(2,1)S(1)} %to_columns.1.own), channel_id=1, source_target_pairs={{0,2},{1,3},{2,4},{3,5},{4,6},{5,7},{6,0},{7,1},{8,10},{9,11},{10,... | collective-permute-start | bytes 3145736 | tf_op jit(solution)/shard_map/ppermute | solution.py:560
  156.1 27.3 %collective-permute-start.9 = (bf16[2,8,128,256]{3,2,1,0:T(8,128)(2,1)S(1)}, bf16[2,8,128,256]{3,2,1,0:T(8,128)(2,1)S(1)}, u32[]{:S(2)}, u32[]{:S(2)}) collective-permute-start(bf16[2,8,128,256]{3,2,1,0:T(8,128)(2,1)S(1)} %to_columns.1.own), channel_id=1, source_target_pairs={{0,6},{1,7},{2,0},{3,1},{4,2},{5,3},{6,4},{7,5},{8,14},{9,15},{10,... | collective-permute-start | bytes 3145736 | tf_op jit(solution)/shard_map/ppermute | solution.py:561
  181.9 13.6 %collective-permute-start.11 = (bf16[8,128,256]{2,1,0:T(8,128)(2,1)}, bf16[8,128,256]{2,1,0:T(8,128)(2,1)}, u32[]{:S(2)}, u32[]{:S(2)}) collective-permute-start(bf16[8,128,256]{2,1,0:T(8,128)(2,1)} %slice_bitcast_fusion.1), channel_id=1, source_target_pairs={{0,2},{1,3},{2,4},{3,5},{4,6},{5,7},{6,0},{7,1},{8,10},{9,11},{10,... | collective-permute-start | bytes 1572872 | tf_op jit(solution)/shard_map/ppermute | solution.py:562
  184.3 1.0 copy-start.4
  185.3 14.5 %collective-permute-start.12 = (bf16[8,128,256]{2,1,0:T(8,128)(2,1)}, bf16[8,128,256]{2,1,0:T(8,128)(2,1)}, u32[]{:S(2)}, u32[]{:S(2)}) collective-permute-start(bf16[8,128,256]{2,1,0:T(8,128)(2,1)} %slice_bitcast_fusion), channel_id=1, source_target_pairs={{0,6},{1,7},{2,0},{3,1},{4,2},{5,3},{6,4},{7,5},{8,14},{9,15},{10,... | collective-permute-start | bytes 1572872 | tf_op jit(solution)/shard_map/ppermute | solution.py:563
  186.1 13.7 %copy-start.5 = (bf16[2,8,128,256]{3,2,1,0:T(8,128)(2,1)S(1)}, bf16[2,8,128,256]{3,2,1,0:T(8,128)(2,1)}, u32[]{:S(2)}) copy-start(bf16[2,8,128,256]{3,2,1,0:T(8,128)(2,1)} %copy-done.4) | copy-start | bytes 3145732
  203.4 6.5 %collective-permute-start.13 = (bf16[8,320,256]{2,1,0:T(8,128)(2,1)}, bf16[8,320,256]{2,1,0:T(8,128)(2,1)}, u32[]{:S(2)}, u32[]{:S(2)}) collective-permute-start(bf16[8,320,256]{2,1,0:T(8,128)(2,1)} %idft.3), channel_id=1, source_target_pairs={{0,1},{1,0},{2,3},{3,2},{4,5},{5,4},{6,7},{7,6},{8,9},{9,8},{10,11... | collective-permute-start | bytes 3932168 | tf_op jit(solution)/shard_map/ppermute | solution.py:565
  204.7 1.2 copy-start.6
  206.0 1.1 copy-start.7
  224.8 2.5 %copy-start.3 = (f32[8,320,512]{2,1,0:T(8,128)S(1)}, f32[8,320,512]{2,1,0:T(8,128)}, u32[]{:S(2)}) copy-start(f32[8,320,512]{2,1,0:T(8,128)} %base.1.begun_hbm) | copy-start | bytes 15728644

commit v4 on v3

--- a/solution.py
+++ b/solution.py
@@ -44,22 +44,29 @@
     return pltpu.with_memory_space_constraint(value, pltpu.VMEM)
 
 
-def half_body(side_ref, x_ref, o_ref):
-    o_ref[...] = x_ref[...]
-
-
 def take_half(side, x):
     lat, lon, channels = x.shape
     half = channels // 2
-    step = lat // 2
-    return pl.pallas_call(
-        half_body,
-        out_shape=jax.ShapeDtypeStruct((lat, lon, half), BF),
+
+    def body(side_ref, x_hbm, o_ref, sem):
+        lanes = pl.ds(pl.multiple_of(side_ref[0] * half, half), half)
+        copies = [
+            pltpu.make_async_copy(x_hbm.at[i, :, lanes], o_ref.at[i], sem.at[i]) for i in range(lat)
+        ]
+        for c in copies:
+            c.start()
+        for c in copies:
+            c.wait()
+
+    return pl.pallas_call(
+        body,
+        out_shape=pltpu.VMEM((lat, lon, half), BF),
         grid_spec=pltpu.PrefetchScalarGridSpec(
             num_scalar_prefetch=1,
-            grid=(lat // step,),
-            in_specs=[pl.BlockSpec((step, lon, half), lambda i, c: (i, 0, c[0]))],
-            out_specs=pl.BlockSpec((step, lon, half), lambda i, c: (i, 0, 0)),
+            grid=(),
+            in_specs=[pl.BlockSpec(memory_space=pl.ANY)],
+            out_specs=pl.BlockSpec(memory_space=pltpu.VMEM),
+            scratch_shapes=[pltpu.SemaphoreType.DMA((lat,))],
         ),
         name="take_half",
     )(side, x)
@@ -294,41 +301,29 @@
 
 def pack(owner, rank, contrib, owners, first, count):
     blocks, rows, channels = contrib.shape
-    out_parts = 8
-    out_size = owners // out_parts
-
-    def body(owner_ref, rank_ref, contrib_ref, o_hbm, o_ref, out_sem):
-        def step(b, _):
+
+    def body(owner_ref, rank_ref, contrib_ref, o_hbm, sem):
+        def each(b, act):
             r = rank_ref[b] - first
 
             @pl.when((r >= 0) & (r < count))
             def _():
-                o_ref[owner_ref[b], r] = contrib_ref[b]
+                act(pltpu.make_async_copy(contrib_ref.at[b], o_hbm.at[owner_ref[b], r], sem.at[b]))
 
             return 0
 
-        lax.fori_loop(0, blocks, step, 0)
-        stores = []
-        for i in range(out_parts):
-            at = pl.ds(i * out_size, out_size)
-            stores.append(pltpu.make_async_copy(o_ref.at[at], o_hbm.at[at], out_sem.at[i]))
-            stores[-1].start()
-        for c in stores:
-            c.wait()
-
-    out = (owners, count, rows, channels)
+        lax.fori_loop(0, blocks, lambda b, _: each(b, lambda c: c.start()), 0)
+        lax.fori_loop(0, blocks, lambda b, _: each(b, lambda c: c.wait()), 0)
+
     return pl.pallas_call(
         body,
-        out_shape=pltpu.HBM(out, BF),
+        out_shape=pltpu.HBM((owners, count, rows, channels), BF),
         grid_spec=pltpu.PrefetchScalarGridSpec(
             num_scalar_prefetch=2,
             grid=(),
             in_specs=[pl.BlockSpec(memory_space=pltpu.VMEM)],
             out_specs=pl.BlockSpec(memory_space=pl.ANY),
-            scratch_shapes=[
-                pltpu.VMEM(out, BF),
-                pltpu.SemaphoreType.DMA((out_parts,)),
-            ],
+            scratch_shapes=[pltpu.SemaphoreType.DMA((blocks,))],
         ),
         compiler_params=pltpu.CompilerParams(vmem_limit_bytes=48 << 20),
         name="pack",
@@ -375,43 +370,52 @@
 
 
 def finish(begun, lists, piece):
-    lat, lon, channels = begun.shape
-
-    slots = piece.shape[0]
-    parts = 6
-    size = slots // parts
-
-    def body(start, order, target, begun_hbm, piece_hbm, o_hbm, out, piece_ref, sem, read_sem, piece_sem):
-        loads = []
-        for j in range(parts):
-            at = pl.ds(j * size, size)
-            loads.append(pltpu.make_async_copy(piece_hbm.at[at], piece_ref.at[at], piece_sem.at[j]))
-            loads[-1].start()
-
-        def read(i):
-            return pltpu.make_async_copy(begun_hbm.at[i], out.at[i], read_sem.at[i])
-
-        for i in range(lat):
-            read(i).start()
-        for c in loads:
-            c.wait()
-
-        def write(i):
-            return pltpu.make_async_copy(out.at[i], o_hbm.at[i], sem.at[i])
-
-        def latitude(i, _):
-            read(i).wait()
-            add_blocks(i, start, order, target, piece_ref, out, lon // BS)
-            write(i).start()
+    slots, rows, channels = piece.shape
+    blocks = begun.shape[0]
+
+    def body(start, order, target, begun_hbm, piece_hbm, o_hbm, acc, recv, read_sem, recv_sem, write_sem):
+        first = start[0]
+
+        def entry(e):
+            t = target[order[e]]
+            opens = (e == first) | (target[order[jnp.maximum(e - 1, 0)]] != t)
+            closes = (e == slots - 1) | (target[order[jnp.minimum(e + 1, slots - 1)]] != t)
+            return t, opens, closes
+
+        def read(t):
+            return pltpu.make_async_copy(begun_hbm.at[t], acc.at[t], read_sem.at[t])
+
+        def write(t):
+            return pltpu.make_async_copy(acc.at[t], o_hbm.at[t], write_sem.at[t])
+
+        def arrive(e):
+            return pltpu.make_async_copy(piece_hbm.at[order[e]], recv.at[e], recv_sem.at[e])
+
+        def load(e, _):
+            t, opens, _ = entry(e)
+            arrive(e).start()
+            pl.when(opens)(lambda: read(t).start())
             return 0
 
-        lax.fori_loop(0, lat, latitude, 0)
-        for i in range(lat):
-            write(i).wait()
+        def add(e, _):
+            t, opens, closes = entry(e)
+            pl.when(opens)(lambda: read(t).wait())
+            arrive(e).wait()
+            acc[t] = acc[t] + recv[e].astype(F32)
+            pl.when(closes)(lambda: write(t).start())
+            return 0
+
+        def drain(e, _):
+            t, _, closes = entry(e)
+            pl.when(closes)(lambda: write(t).wait())
+            return 0
+
+        for step in (load, add, drain):
+            lax.fori_loop(first, slots, step, 0)
 
     return pl.pallas_call(
         body,
-        out_shape=jax.ShapeDtypeStruct(begun.shape, F32),
+        out_shape=pltpu.HBM(begun.shape, F32),
         grid_spec=pltpu.PrefetchScalarGridSpec(
             num_scalar_prefetch=3,
             grid=(),
@@ -420,11 +424,12 @@
             scratch_shapes=[
                 pltpu.VMEM(begun.shape, F32),
                 pltpu.VMEM(piece.shape, BF),
-                pltpu.SemaphoreType.DMA((lat,)),
-                pltpu.SemaphoreType.DMA((lat,)),
-                pltpu.SemaphoreType.DMA((parts,)),
+                pltpu.SemaphoreType.DMA((blocks,)),
+                pltpu.SemaphoreType.DMA((slots,)),
+                pltpu.SemaphoreType.DMA((blocks,)),
             ],
         ),
+        input_output_aliases={3: 0},
         compiler_params=pltpu.CompilerParams(vmem_limit_bytes=48 << 20),
         name="finish",
     )(*lists, begun, piece)
@@ -565,7 +570,8 @@
     wave_got = lax.ppermute(idft(table_t(slice(lon, 2 * lon)), *pieces, 4), "narrow", swap)
     wave_own = idft(table_t(slice(0, lon)), *pieces, 4)
     begun = base(core_ids, wave_own, wave_got, lists[0], got_1)
-    return finish(begun, lists[1], hbm(got_2))
+    begun = begun.reshape(blocks, BS, channels)
+    return finish(begun, lists[1], hbm(got_2)).reshape(lat, lon, channels)
 
 
 def solution(mesh):

time: 233 us -> 233 us (level)
  local copies, waits for them, and re-layouts: 11.5 us -> 9 us
    unnamed x33, local copies, waits for them, and re-layouts: 8.05 us -> 5.57 us
where the time goes in v4:
time: 233 us; the launch traced here: 232 us
  waiting for transfers between devices  95 us (41%)
  Pallas kernels  45.1 us (19%)
  starting transfers between devices  38.7 us (17%)
  blocking collectives  32.4 us (14%)
  local copies, waits for them, and re-layouts  9 us (4%)
  other arithmetic  8.78 us (4%)
  matrix products  2.56 us (1%)
    all_to_all x1, blocking collectives, shards(): lax.all_to_all(synth, 'wide', split_axis=0, concat_axis=0, tiled=True)  32.4 us
    all_to_all x1, waiting for transfers between devices, shards(): rows = lax.all_to_all(rows, 'wide', split_axis=0, concat_axis=0, tiled=True)  29.6 us
    ppermute x1, waiting for transfers between devices, shards(): below = lax.ppermute(own, 'narrow', up)  23.2 us
    all_to_all x2, starting transfers between devices, send_deposit(): lax.all_to_all(piece.reshape(wide, -1, channels), 'wide', split_axis=0, c...  17.4 us
    all_to_all x1, starting transfers between devices, shards(): rows = lax.all_to_all(rows, 'wide', split_axis=0, concat_axis=0, tiled=True)  9.52 us
    ppermute x1, waiting for transfers between devices, shards(): lax.ppermute((relay_a.astype(F32) + up_a.astype(F32)).astype(BF), 'narrow...  9.07 us
    all_to_all x2, waiting for transfers between devices, send_deposit(): lax.all_to_all(piece.reshape(wide, -1, channels), 'wide', split_axis=0, c...  8.86 us
    pallas_call x2, Pallas kernels, dft(): pl.pallas_call(dft_body, out_shape=[jax.ShapeDtypeStruct((lat, 128, half)...  7.17 us
  transfers between devices with their start and end apart: 17, of which 13 were waited for; matrix products, arithmetic and copies ran while one was open for 5% of the time, Pallas kernels for 12%

profile of v4, /device:TPU:26, one launch (start us, length us, event | category | flops | bytes accessed | tf_op | source)
XLA Modules:
  0.0 232.3 jit_solution(12119086554929388014)
XLA Ops:
  0.0 1.5 take_half.1
  1.7 1.1 copy.34
  2.8 2.6 %convert_bitcast_fusion.contrib_ref = bf16[80,32,512]{2,1,0:T(8,128)(2,1)S(1)} fusion(bf16[80,32,32]{1,2,0:T(8,128)(2,1)S(1)} %copy.34, bf16[80,32,512]{2,1,0:T(8,128)(2,1)} %bitcast.27), kind=kOutput, calls=%fused_computation.1 | convolution fusion | flops 85196800 | bytes 5406720 | tf_op jit(solution)/shard_map/bai,bac->bic/dot_general | solution.py:498
  5.4 3.1 %pack.2 = bf16[32,2,32,512]{3,2,1,0:T(8,128)(2,1)} custom-call(s32[80]{0:T(128)S(1)} %bitcast.34, s32[80]{0:T(128)S(1)} %convert_reduce_fusion.1.rank_ref, bf16[80,32,512]{2,1,0:T(8,128)(2,1)S(1)} %convert_bitcast_fusion.contrib_ref), custom_call_target="tpu_custom_call" | custom-call | tf_op jit(solution)/shard_map/pack/pallas_call | solution.py:318
  8.5 11.8 %all-to-all-start = ((bf16[32,64,512]{2,1,0:T(8,128)(2,1)}), bf16[32,64,512]{2,1,0:T(8,128)(2,1)}, u32[]{:S(2)}, u32[]{:S(2)}) async-start(bf16[32,64,512]{2,1,0:T(8,128)(2,1)} %bitcast.38), calls=%async_computation | async-start | bytes 4194304 | tf_op jit(solution)/shard_map/all_to_all | solution.py:514
  21.5 0.6 fusion.16.t_ref
  22.1 1.7 collective-permute-done.got_ref
  23.8 2.3 dft.3
  26.4 1.8 collective-permute-start.4
  28.2 1.8 fusion.1.t_ref
  30.0 4.8 %dft.2 = (bf16[8,128,256]{2,1,0:T(8,128)(2,1)}, bf16[8,128,256]{2,1,0:T(8,128)(2,1)S(1)}, bf16[8,128,256]{2,1,0:T(8,128)(2,1)S(1)}, bf16[8,128,256]{2,1,0:T(8,12...) custom-call(s32[1]{0:T(128)} %bitcast.core_ref, bf16[768,640]{1,0:T(8,128)(2,1)S(1)} %fusion.1.t_ref, ...), custom_call_target="tpu_custom_call" | custom-call | tf_op jit(solution)/shard_map/dft/pallas_call | solution.py:88
  34.9 0.7 collective-permute-start.3
  35.6 2.5 %collective-permute-start.6 = (bf16[8,128,256]{2,1,0:T(8,128)(2,1)}, bf16[8,128,256]{2,1,0:T(8,128)(2,1)S(1)}, u32[]{:S(2)}, u32[]{:S(2)}) collective-permute-start(bf16[8,128,256]{2,1,0:T(8,128)(2,1)} %get-tuple-element.38), channel_id=1, source_target_pairs={{0,2},{1,3},{2,4},{3,5},{4,6},{5,7},{6,0},{7,1},{8,10},{9,11},{10,... | collective-permute-start | bytes 1572872 | tf_op jit(solution)/shard_map/ppermute | solution.py:534
  38.1 2.8 %collective-permute-done.1 = bf16[8,128,256]{2,1,0:T(8,128)(2,1)S(1)} collective-permute-done((bf16[8,128,256]{2,1,0:T(8,128)(2,1)S(1)}, bf16[8,128,256]{2,1,0:T(8,128)(2,1)S(1)}, u32[]{:S(2)}, u32[]{:S(2)}) %collective-permute-start.1) | collective-permute-done | bytes 524320 | tf_op jit(solution)/shard_map/ppermute | solution.py:532
  40.9 1.0 add_convert_fusion.1
  41.9 0.8 collective-permute-start.2
  42.8 1.0 add_convert_fusion
  43.7 1.2 collective-permute-start.5
  44.9 3.2 %pack.3 = bf16[32,3,32,512]{3,2,1,0:T(8,128)(2,1)} custom-call(s32[80]{0:T(128)S(1)} %bitcast.35, s32[80]{0:T(128)S(1)} %convert_reduce_fusion.1.rank_ref, bf16[80,32,512]{2,1,0:T(8,128)(2,1)S(1)} %copy-done.2), custom_call_target="tpu_custom_call" | custom-call | tf_op jit(solution)/shard_map/pack/pallas_call | solution.py:318
  48.2 1.1 copy-done.11
  49.7 3.9 %collective-permute-done.3.direct_a = bf16[8,128,256]{2,1,0:T(8,128)(2,1)S(1)} collective-permute-done((bf16[8,128,256]{2,1,0:T(8,128)(2,1)}, bf16[8,128,256]{2,1,0:T(8,128)(2,1)S(1)}, u32[]{:S(2)}, u32[]{:S(2)}) %collective-permute-start.3) | collective-permute-done | bytes 524320 | tf_op jit(solution)/shard_map/ppermute | solution.py:535
  53.6 9.1 %collective-permute-done.2.sum_a = bf16[8,128,256]{2,1,0:T(8,128)(2,1)} collective-permute-done((bf16[8,128,256]{2,1,0:T(8,128)(2,1)}, bf16[8,128,256]{2,1,0:T(8,128)(2,1)}, u32[]{:S(2)}, u32[]{:S(2)}) %collective-permute-start.2) | collective-permute-done | bytes 524320 | tf_op jit(solution)/shard_map/ppermute | solution.py:536
  62.7 1.3 collective-permute-done.5.sum_b
  64.0 2.4 %to_rows.1 = (bf16[32,8,2176]{2,1,0:T(8,128)(2,1)}, bf16[32,8,1024]{2,1,0:T(8,128)(2,1)S(1)}) custom-call(bf16[8,128,256]{2,1,0:T(8,128)(2,1)S(1)} %get-tuple-element.31.own_a, bf16[8,128,256]{2,1,0:T(8,128)(2,1)} %collective-permute-done.2.sum_a, bf16[8,128,256]{2,1,0:T(8,128)(2,1)S(1)} %collective-permute-done.3.direct_a, ...), custom_call_target="tpu_custom_call" | custom-call | tf_op jit(solution)/shard_map/to_rows/pallas_call | solution.py:138
  66.6 1.9 collective-permute-done.7.got_ref
  68.5 0.8 join.1
  69.6 9.5 %all-to-all-start.1 = ((bf16[32,8,2176]{2,1,0:T(8,128)(2,1)}), bf16[32,8,2176]{2,1,0:T(8,128)(2,1)S(1)}, u32[]{:S(2)}, u32[]{:S(2)}) async-start(bf16[32,8,2176]{2,1,0:T(8,128)(2,1)} %join.1), calls=%async_computation.1 | async-start | bytes 2228224 | tf_op jit(solution)/shard_map/all_to_all | solution.py:551
  79.3 29.6 %all-to-all-done.1 = bf16[32,8,2176]{2,1,0:T(8,128)(2,1)S(1)} async-done(((bf16[32,8,2176]{2,1,0:T(8,128)(2,1)}), bf16[32,8,2176]{2,1,0:T(8,128)(2,1)S(1)}, u32[]{:S(2)}, u32[]{:S(2)}) %all-to-all-start.1) | async-done | bytes 1114144 | tf_op jit(solution)/shard_map/all_to_all | solution.py:551
  108.9 6.9 %modes.1 = bf16[32,2,8,1024]{3,2,1,0:T(8,128)(2,1)S(1)} custom-call(s32[3]{0:T(128)S(1)} %pad_add_fusion.1.ids_ref, bf16[256,2176]{1,0:T(8,128)(2,1)S(1)} %bitcast.28, bf16[256,2176]{1,0:T(8,128)(2,1)S(1)} %bitcast.29, bf16[256,2176]{1,0:T(8,128)(2,1)S(1)} %bitcast.30, bf16[256,2176]{1,0:T(8,128)(2,1)S(1)} %bitcast.31, bf16[2,256,512]{2,1,0:T(8,128)(2,1)} %leg_ref.1, ...), custom_call_target="tpu_custom_call" | custom-call | tf_op jit(solution)/shard_map/modes/pallas_call | solution.py:221
  115.8 32.4 %all_to_all.20.keep = bf16[32,2,8,1024]{3,2,1,0:T(8,128)(2,1)S(1)} all-to-all(bf16[32,2,8,1024]{3,2,1,0:T(8,128)(2,1)S(1)} %modes.1), channel_id=1, replica_groups=mesh['wide'=32,'narrow'=8] {'wide'}, dimensions={0} | all-to-all | bytes 2097152 | tf_op jit(solution)/shard_map/all_to_all | solution.py:560
  148.3 5.6 %all-to-all-start.3 = ((bf16[32,96,512]{2,1,0:T(8,128)(2,1)}), bf16[32,96,512]{2,1,0:T(8,128)(2,1)}, u32[]{:S(2)}, u32[]{:S(2)}) async-start(bf16[32,96,512]{2,1,0:T(8,128)(2,1)} %bitcast.37), calls=%async_computation.3 | async-start | bytes 6291456 | tf_op jit(solution)/shard_map/all_to_all | solution.py:514
  154.0 1.9 collective-permute-done.8.take
  156.8 1.8 collective-permute-start.9
  158.6 23.2 %collective-permute-done.10.below = bf16[2,8,128,256]{3,2,1,0:T(8,128)(2,1)S(1)} collective-permute-done((bf16[2,8,128,256]{3,2,1,0:T(8,128)(2,1)S(1)}, bf16[2,8,128,256]{3,2,1,0:T(8,128)(2,1)S(1)}, u32[]{:S(2)}, u32[]{:S(2)}) %collective-permute-start.10) | collective-permute-done | bytes 1048608 | tf_op jit(solution)/shard_map/ppermute | solution.py:565
  181.8 0.8 slice_bitcast_fusion.1
  182.6 1.5 collective-permute-start.11
  184.1 0.9 slice_bitcast_fusion
  185.0 1.0 copy-done.3
  186.8 2.9 %fusion.8 = (bf16[320,1024]{1,0:T(8,128)(2,1)S(1)}, bf16[320,1024]{1,0:T(8,128)(2,1)}) fusion(f32[320]{0:T(512)S(1)} %get-tuple-element.53, f32[1024]{0:T(1024)S(1)} %sub.80, f32[1024]{0:T(1024)S(1)} %convert_element_type.119, f32[320]{0:T(512)S(1)} %get-tuple-element.54), kind=kLoop, calls=%fused_computation.15 | loop fusion | flops 15073280 | bytes 1321472 | tf_op jit(solution)/shard_map/convert_element_type | solution.py:36
  189.7 6.5 %collective-permute-done.11.across_a = bf16[8,128,256]{2,1,0:T(8,128)(2,1)} collective-permute-done((bf16[8,128,256]{2,1,0:T(8,128)(2,1)}, bf16[8,128,256]{2,1,0:T(8,128)(2,1)}, u32[]{:S(2)}, u32[]{:S(2)}) %collective-permute-start.11) | collective-permute-done | bytes 524320 | tf_op jit(solution)/shard_map/ppermute | solution.py:567
  196.2 4.3 %collective-permute-done.12.across_b = bf16[8,128,256]{2,1,0:T(8,128)(2,1)} collective-permute-done((bf16[8,128,256]{2,1,0:T(8,128)(2,1)}, bf16[8,128,256]{2,1,0:T(8,128)(2,1)}, u32[]{:S(2)}, u32[]{:S(2)}) %collective-permute-start.12) | collective-permute-done | bytes 524320 | tf_op jit(solution)/shard_map/ppermute | solution.py:568
  200.5 3.7 %idft.3 = bf16[8,320,256]{2,1,0:T(8,128)(2,1)} custom-call(bf16[320,1024]{1,0:T(8,128)(2,1)S(1)} %get-tuple-element.49.t_ref, bf16[2,8,128,256]{3,2,1,0:T(8,128)(2,1)S(1)} %to_columns.1.own, bf16[2,8,128,256]{3,2,1,0:T(8,128)(2,1)S(1)} %copy-done.4, bf16[8,128,256]{2,1,0:T(8,128)(2,1)} %collective-permute-done.11.across_a, ...), custom_call_target="tpu_custom_call" | custom-call | tf_op jit(solution)/shard_map/idft/pallas_call | solution.py:291
  205.4 1.2 copy-done.5
  206.7 1.1 copy-done.6
  207.8 2.8 %idft.2.own_ref = bf16[8,320,256]{2,1,0:T(8,128)(2,1)S(1)} custom-call(bf16[320,1024]{1,0:T(8,128)(2,1)S(1)} %copy-done.6, bf16[2,8,128,256]{3,2,1,0:T(8,128)(2,1)S(1)} %to_columns.1.own, bf16[2,8,128,256]{3,2,1,0:T(8,128)(2,1)S(1)} %copy-done.5, bf16[8,128,256]{2,1,0:T(8,128)(2,1)} %collective-permute-done.11.across_a, ...), custom_call_target="tpu_custom_call" | custom-call | tf_op jit(solution)/shard_map/idft/pallas_call | solution.py:291
  210.6 6.3 %base.1 = f32[8,320,512]{2,1,0:T(8,128)} custom-call(s32[1]{0:T(128)} %bitcast.core_ref, s32[9]{0:T(128)S(1)} %convert_reduce_fusion.3.start, s32[64]{0:T(128)S(1)} %select_reduce_fusion.2.order, s32[64]{0:T(128)S(1)} %lt.143.target, bf16[8,320,256]{2,1,0:T(8,128)(2,1)S(1)} %idft.2.own_ref, bf16[8,320,256]{2,1,0:T(8,128)(2,1)} %collective-permute-done.13.got_ref, ...), custom_call_target="tpu_custom_call" | custom-call | tf_op jit(solution)/shard_map/base/pallas_call | solution.py:358
  216.9 8.6 %all-to-all-done.3 = bf16[32,96,512]{2,1,0:T(8,128)(2,1)} async-done(((bf16[32,96,512]{2,1,0:T(8,128)(2,1)}), bf16[32,96,512]{2,1,0:T(8,128)(2,1)}, u32[]{:S(2)}, u32[]{:S(2)}) %all-to-all-start.3) | async-done | bytes 3145760 | tf_op jit(solution)/shard_map/all_to_all | solution.py:514
  225.5 6.6 %finish.1 = f32[80,32,512]{2,1,0:T(8,128)} custom-call(s32[9]{0:T(128)S(1)} %convert_reduce_fusion.4.start, s32[96]{0:T(128)S(1)} %select_reduce_fusion.1.order, s32[96]{0:T(128)S(1)} %lt.131.target, f32[80,32,512]{2,1,0:T(8,128)} %bitcast.36, bf16[96,32,512]{2,1,0:T(8,128)(2,1)} %bitcast.17.piece_hbm), custom_call_target="tpu_custom_call", output_to_operand_aliasing={{}: (3, {})} | custom-call | tf_op jit(solution)/shard_map/finish/pallas_call | solution.py:416
  (90 shorter events, 5.6 us)
Async XLA Ops:
  0.0 1.5 copy-start.9
  0.0 1.7 copy-start.12
  1.5 3.8 %copy-start.7 = (bf16[8,320,256]{2,1,0:T(8,128)(2,1)}, bf16[8,320,256]{2,1,0:T(8,128)(2,1)S(1)}, u32[]{:S(2)}) copy-start(bf16[8,320,256]{2,1,0:T(8,128)(2,1)S(1)} %take_half.1) | copy-start | bytes 3932164
  5.4 3.1 %copy-start.1 = (bf16[80,32,512]{2,1,0:T(8,128)(2,1)}, bf16[80,32,512]{2,1,0:T(8,128)(2,1)S(1)}, u32[]{:S(2)}) copy-start(bf16[80,32,512]{2,1,0:T(8,128)(2,1)S(1)} %convert_bitcast_fusion.contrib_ref) | copy-start | bytes 7864324
  8.4 12.0 %copy-start.13 = (s32[512]{0:T(512)S(1)}, s32[512]{0:T(512)}, u32[]{:S(2)}) copy-start(s32[512]{0:T(512)} %param.14) | copy-start | bytes 6148
  8.5 12.6 %copy-start.15 = (f32[2]{0:T(128)S(1)}, f32[2]{0:T(128)}, u32[]{:S(2)}) copy-start(f32[2]{0:T(128)} %constant.63.clone) | copy-start | bytes 28
  8.5 15.3 %copy-start = (bf16[8,320,512]{2,1,0:T(8,128)(2,1)S(1)}, bf16[8,320,512]{2,1,0:T(8,128)(2,1)}, u32[]{:S(2)}) copy-start(bf16[8,320,512]{2,1,0:T(8,128)(2,1)} %own_ref.1) | copy-start | bytes 7864324
  8.5 61.1 %all-to-all-start = ((bf16[32,64,512]{2,1,0:T(8,128)(2,1)}), bf16[32,64,512]{2,1,0:T(8,128)(2,1)}, u32[]{:S(2)}, u32[]{:S(2)}) async-start(bf16[32,64,512]{2,1,0:T(8,128)(2,1)} %bitcast.38), calls=%async_computation | async-start | bytes 4194304 | tf_op jit(solution)/shard_map/all_to_all | solution.py:514
  20.3 3.5 %collective-permute-start = (bf16[8,320,256]{2,1,0:T(8,128)(2,1)}, bf16[8,320,256]{2,1,0:T(8,128)(2,1)}, u32[]{:S(2)}, u32[]{:S(2)}) collective-permute-start(bf16[8,320,256]{2,1,0:T(8,128)(2,1)} %copy-done.7), channel_id=1, source_target_pairs={{0,1},{1,0},{2,3},{3,2},{4,5},{5,4},{6,7},{7,6},{8,9},{9,8},{10,11... | collective-permute-start | bytes 3932168 | tf_op jit(solution)/shard_map/ppermute | solution.py:478
  26.1 14.8 %collective-permute-start.1 = (bf16[8,128,256]{2,1,0:T(8,128)(2,1)S(1)}, bf16[8,128,256]{2,1,0:T(8,128)(2,1)S(1)}, u32[]{:S(2)}, u32[]{:S(2)}) collective-permute-start(bf16[8,128,256]{2,1,0:T(8,128)(2,1)S(1)} %get-tuple-element.32), channel_id=1, source_target_pairs={{0,2},{1,3},{2,4},{3,5},{4,6},{5,7},{6,0},{7,1},{8,10},{9,11},{10,... | collective-permute-start | bytes 1572872 | tf_op jit(solution)/shard_map/ppermute | solution.py:532
  26.4 16.4 %collective-permute-start.4 = (bf16[8,128,256]{2,1,0:T(8,128)(2,1)S(1)}, bf16[8,128,256]{2,1,0:T(8,128)(2,1)S(1)}, u32[]{:S(2)}, u32[]{:S(2)}) collective-permute-start(bf16[8,128,256]{2,1,0:T(8,128)(2,1)S(1)} %get-tuple-element.36), channel_id=1, source_target_pairs={{0,6},{1,7},{2,0},{3,1},{4,2},{5,3},{6,4},{7,5},{8,14},{9,15},{10,... | collective-permute-start | bytes 1572872 | tf_op jit(solution)/shard_map/ppermute | solution.py:533
  34.9 18.8 %collective-permute-start.3 = (bf16[8,128,256]{2,1,0:T(8,128)(2,1)}, bf16[8,128,256]{2,1,0:T(8,128)(2,1)S(1)}, u32[]{:S(2)}, u32[]{:S(2)}) collective-permute-start(bf16[8,128,256]{2,1,0:T(8,128)(2,1)} %get-tuple-element.34), channel_id=1, source_target_pairs={{0,6},{1,7},{2,0},{3,1},{4,2},{5,3},{6,4},{7,5},{8,14},{9,15},{10,... | collective-permute-start | bytes 1572872 | tf_op jit(solution)/shard_map/ppermute | solution.py:535
  35.6 18.0 %collective-permute-start.6 = (bf16[8,128,256]{2,1,0:T(8,128)(2,1)}, bf16[8,128,256]{2,1,0:T(8,128)(2,1)S(1)}, u32[]{:S(2)}, u32[]{:S(2)}) collective-permute-start(bf16[8,128,256]{2,1,0:T(8,128)(2,1)} %get-tuple-element.38), channel_id=1, source_target_pairs={{0,2},{1,3},{2,4},{3,5},{4,6},{5,7},{6,0},{7,1},{8,10},{9,11},{10,... | collective-permute-start | bytes 1572872 | tf_op jit(solution)/shard_map/ppermute | solution.py:534
  40.9 4.0 %copy-start.2 = (bf16[80,32,512]{2,1,0:T(8,128)(2,1)S(1)}, bf16[80,32,512]{2,1,0:T(8,128)(2,1)}, u32[]{:S(2)}) copy-start(bf16[80,32,512]{2,1,0:T(8,128)(2,1)} %copy-done.1) | copy-start | bytes 7864324
  41.9 20.8 %collective-permute-start.2 = (bf16[8,128,256]{2,1,0:T(8,128)(2,1)}, bf16[8,128,256]{2,1,0:T(8,128)(2,1)}, u32[]{:S(2)}, u32[]{:S(2)}) collective-permute-start(bf16[8,128,256]{2,1,0:T(8,128)(2,1)} %add_convert_fusion.1), channel_id=1, source_target_pairs={{0,2},{1,3},{2,4},{3,5},{4,6},{5,7},{6,0},{7,1},{8,10},{9,11},{10,... | collective-permute-start | bytes 1572872 | tf_op jit(solution)/shard_map/ppermute | solution.py:536
  43.7 4.4 %copy-start.10 = (f32[512,512]{1,0:T(8,128)S(1)}, f32[512,512]{1,0:T(8,128)}, u32[]{:S(2)}) copy-start(f32[512,512]{1,0:T(8,128)} %param.16) | copy-start | bytes 3145732
  43.7 20.3 %collective-permute-start.5 = (bf16[8,128,256]{2,1,0:T(8,128)(2,1)}, bf16[8,128,256]{2,1,0:T(8,128)(2,1)}, u32[]{:S(2)}, u32[]{:S(2)}) collective-permute-start(bf16[8,128,256]{2,1,0:T(8,128)(2,1)} %add_convert_fusion), channel_id=1, source_target_pairs={{0,6},{1,7},{2,0},{3,1},{4,2},{5,3},{6,4},{7,5},{8,14},{9,15},{10,... | collective-permute-start | bytes 1572872 | tf_op jit(solution)/shard_map/ppermute | solution.py:537
  48.1 1.2 copy-start.11
  48.1 1.3 copy-start.14
  66.5 2.0 collective-permute-start.7
  69.3 39.6 %copy-start.8 = (f32[512]{0:T(512)S(1)}, f32[512]{0:T(512)}, u32[]{:S(2)}) copy-start(f32[512]{0:T(512)} %param.18) | copy-start | bytes 6148
  69.6 39.3 %all-to-all-start.1 = ((bf16[32,8,2176]{2,1,0:T(8,128)(2,1)}), bf16[32,8,2176]{2,1,0:T(8,128)(2,1)S(1)}, u32[]{:S(2)}, u32[]{:S(2)}) async-start(bf16[32,8,2176]{2,1,0:T(8,128)(2,1)} %join.1), calls=%async_computation.1 | async-start | bytes 2228224 | tf_op jit(solution)/shard_map/all_to_all | solution.py:551
  148.3 77.2 %all-to-all-start.3 = ((bf16[32,96,512]{2,1,0:T(8,128)(2,1)}), bf16[32,96,512]{2,1,0:T(8,128)(2,1)}, u32[]{:S(2)}, u32[]{:S(2)}) async-start(bf16[32,96,512]{2,1,0:T(8,128)(2,1)} %bitcast.37), calls=%async_computation.3 | async-start | bytes 6291456 | tf_op jit(solution)/shard_map/all_to_all | solution.py:514
  153.9 2.0 collective-permute-start.8
  156.5 25.3 %collective-permute-start.10 = (bf16[2,8,128,256]{3,2,1,0:T(8,128)(2,1)S(1)}, bf16[2,8,128,256]{3,2,1,0:T(8,128)(2,1)S(1)}, u32[]{:S(2)}, u32[]{:S(2)}) collective-permute-start(bf16[2,8,128,256]{3,2,1,0:T(8,128)(2,1)S(1)} %to_columns.1.own), channel_id=1, source_target_pairs={{0,2},{1,3},{2,4},{3,5},{4,6},{5,7},{6,0},{7,1},{8,10},{9,11},{10,... | collective-permute-start | bytes 3145736 | tf_op jit(solution)/shard_map/ppermute | solution.py:565
  156.8 27.3 %collective-permute-start.9 = (bf16[2,8,128,256]{3,2,1,0:T(8,128)(2,1)S(1)}, bf16[2,8,128,256]{3,2,1,0:T(8,128)(2,1)S(1)}, u32[]{:S(2)}, u32[]{:S(2)}) collective-permute-start(bf16[2,8,128,256]{3,2,1,0:T(8,128)(2,1)S(1)} %to_columns.1.own), channel_id=1, source_target_pairs={{0,6},{1,7},{2,0},{3,1},{4,2},{5,3},{6,4},{7,5},{8,14},{9,15},{10,... | collective-permute-start | bytes 3145736 | tf_op jit(solution)/shard_map/ppermute | solution.py:566
  182.6 13.6 %collective-permute-start.11 = (bf16[8,128,256]{2,1,0:T(8,128)(2,1)}, bf16[8,128,256]{2,1,0:T(8,128)(2,1)}, u32[]{:S(2)}, u32[]{:S(2)}) collective-permute-start(bf16[8,128,256]{2,1,0:T(8,128)(2,1)} %slice_bitcast_fusion.1), channel_id=1, source_target_pairs={{0,2},{1,3},{2,4},{3,5},{4,6},{5,7},{6,0},{7,1},{8,10},{9,11},{10,... | collective-permute-start | bytes 1572872 | tf_op jit(solution)/shard_map/ppermute | solution.py:567
  185.0 1.0 copy-start.3
  186.0 14.5 %collective-permute-start.12 = (bf16[8,128,256]{2,1,0:T(8,128)(2,1)}, bf16[8,128,256]{2,1,0:T(8,128)(2,1)}, u32[]{:S(2)}, u32[]{:S(2)}) collective-permute-start(bf16[8,128,256]{2,1,0:T(8,128)(2,1)} %slice_bitcast_fusion), channel_id=1, source_target_pairs={{0,6},{1,7},{2,0},{3,1},{4,2},{5,3},{6,4},{7,5},{8,14},{9,15},{10,... | collective-permute-start | bytes 1572872 | tf_op jit(solution)/shard_map/ppermute | solution.py:568
  186.8 13.7 %copy-start.4 = (bf16[2,8,128,256]{3,2,1,0:T(8,128)(2,1)S(1)}, bf16[2,8,128,256]{3,2,1,0:T(8,128)(2,1)}, u32[]{:S(2)}) copy-start(bf16[2,8,128,256]{3,2,1,0:T(8,128)(2,1)} %copy-done.3) | copy-start | bytes 3145732
  204.1 6.5 %collective-permute-start.13 = (bf16[8,320,256]{2,1,0:T(8,128)(2,1)}, bf16[8,320,256]{2,1,0:T(8,128)(2,1)}, u32[]{:S(2)}, u32[]{:S(2)}) collective-permute-start(bf16[8,320,256]{2,1,0:T(8,128)(2,1)} %idft.3), channel_id=1, source_target_pairs={{0,1},{1,0},{2,3},{3,2},{4,5},{5,4},{6,7},{7,6},{8,9},{9,8},{10,11... | collective-permute-start | bytes 3932168 | tf_op jit(solution)/shard_map/ppermute | solution.py:570
  205.4 1.2 copy-start.5
  206.7 1.1 copy-start.6

commit v5 on v3

--- a/solution.py
+++ b/solution.py
@@ -565,7 +565,7 @@
     wave_got = lax.ppermute(idft(table_t(slice(lon, 2 * lon)), *pieces, 4), "narrow", swap)
     wave_own = idft(table_t(slice(0, lon)), *pieces, 4)
     begun = base(core_ids, wave_own, wave_got, lists[0], got_1)
-    return finish(begun, lists[1], hbm(got_2))
+    return finish(hbm(begun), lists[1], hbm(got_2))
 
 
 def solution(mesh):

time: 233 us -> 232 us (level)
  local copies, waits for them, and re-layouts: 11.5 us -> 8.93 us
    unnamed x33 -> x31, local copies, waits for them, and re-layouts: 8.05 us -> 5.53 us
where the time goes in v5:
time: 232 us; the launch traced here: 231 us
  waiting for transfers between devices  94.7 us (41%)
  Pallas kernels  46.3 us (20%)
  starting transfers between devices  38.7 us (17%)
  blocking collectives  32.4 us (14%)
  local copies, waits for them, and re-layouts  8.93 us (4%)
  other arithmetic  8.77 us (4%)
    all_to_all x1, blocking collectives, shards(): lax.all_to_all(synth, 'wide', split_axis=0, concat_axis=0, tiled=True)  32.4 us
    all_to_all x1, waiting for transfers between devices, shards(): rows = lax.all_to_all(rows, 'wide', split_axis=0, concat_axis=0, tiled=True)  29.6 us
    ppermute x1, waiting for transfers between devices, shards(): below = lax.ppermute(own, 'narrow', up)  23.2 us
    all_to_all x2, starting transfers between devices, send_deposit(): lax.all_to_all(piece.reshape(wide, -1, channels), 'wide', split_axis=0, c...  17.3 us
    all_to_all x1, starting transfers between devices, shards(): rows = lax.all_to_all(rows, 'wide', split_axis=0, concat_axis=0, tiled=True)  9.66 us
    ppermute x1, waiting for transfers between devices, shards(): lax.ppermute((relay_a.astype(F32) + up_a.astype(F32)).astype(BF), 'narrow...  9.07 us
    all_to_all x2, waiting for transfers between devices, send_deposit(): lax.all_to_all(piece.reshape(wide, -1, channels), 'wide', split_axis=0, c...  8.83 us
    pallas_call x2, Pallas kernels, dft(): pl.pallas_call(dft_body, out_shape=[jax.ShapeDtypeStruct((lat, 128, half)...  7.13 us
  transfers between devices with their start and end apart: 17, of which 13 were waited for; matrix products, arithmetic and copies ran while one was open for 5% of the time, Pallas kernels for 12%

profile of v5, /device:TPU:26, one launch (start us, length us, event | category | flops | bytes accessed | tf_op | source)
XLA Modules:
  0.0 231.3 jit_solution(7206476750147323441)
XLA Ops:
  0.0 2.4 %take_half.1 = bf16[8,320,256]{2,1,0:T(8,128)(2,1)} custom-call(s32[1]{0:T(128)S(6)} %sub.75.side_ref, bf16[8,320,512]{2,1,0:T(8,128)(2,1)} %own_ref.1), custom_call_target="tpu_custom_call" | custom-call | tf_op jit(solution)/shard_map/take_half/pallas_call | solution.py:55
  2.6 1.1 copy.33
  3.7 0.8 convert_bitcast_fusion.contrib_ref
  4.5 3.3 %pack.2 = bf16[32,2,32,512]{3,2,1,0:T(8,128)(2,1)} custom-call(s32[80]{0:T(128)S(1)} %bitcast.32, s32[80]{0:T(128)S(1)} %convert_reduce_fusion.1.rank_ref, bf16[80,32,512]{2,1,0:T(8,128)(2,1)S(1)} %convert_bitcast_fusion.contrib_ref), custom_call_target="tpu_custom_call" | custom-call | tf_op jit(solution)/shard_map/pack/pallas_call | solution.py:320
  7.9 11.7 %all-to-all-start = ((bf16[32,64,512]{2,1,0:T(8,128)(2,1)}), bf16[32,64,512]{2,1,0:T(8,128)(2,1)}, u32[]{:S(2)}, u32[]{:S(2)}) async-start(bf16[32,64,512]{2,1,0:T(8,128)(2,1)} %bitcast.35), calls=%async_computation | async-start | bytes 4194304 | tf_op jit(solution)/shard_map/all_to_all | solution.py:509
  20.7 0.6 fusion.16.t_ref
  21.3 1.7 collective-permute-done.got_ref
  23.0 2.3 %dft.3 = (bf16[8,128,256]{2,1,0:T(8,128)(2,1)S(1)}, bf16[8,128,256]{2,1,0:T(8,128)(2,1)S(1)}) custom-call(s32[1]{0:T(128)} %bitcast.core_ref, bf16[256,640]{1,0:T(8,128)(2,1)S(1)} %fusion.16.t_ref, bf16[8,320,512]{2,1,0:T(8,128)(2,1)S(1)} %copy-done, bf16[8,320,256]{2,1,0:T(8,128)(2,1)} %collective-permute-done.got_ref), custom_call_target="tpu_custom_call" | custom-call | tf_op jit(solution)/shard_map/dft/pallas_call | solution.py:81
  25.6 1.8 collective-permute-start.4
  27.4 1.8 fusion.1.t_ref
  29.3 4.8 %dft.2 = (bf16[8,128,256]{2,1,0:T(8,128)(2,1)}, bf16[8,128,256]{2,1,0:T(8,128)(2,1)S(1)}, bf16[8,128,256]{2,1,0:T(8,128)(2,1)S(1)}, bf16[8,128,256]{2,1,0:T(8,12...) custom-call(s32[1]{0:T(128)} %bitcast.core_ref, bf16[768,640]{1,0:T(8,128)(2,1)S(1)} %fusion.1.t_ref, ...), custom_call_target="tpu_custom_call" | custom-call | tf_op jit(solution)/shard_map/dft/pallas_call | solution.py:81
  34.1 0.7 collective-permute-start.3
  34.8 2.5 %collective-permute-start.6 = (bf16[8,128,256]{2,1,0:T(8,128)(2,1)}, bf16[8,128,256]{2,1,0:T(8,128)(2,1)S(1)}, u32[]{:S(2)}, u32[]{:S(2)}) collective-permute-start(bf16[8,128,256]{2,1,0:T(8,128)(2,1)} %get-tuple-element.38), channel_id=1, source_target_pairs={{0,2},{1,3},{2,4},{3,5},{4,6},{5,7},{6,0},{7,1},{8,10},{9,11},{10,... | collective-permute-start | bytes 1572872 | tf_op jit(solution)/shard_map/ppermute | solution.py:529
  37.3 2.9 %collective-permute-done.1 = bf16[8,128,256]{2,1,0:T(8,128)(2,1)S(1)} collective-permute-done((bf16[8,128,256]{2,1,0:T(8,128)(2,1)S(1)}, bf16[8,128,256]{2,1,0:T(8,128)(2,1)S(1)}, u32[]{:S(2)}, u32[]{:S(2)}) %collective-permute-start.1) | collective-permute-done | bytes 524320 | tf_op jit(solution)/shard_map/ppermute | solution.py:527
  40.2 1.0 add_convert_fusion.1
  41.1 0.9 collective-permute-start.2
  42.0 0.9 add_convert_fusion
  43.0 1.1 collective-permute-start.5
  44.1 3.5 %pack.3 = bf16[32,3,32,512]{3,2,1,0:T(8,128)(2,1)} custom-call(s32[80]{0:T(128)S(1)} %bitcast.33, s32[80]{0:T(128)S(1)} %convert_reduce_fusion.1.rank_ref, bf16[80,32,512]{2,1,0:T(8,128)(2,1)S(1)} %copy-done.2), custom_call_target="tpu_custom_call" | custom-call | tf_op jit(solution)/shard_map/pack/pallas_call | solution.py:320
  47.8 1.1 copy-done.10
  49.3 3.6 %collective-permute-done.3.direct_a = bf16[8,128,256]{2,1,0:T(8,128)(2,1)S(1)} collective-permute-done((bf16[8,128,256]{2,1,0:T(8,128)(2,1)}, bf16[8,128,256]{2,1,0:T(8,128)(2,1)S(1)}, u32[]{:S(2)}, u32[]{:S(2)}) %collective-permute-start.3) | collective-permute-done | bytes 524320 | tf_op jit(solution)/shard_map/ppermute | solution.py:530
  52.9 9.1 %collective-permute-done.2.sum_a = bf16[8,128,256]{2,1,0:T(8,128)(2,1)} collective-permute-done((bf16[8,128,256]{2,1,0:T(8,128)(2,1)}, bf16[8,128,256]{2,1,0:T(8,128)(2,1)}, u32[]{:S(2)}, u32[]{:S(2)}) %collective-permute-start.2) | collective-permute-done | bytes 524320 | tf_op jit(solution)/shard_map/ppermute | solution.py:531
  62.0 1.3 collective-permute-done.5.sum_b
  63.3 2.5 %to_rows.1 = (bf16[32,8,2176]{2,1,0:T(8,128)(2,1)}, bf16[32,8,1024]{2,1,0:T(8,128)(2,1)S(1)}) custom-call(bf16[8,128,256]{2,1,0:T(8,128)(2,1)S(1)} %get-tuple-element.31.own_a, bf16[8,128,256]{2,1,0:T(8,128)(2,1)} %collective-permute-done.2.sum_a, bf16[8,128,256]{2,1,0:T(8,128)(2,1)S(1)} %collective-permute-done.3.direct_a, ...), custom_call_target="tpu_custom_call" | custom-call | tf_op jit(solution)/shard_map/to_rows/pallas_call | solution.py:131
  65.9 1.9 collective-permute-done.7.got_ref
  67.8 0.9 join.1
  68.8 9.7 %all-to-all-start.1 = ((bf16[32,8,2176]{2,1,0:T(8,128)(2,1)}), bf16[32,8,2176]{2,1,0:T(8,128)(2,1)S(1)}, u32[]{:S(2)}, u32[]{:S(2)}) async-start(bf16[32,8,2176]{2,1,0:T(8,128)(2,1)} %join.1), calls=%async_computation.1 | async-start | bytes 2228224 | tf_op jit(solution)/shard_map/all_to_all | solution.py:546
  78.7 29.6 %all-to-all-done.1 = bf16[32,8,2176]{2,1,0:T(8,128)(2,1)S(1)} async-done(((bf16[32,8,2176]{2,1,0:T(8,128)(2,1)}), bf16[32,8,2176]{2,1,0:T(8,128)(2,1)S(1)}, u32[]{:S(2)}, u32[]{:S(2)}) %all-to-all-start.1) | async-done | bytes 1114144 | tf_op jit(solution)/shard_map/all_to_all | solution.py:546
  108.3 6.9 %modes.1 = bf16[32,2,8,1024]{3,2,1,0:T(8,128)(2,1)S(1)} custom-call(s32[3]{0:T(128)S(1)} %pad_add_fusion.1.ids_ref, bf16[256,2176]{1,0:T(8,128)(2,1)S(1)} %bitcast.26, bf16[256,2176]{1,0:T(8,128)(2,1)S(1)} %bitcast.27, bf16[256,2176]{1,0:T(8,128)(2,1)S(1)} %bitcast.28, bf16[256,2176]{1,0:T(8,128)(2,1)S(1)} %bitcast.29, bf16[2,256,512]{2,1,0:T(8,128)(2,1)} %leg_ref.1, ...), custom_call_target="tpu_custom_call" | custom-call | tf_op jit(solution)/shard_map/modes/pallas_call | solution.py:214
  115.2 32.4 %all_to_all.20.keep = bf16[32,2,8,1024]{3,2,1,0:T(8,128)(2,1)S(1)} all-to-all(bf16[32,2,8,1024]{3,2,1,0:T(8,128)(2,1)S(1)} %modes.1), channel_id=1, replica_groups=mesh['wide'=32,'narrow'=8] {'wide'}, dimensions={0} | all-to-all | bytes 2097152 | tf_op jit(solution)/shard_map/all_to_all | solution.py:555
  147.7 5.6 %all-to-all-start.3 = ((bf16[32,96,512]{2,1,0:T(8,128)(2,1)}), bf16[32,96,512]{2,1,0:T(8,128)(2,1)}, u32[]{:S(2)}, u32[]{:S(2)}) async-start(bf16[32,96,512]{2,1,0:T(8,128)(2,1)} %bitcast.34), calls=%async_computation.3 | async-start | bytes 6291456 | tf_op jit(solution)/shard_map/all_to_all | solution.py:509
  153.4 1.9 collective-permute-done.8.take
  156.2 1.8 collective-permute-start.9
  158.0 23.2 %collective-permute-done.10.below = bf16[2,8,128,256]{3,2,1,0:T(8,128)(2,1)S(1)} collective-permute-done((bf16[2,8,128,256]{3,2,1,0:T(8,128)(2,1)S(1)}, bf16[2,8,128,256]{3,2,1,0:T(8,128)(2,1)S(1)}, u32[]{:S(2)}, u32[]{:S(2)}) %collective-permute-start.10) | collective-permute-done | bytes 1048608 | tf_op jit(solution)/shard_map/ppermute | solution.py:560
  181.2 0.8 slice_bitcast_fusion.1
  182.0 1.5 collective-permute-start.11
  183.5 0.8 slice_bitcast_fusion
  184.4 1.0 copy-done.3
  186.1 2.9 %fusion.8 = (bf16[320,1024]{1,0:T(8,128)(2,1)S(1)}, bf16[320,1024]{1,0:T(8,128)(2,1)}) fusion(f32[320]{0:T(512)S(1)} %get-tuple-element.53, f32[1024]{0:T(1024)S(1)} %sub.80, f32[1024]{0:T(1024)S(1)} %convert_element_type.119, f32[320]{0:T(512)S(1)} %get-tuple-element.54), kind=kLoop, calls=%fused_computation.15 | loop fusion | flops 15073280 | bytes 1321472 | tf_op jit(solution)/shard_map/convert_element_type | solution.py:36
  189.0 6.5 %collective-permute-done.11.across_a = bf16[8,128,256]{2,1,0:T(8,128)(2,1)} collective-permute-done((bf16[8,128,256]{2,1,0:T(8,128)(2,1)}, bf16[8,128,256]{2,1,0:T(8,128)(2,1)}, u32[]{:S(2)}, u32[]{:S(2)}) %collective-permute-start.11) | collective-permute-done | bytes 524320 | tf_op jit(solution)/shard_map/ppermute | solution.py:562
  195.6 4.2 %collective-permute-done.12.across_b = bf16[8,128,256]{2,1,0:T(8,128)(2,1)} collective-permute-done((bf16[8,128,256]{2,1,0:T(8,128)(2,1)}, bf16[8,128,256]{2,1,0:T(8,128)(2,1)}, u32[]{:S(2)}, u32[]{:S(2)}) %collective-permute-start.12) | collective-permute-done | bytes 524320 | tf_op jit(solution)/shard_map/ppermute | solution.py:563
  199.8 3.7 %idft.3 = bf16[8,320,256]{2,1,0:T(8,128)(2,1)} custom-call(bf16[320,1024]{1,0:T(8,128)(2,1)S(1)} %get-tuple-element.49.t_ref, bf16[2,8,128,256]{3,2,1,0:T(8,128)(2,1)S(1)} %to_columns.1.own, bf16[2,8,128,256]{3,2,1,0:T(8,128)(2,1)S(1)} %copy-done.4, bf16[8,128,256]{2,1,0:T(8,128)(2,1)} %collective-permute-done.11.across_a, ...), custom_call_target="tpu_custom_call" | custom-call | tf_op jit(solution)/shard_map/idft/pallas_call | solution.py:284
  204.8 1.2 copy-done.5
  206.0 1.1 copy-done.6
  207.1 2.8 %idft.2.own_ref = bf16[8,320,256]{2,1,0:T(8,128)(2,1)S(1)} custom-call(bf16[320,1024]{1,0:T(8,128)(2,1)S(1)} %copy-done.6, bf16[2,8,128,256]{3,2,1,0:T(8,128)(2,1)S(1)} %to_columns.1.own, bf16[2,8,128,256]{3,2,1,0:T(8,128)(2,1)S(1)} %copy-done.5, bf16[8,128,256]{2,1,0:T(8,128)(2,1)} %collective-permute-done.11.across_a, ...), custom_call_target="tpu_custom_call" | custom-call | tf_op jit(solution)/shard_map/idft/pallas_call | solution.py:284
  209.9 6.3 %base.1.begun_hbm = f32[8,320,512]{2,1,0:T(8,128)} custom-call(s32[1]{0:T(128)} %bitcast.core_ref, s32[9]{0:T(128)S(1)} %convert_reduce_fusion.3.start, s32[64]{0:T(128)S(1)} %select_reduce_fusion.2.order, s32[64]{0:T(128)S(1)} %lt.143.target, bf16[8,320,256]{2,1,0:T(8,128)(2,1)S(1)} %idft.2.own_ref, bf16[8,320,256]{2,1,0:T(8,128)(2,1)} %collective-permute-done.13.got_ref, ...), custom_call_target="tpu_custom_call" | custom-call | tf_op jit(solution)/shard_map/base/pallas_call | solution.py:363
  216.2 8.7 %all-to-all-done.3 = bf16[32,96,512]{2,1,0:T(8,128)(2,1)} async-done(((bf16[32,96,512]{2,1,0:T(8,128)(2,1)}), bf16[32,96,512]{2,1,0:T(8,128)(2,1)}, u32[]{:S(2)}, u32[]{:S(2)}) %all-to-all-start.3) | async-done | bytes 3145760 | tf_op jit(solution)/shard_map/all_to_all | solution.py:509
  224.9 6.3 %finish.1 = f32[8,320,512]{2,1,0:T(8,128)} custom-call(s32[9]{0:T(128)S(1)} %convert_reduce_fusion.4.start, s32[96]{0:T(128)S(1)} %select_reduce_fusion.1.order, s32[96]{0:T(128)S(1)} %lt.131.target, f32[8,320,512]{2,1,0:T(8,128)} %base.1.begun_hbm, bf16[96,32,512]{2,1,0:T(8,128)(2,1)} %bitcast.16.piece_hbm), custom_call_target="tpu_custom_call" | custom-call | tf_op jit(solution)/shard_map/finish/pallas_call | solution.py:412
  (88 shorter events, 5.5 us)
Async XLA Ops:
  0.0 2.4 %copy-start.8 = (s32[80,1]{0,1:T(1,128)S(1)}, s32[80,1]{0,1:T(1,128)}, u32[]{:S(2)}) copy-start(s32[80,1]{0,1:T(1,128)} %param.12) | copy-start | bytes 964
  0.0 2.6 %copy-start.11 = (bf16[80,32,32]{0,2,1:T(8,128)(2,1)S(1)}, bf16[80,32,32]{0,2,1:T(8,128)(2,1)}, u32[]{:S(2)}) copy-start(bf16[80,32,32]{0,2,1:T(8,128)(2,1)} %param.11) | copy-start | bytes 491524
  0.0 3.6 %copy-start = (bf16[8,320,512]{2,1,0:T(8,128)(2,1)S(1)}, bf16[8,320,512]{2,1,0:T(8,128)(2,1)}, u32[]{:S(2)}) copy-start(bf16[8,320,512]{2,1,0:T(8,128)(2,1)} %own_ref.1) | copy-start | bytes 7864324
  4.5 3.4 %copy-start.1 = (bf16[80,32,512]{2,1,0:T(8,128)(2,1)}, bf16[80,32,512]{2,1,0:T(8,128)(2,1)S(1)}, u32[]{:S(2)}) copy-start(bf16[80,32,512]{2,1,0:T(8,128)(2,1)S(1)} %convert_bitcast_fusion.contrib_ref) | copy-start | bytes 7864324
  7.8 11.8 %copy-start.12 = (s32[512]{0:T(512)S(1)}, s32[512]{0:T(512)}, u32[]{:S(2)}) copy-start(s32[512]{0:T(512)} %param.14) | copy-start | bytes 6148
  7.9 12.5 %copy-start.14 = (f32[2]{0:T(128)S(1)}, f32[2]{0:T(128)}, u32[]{:S(2)}) copy-start(f32[2]{0:T(128)} %constant.63.clone) | copy-start | bytes 28
  7.9 61.0 %all-to-all-start = ((bf16[32,64,512]{2,1,0:T(8,128)(2,1)}), bf16[32,64,512]{2,1,0:T(8,128)(2,1)}, u32[]{:S(2)}, u32[]{:S(2)}) async-start(bf16[32,64,512]{2,1,0:T(8,128)(2,1)} %bitcast.35), calls=%async_computation | async-start | bytes 4194304 | tf_op jit(solution)/shard_map/all_to_all | solution.py:509
  19.5 3.5 %collective-permute-start = (bf16[8,320,256]{2,1,0:T(8,128)(2,1)}, bf16[8,320,256]{2,1,0:T(8,128)(2,1)}, u32[]{:S(2)}, u32[]{:S(2)}) collective-permute-start(bf16[8,320,256]{2,1,0:T(8,128)(2,1)} %take_half.1), channel_id=1, source_target_pairs={{0,1},{1,0},{2,3},{3,2},{4,5},{5,4},{6,7},{7,6},{8,9},{9,8},{10,11... | collective-permute-start | bytes 3932168 | tf_op jit(solution)/shard_map/ppermute | solution.py:473
  25.3 14.8 %collective-permute-start.1 = (bf16[8,128,256]{2,1,0:T(8,128)(2,1)S(1)}, bf16[8,128,256]{2,1,0:T(8,128)(2,1)S(1)}, u32[]{:S(2)}, u32[]{:S(2)}) collective-permute-start(bf16[8,128,256]{2,1,0:T(8,128)(2,1)S(1)} %get-tuple-element.32), channel_id=1, source_target_pairs={{0,2},{1,3},{2,4},{3,5},{4,6},{5,7},{6,0},{7,1},{8,10},{9,11},{10,... | collective-permute-start | bytes 1572872 | tf_op jit(solution)/shard_map/ppermute | solution.py:527
  25.6 16.4 %collective-permute-start.4 = (bf16[8,128,256]{2,1,0:T(8,128)(2,1)S(1)}, bf16[8,128,256]{2,1,0:T(8,128)(2,1)S(1)}, u32[]{:S(2)}, u32[]{:S(2)}) collective-permute-start(bf16[8,128,256]{2,1,0:T(8,128)(2,1)S(1)} %get-tuple-element.36), channel_id=1, source_target_pairs={{0,6},{1,7},{2,0},{3,1},{4,2},{5,3},{6,4},{7,5},{8,14},{9,15},{10,... | collective-permute-start | bytes 1572872 | tf_op jit(solution)/shard_map/ppermute | solution.py:528
  34.1 18.8 %collective-permute-start.3 = (bf16[8,128,256]{2,1,0:T(8,128)(2,1)}, bf16[8,128,256]{2,1,0:T(8,128)(2,1)S(1)}, u32[]{:S(2)}, u32[]{:S(2)}) collective-permute-start(bf16[8,128,256]{2,1,0:T(8,128)(2,1)} %get-tuple-element.34), channel_id=1, source_target_pairs={{0,6},{1,7},{2,0},{3,1},{4,2},{5,3},{6,4},{7,5},{8,14},{9,15},{10,... | collective-permute-start | bytes 1572872 | tf_op jit(solution)/shard_map/ppermute | solution.py:530
  34.8 18.1 %collective-permute-start.6 = (bf16[8,128,256]{2,1,0:T(8,128)(2,1)}, bf16[8,128,256]{2,1,0:T(8,128)(2,1)S(1)}, u32[]{:S(2)}, u32[]{:S(2)}) collective-permute-start(bf16[8,128,256]{2,1,0:T(8,128)(2,1)} %get-tuple-element.38), channel_id=1, source_target_pairs={{0,2},{1,3},{2,4},{3,5},{4,6},{5,7},{6,0},{7,1},{8,10},{9,11},{10,... | collective-permute-start | bytes 1572872 | tf_op jit(solution)/shard_map/ppermute | solution.py:529
  40.2 3.9 %copy-start.2 = (bf16[80,32,512]{2,1,0:T(8,128)(2,1)S(1)}, bf16[80,32,512]{2,1,0:T(8,128)(2,1)}, u32[]{:S(2)}) copy-start(bf16[80,32,512]{2,1,0:T(8,128)(2,1)} %copy-done.1) | copy-start | bytes 7864324
  41.1 20.8 %collective-permute-start.2 = (bf16[8,128,256]{2,1,0:T(8,128)(2,1)}, bf16[8,128,256]{2,1,0:T(8,128)(2,1)}, u32[]{:S(2)}, u32[]{:S(2)}) collective-permute-start(bf16[8,128,256]{2,1,0:T(8,128)(2,1)} %add_convert_fusion.1), channel_id=1, source_target_pairs={{0,2},{1,3},{2,4},{3,5},{4,6},{5,7},{6,0},{7,1},{8,10},{9,11},{10,... | collective-permute-start | bytes 1572872 | tf_op jit(solution)/shard_map/ppermute | solution.py:531
  43.0 4.7 %copy-start.9 = (f32[512,512]{1,0:T(8,128)S(1)}, f32[512,512]{1,0:T(8,128)}, u32[]{:S(2)}) copy-start(f32[512,512]{1,0:T(8,128)} %param.16) | copy-start | bytes 3145732
  43.0 20.3 %collective-permute-start.5 = (bf16[8,128,256]{2,1,0:T(8,128)(2,1)}, bf16[8,128,256]{2,1,0:T(8,128)(2,1)}, u32[]{:S(2)}, u32[]{:S(2)}) collective-permute-start(bf16[8,128,256]{2,1,0:T(8,128)(2,1)} %add_convert_fusion), channel_id=1, source_target_pairs={{0,6},{1,7},{2,0},{3,1},{4,2},{5,3},{6,4},{7,5},{8,14},{9,15},{10,... | collective-permute-start | bytes 1572872 | tf_op jit(solution)/shard_map/ppermute | solution.py:532
  47.7 1.2 copy-start.10
  47.7 1.3 copy-start.13
  65.8 2.0 collective-permute-start.7
  68.7 39.6 %copy-start.7 = (f32[512]{0:T(512)S(1)}, f32[512]{0:T(512)}, u32[]{:S(2)}) copy-start(f32[512]{0:T(512)} %param.18) | copy-start | bytes 6148
  68.8 39.4 %all-to-all-start.1 = ((bf16[32,8,2176]{2,1,0:T(8,128)(2,1)}), bf16[32,8,2176]{2,1,0:T(8,128)(2,1)S(1)}, u32[]{:S(2)}, u32[]{:S(2)}) async-start(bf16[32,8,2176]{2,1,0:T(8,128)(2,1)} %join.1), calls=%async_computation.1 | async-start | bytes 2228224 | tf_op jit(solution)/shard_map/all_to_all | solution.py:546
  147.7 77.2 %all-to-all-start.3 = ((bf16[32,96,512]{2,1,0:T(8,128)(2,1)}), bf16[32,96,512]{2,1,0:T(8,128)(2,1)}, u32[]{:S(2)}, u32[]{:S(2)}) async-start(bf16[32,96,512]{2,1,0:T(8,128)(2,1)} %bitcast.34), calls=%async_computation.3 | async-start | bytes 6291456 | tf_op jit(solution)/shard_map/all_to_all | solution.py:509
  153.3 2.0 collective-permute-start.8
  155.9 25.3 %collective-permute-start.10 = (bf16[2,8,128,256]{3,2,1,0:T(8,128)(2,1)S(1)}, bf16[2,8,128,256]{3,2,1,0:T(8,128)(2,1)S(1)}, u32[]{:S(2)}, u32[]{:S(2)}) collective-permute-start(bf16[2,8,128,256]{3,2,1,0:T(8,128)(2,1)S(1)} %to_columns.1.own), channel_id=1, source_target_pairs={{0,2},{1,3},{2,4},{3,5},{4,6},{5,7},{6,0},{7,1},{8,10},{9,11},{10,... | collective-permute-start | bytes 3145736 | tf_op jit(solution)/shard_map/ppermute | solution.py:560
  156.2 27.3 %collective-permute-start.9 = (bf16[2,8,128,256]{3,2,1,0:T(8,128)(2,1)S(1)}, bf16[2,8,128,256]{3,2,1,0:T(8,128)(2,1)S(1)}, u32[]{:S(2)}, u32[]{:S(2)}) collective-permute-start(bf16[2,8,128,256]{3,2,1,0:T(8,128)(2,1)S(1)} %to_columns.1.own), channel_id=1, source_target_pairs={{0,6},{1,7},{2,0},{3,1},{4,2},{5,3},{6,4},{7,5},{8,14},{9,15},{10,... | collective-permute-start | bytes 3145736 | tf_op jit(solution)/shard_map/ppermute | solution.py:561
  182.0 13.6 %collective-permute-start.11 = (bf16[8,128,256]{2,1,0:T(8,128)(2,1)}, bf16[8,128,256]{2,1,0:T(8,128)(2,1)}, u32[]{:S(2)}, u32[]{:S(2)}) collective-permute-start(bf16[8,128,256]{2,1,0:T(8,128)(2,1)} %slice_bitcast_fusion.1), channel_id=1, source_target_pairs={{0,2},{1,3},{2,4},{3,5},{4,6},{5,7},{6,0},{7,1},{8,10},{9,11},{10,... | collective-permute-start | bytes 1572872 | tf_op jit(solution)/shard_map/ppermute | solution.py:562
  184.3 1.0 copy-start.3
  185.3 14.5 %collective-permute-start.12 = (bf16[8,128,256]{2,1,0:T(8,128)(2,1)}, bf16[8,128,256]{2,1,0:T(8,128)(2,1)}, u32[]{:S(2)}, u32[]{:S(2)}) collective-permute-start(bf16[8,128,256]{2,1,0:T(8,128)(2,1)} %slice_bitcast_fusion), channel_id=1, source_target_pairs={{0,6},{1,7},{2,0},{3,1},{4,2},{5,3},{6,4},{7,5},{8,14},{9,15},{10,... | collective-permute-start | bytes 1572872 | tf_op jit(solution)/shard_map/ppermute | solution.py:563
  186.1 13.7 %copy-start.4 = (bf16[2,8,128,256]{3,2,1,0:T(8,128)(2,1)S(1)}, bf16[2,8,128,256]{3,2,1,0:T(8,128)(2,1)}, u32[]{:S(2)}) copy-start(bf16[2,8,128,256]{3,2,1,0:T(8,128)(2,1)} %copy-done.3) | copy-start | bytes 3145732
  203.5 6.5 %collective-permute-start.13 = (bf16[8,320,256]{2,1,0:T(8,128)(2,1)}, bf16[8,320,256]{2,1,0:T(8,128)(2,1)}, u32[]{:S(2)}, u32[]{:S(2)}) collective-permute-start(bf16[8,320,256]{2,1,0:T(8,128)(2,1)} %idft.3), channel_id=1, source_target_pairs={{0,1},{1,0},{2,3},{3,2},{4,5},{5,4},{6,7},{7,6},{8,9},{9,8},{10,11... | collective-permute-start | bytes 3932168 | tf_op jit(solution)/shard_map/ppermute | solution.py:565
  204.8 1.2 copy-start.5
  206.0 1.1 copy-start.6
